TPU v7x, 32 devices: a whole 2x2x4 slice. The times are simulated.
32 devices in a mesh: groups: 2 (over y), tiles: 4 (over z), rows: 2 (over x), chan: 2 (over core).
Axes of the slice: x: 2, y: 2, z: 4, core: 2. Of those that a mesh axis runs over, the one named last changes fastest.
Arguments:
- acts: bfloat16 [96, 24576], P(('groups', 'rows'), 'tiles'), parts along dimension 0, may hold values from -6 to 6
- shift: float32 [128], replicated, may hold values from -3 to 3
- weight_one: bfloat16 [3, 3, 64, 128], replicated, may hold values from -0.25 to 0.25
- weight_two: bfloat16 [3, 3, 128, 128], P(None, None, None, 'chan'), may hold values from -0.1875 to 0.1875
- cotangent: bfloat16 [48, 192, 128], P(('groups', 'rows'), 'tiles', 'chan'), parts along dimension 0, may hold values from -6 to 6
- tissue_count: int32 [4, 4], P(('groups', 'rows'), 'tiles'), parts along dimension 0, may hold values from 1 to 16, 32 in all within a row
- tile_order: int32 [4, 4, 16], P(('groups', 'rows'), 'tiles'), parts along dimension 0, may hold values from 0 to 15, each once within a row
Outputs:
- input_grad: bfloat16 [96, 24576], P(('groups', 'rows'), 'tiles'), parts along dimension 0
- first_grad: float32 [6, 3, 64, 128], P('groups', None, None, 'chan'), parts along dimension 0
- second_grad: float32 [6, 3, 128, 128], P('groups', None, None, 'chan'), parts along dimension 0
There are 2 independent parts, one for each index of `groups`. A program takes and returns all parts, laid end to end along the dimension named above; an argument that names none is the same for every part. Nothing has to cross between parts.
Inputs may be any that keep to these rules, and one draw needn't show every extreme that they name: `tissue_count`: in each block of tile rows the counts add up to exactly 32, and some device there holds 16 tissue tiles. `tile_order`: each device's list names each of its 16 tiles once.
All inputs are finite; a program needn't handle non-finite values.
Results may differ from a plain program's by a relative error of at most 0.015.
Values may be sent and summed in bfloat16 or wider, within the bound.
No kernel may reach another device: no remote copies, remote signals or barrier semaphores. Data moves between devices by JAX's collectives and lax.ppermute only.
A program may use at most 64 MiB of HBM per device.

v0:
```python
import functools
import math

import jax
import jax.numpy as jnp
from jax import lax
from jax.experimental import pallas as pl
from jax.experimental.pallas import tpu as pltpu
from jax.sharding import PartitionSpec as P

TP = 12
TISS_MEAN = 8
BF = jnp.bfloat16
F32 = jnp.float32
SLOTS = 64


def swaps(size, distance):
    return [(i, i ^ distance) for i in range(size) if (i ^ distance) < size]


def odd_swaps(size):
    return [p for i in range(1, size - 1, 2) for p in ((i, i + 1), (i + 1, i))]


def neighbour_strips(first, last, axis):
    size = lax.axis_size(axis)
    even = lax.axis_index(axis) % 2 == 0
    if size == 1:
        return jnp.zeros_like(first), jnp.zeros_like(first)
    got_even = lax.ppermute(jnp.where(even, last, first), axis, swaps(size, 1))
    if size == 2:
        got_odd = jnp.zeros_like(first)
    else:
        got_odd = lax.ppermute(jnp.where(even, first, last), axis, odd_swaps(size))
    return jnp.where(even, got_odd, got_even), jnp.where(even, got_even, got_odd)


def joined_halves(own, axis_dim):
    other = lax.ppermute(own, "chan", [(0, 1), (1, 0)])
    low = lax.axis_index("chan") == 0
    return jnp.concatenate(
        [jnp.where(low, own, other), jnp.where(low, other, own)], axis=axis_dim
    )


def roll_columns(value, amount):
    return pltpu.roll(value, amount % SLOTS, axis=1)


def main_kernel(flags, a_ref, u_ref, wa_ref, w2_ref, shift_ref, grad_ref, weight_ref):
    rows = a_ref.shape[0] - 2
    tall = rows + 1
    own_cols = grad_ref.shape[2]
    lanes = a_ref.shape[3]

    def flat(value):
        return value.reshape(value.shape[0] * SLOTS, value.shape[2])

    def image(value):
        return value.reshape(value.shape[0] // SLOTS, SLOTS, value.shape[1])

    def a_rows(count):
        return jnp.concatenate(
            [
                flat(a_ref[0:count, 1]),
                flat(a_ref[1 : count + 1, 0]),
                flat(a_ref[1 : count + 1, 1]),
            ],
            axis=1,
        )

    def u_rows(count):
        return jnp.concatenate([flat(u_ref[5 - 2 * u : 5 - 2 * u + count]) for u in range(3)], axis=1)

    row_id = lax.broadcasted_iota(jnp.int32, (tall, SLOTS, lanes), 0)
    col_id = lax.broadcasted_iota(jnp.int32, (tall, SLOTS, lanes), 1)
    own = (row_id < rows) & (col_id < own_cols)
    last_row = rows + flags[0]
    last_col = own_cols + flags[1]
    valid = (row_id < last_row) & (col_id < last_col)

    wa = wa_ref[...]
    part = jnp.dot(a_rows(tall), wa, preferred_element_type=F32)
    pre = image(part[:, lanes:]) + roll_columns(image(part[:, :lanes]), 1) + shift_ref[0]
    middle = jnp.maximum(pre, 0.0).astype(BF).astype(F32)

    mid_part = jnp.dot(u_rows(tall), w2_ref[...], preferred_element_type=F32)
    mid_raw = (
        roll_columns(image(mid_part[:, :lanes]), -2)
        + image(mid_part[:, lanes : 2 * lanes])
        + roll_columns(image(mid_part[:, 2 * lanes :]), 2)
    )
    mid_grad = jnp.where((middle > 0) & valid, mid_raw, 0.0)

    middle_own = jnp.where(own, middle, 0.0)[:rows]
    middle_taps = jnp.concatenate(
        [
            flat(roll_columns(middle_own, 2)).astype(BF),
            flat(middle_own).astype(BF),
            flat(roll_columns(middle_own, -2)).astype(BF),
        ],
        axis=1,
    )
    over_pixels = (((0,), (0,)), ((), ()))
    second = lax.dot_general(middle_taps, u_rows(rows), over_pixels, preferred_element_type=F32)

    grad_own = jnp.where(own, mid_grad, 0.0)[:rows]
    grad_taps = jnp.concatenate(
        [flat(roll_columns(grad_own, -1)).astype(BF), flat(grad_own).astype(BF)], axis=1
    )
    first = lax.dot_general(a_rows(rows), grad_taps, over_pixels, preferred_element_type=F32)

    low = flags[2] == 0
    half = lanes // 2
    left = lax.broadcasted_iota(jnp.int32, (48, lanes), 1) < half
    for u in range(3):
        for w in range(3):
            a_row = u * lanes + (0 if w == 1 else half)
            a_col = 0 if w == 0 else lanes
            both = jnp.concatenate(
                [
                    second[w * lanes : (w + 1) * lanes, u * lanes : (u + 1) * lanes],
                    first[a_row : a_row + half, a_col : a_col + lanes],
                ],
                axis=0,
            )
            turned = pltpu.roll(both, half, axis=1)
            at_left = jnp.where(low, both, turned)
            at_right = jnp.where(low, turned, both)
            tap = u * 3 + w
            for h in range(2):
                packed = jnp.where(
                    left, at_left[96 * h : 96 * h + 48], at_right[96 * h + 48 : 96 * h + 96]
                )
                weight_ref[h, tap * 48 : tap * 48 + 48, :] = packed.astype(BF)

    by_lanes = (((1,), (1,)), ((), ()))
    grads = flat(mid_grad).astype(BF)
    straight = lax.dot_general(grads, wa[:, lanes:], by_lanes, preferred_element_type=F32)
    shifted = lax.dot_general(grads, wa[:, :lanes], by_lanes, preferred_element_type=F32)

    def taps(u):
        s = slice(u * lanes, (u + 1) * lanes)
        return image(straight[:, s]) + roll_columns(image(shifted[:, s]), -1)

    above, level, below = taps(0), taps(1), taps(2)
    grad_ref[:, 0] = level[:rows, :own_cols].astype(BF)
    grad_ref[:, 1] = (below[:rows, :own_cols] + above[1:tall, :own_cols]).astype(BF)


def unpack_kernel(scale, flags, own_ref, other_ref, first_ref, second_ref):
    low = flags[0] == 0
    half = first_ref.shape[2]
    for h in range(2):
        here = low if h == 0 else jnp.logical_not(low)
        for tap in range(9):
            rows = slice(tap * 48, tap * 48 + 48)
            value = (
                jnp.where(here, own_ref[rows, :].astype(F32), other_ref[rows, :].astype(F32)) * scale
            )
            for side in range(2):
                part = value[:, side * half : (side + 1) * half]
                start = 96 * h + 48 * side
                to_second = max(0, min(48, 128 - start))
                if to_second > 0:
                    second_ref[tap, start : start + to_second, :] = part[:to_second]
                if to_second < 48:
                    at = start + to_second - 128
                    first_ref[tap, at : at + 48 - to_second, :] = part[to_second:]


def summed_pair(value, axis, size, distance):
    got = lax.ppermute(value, axis, swaps(size, distance))
    return (value.astype(F32) + got.astype(F32)).astype(BF)


def shards(acts, shift, weight_one, weight_two, cotangent, tissue_count, tile_order):
    channels, mids = weight_one.shape[2], weight_one.shape[3]
    height = acts.shape[0]
    lanes = 2 * channels
    pairs = acts.shape[1] // lanes
    rows, cols = height // 2, pairs
    tile_rows, tile_cols = height // TP, 2 * pairs // TP
    out_side = TP // 2
    n_rows, n_tiles = lax.axis_size("rows"), lax.axis_size("tiles")
    row_index, tile_index = lax.axis_index("rows"), lax.axis_index("tiles")
    chan_index = lax.axis_index("chan")

    order = tile_order[0, 0]
    ranks = jnp.arange(order.shape[0], dtype=jnp.int32)
    hits = (order[:, None] == ranks[None, :]) & (ranks[:, None] < tissue_count[0, 0])
    tissue = jnp.sum(hits.astype(jnp.int32), axis=0).reshape(tile_rows, tile_cols)
    pixel_mask = jnp.repeat(jnp.repeat(tissue, out_side, axis=0), out_side, axis=1)
    masked = jnp.where(pixel_mask[:, :, None] > 0, cotangent, jnp.zeros_like(cotangent))
    upstream = joined_halves(masked, 2)
    second_full = joined_halves(weight_two, 3)

    picture = acts.reshape(height, pairs, lanes)
    strip = lambda a, u: jnp.concatenate([a, u], axis=0)
    before, after = neighbour_strips(
        strip(picture[:2], upstream[:3]), strip(picture[height - 2 :], upstream[rows - 3 :]), "rows"
    )
    tall_a = jnp.concatenate([before[:2], picture, after[:2]], axis=0)
    tall_u = jnp.concatenate([before[2:], upstream, after[2:]], axis=0)

    n_a, n_u = tall_a.shape[0], tall_u.shape[0]
    side = lambda a, u: jnp.concatenate([a.reshape(n_a, lanes), u.reshape(4 * n_u, lanes)], axis=0)
    before, after = neighbour_strips(
        side(tall_a[:, :1], tall_u[:, :4]), side(tall_a[:, cols - 1 :], tall_u[:, cols - 4 :]), "tiles"
    )

    def circular(middle, a, b):
        gap = SLOTS - cols - a.shape[1] - b.shape[1]
        fill = jnp.zeros((middle.shape[0], gap, lanes), BF)
        return jnp.concatenate([middle, a, fill, b], axis=1)

    full_a = circular(tall_a, after[:n_a].reshape(n_a, 1, lanes), before[:n_a].reshape(n_a, 1, lanes))
    full_u = circular(
        tall_u, after[n_a:].reshape(n_u, 4, lanes), before[n_a:].reshape(n_u, 4, lanes)
    )

    straight = weight_one[:, 1:].reshape(3, lanes, mids)
    shifted = jnp.concatenate([jnp.zeros_like(weight_one[:, 0]), weight_one[:, 0]], axis=1)
    wa = jnp.concatenate([shifted, straight], axis=2).reshape(3 * lanes, 2 * mids)
    w2 = second_full.transpose(0, 3, 1, 2).reshape(3 * lanes, 3 * mids)
    flags = jnp.stack(
        [
            (row_index < n_rows - 1).astype(jnp.int32),
            (tile_index < n_tiles - 1).astype(jnp.int32),
            chan_index,
        ]
    )
    whole = pl.BlockSpec(memory_space=pltpu.VMEM)
    scalars = pl.BlockSpec(memory_space=pltpu.SMEM)
    limit = pltpu.CompilerParams(vmem_limit_bytes=48 << 20)
    input_grad, weights = pl.pallas_call(
        main_kernel,
        out_shape=(
            jax.ShapeDtypeStruct((rows, 2, cols, lanes), BF),
            jax.ShapeDtypeStruct((2, 9 * 48, lanes), BF),
        ),
        in_specs=[scalars] + [whole] * 5,
        out_specs=(whole, whole),
        compiler_params=limit,
    )(flags, full_a.reshape(rows + 2, 2, SLOTS, lanes), full_u, wa, w2, shift.reshape(1, mids))

    even = row_index % 2 == 0
    if n_rows > 1:
        kept = jnp.where(even, weights[0], weights[1])
        sent = jnp.where(even, weights[1], weights[0])
        got = lax.ppermute(sent, "rows", swaps(n_rows, 1))
        total = (kept.astype(F32) + got.astype(F32)).astype(BF)
    distance = 2
    while distance < n_rows:
        total = summed_pair(total, "rows", n_rows, distance)
        distance *= 2
    if n_tiles == 4:
        one, two, three = (lax.ppermute(total, "tiles", swaps(4, d)) for d in (1, 2, 3))
        total = (
            (total.astype(F32) + one.astype(F32)) + (two.astype(F32) + three.astype(F32))
        ).astype(BF)
    else:
        distance = 1
        while distance < n_tiles:
            total = summed_pair(total, "tiles", n_tiles, distance)
            distance *= 2
    other = lax.ppermute(total, "rows", swaps(n_rows, 1))

    pixels = n_rows * TISS_MEAN * n_tiles * out_side * out_side
    scale = 1.0 / math.sqrt(pixels)
    half = mids // 2
    first, second = pl.pallas_call(
        functools.partial(unpack_kernel, scale),
        out_shape=(
            jax.ShapeDtypeStruct((9, channels, half), F32),
            jax.ShapeDtypeStruct((9, mids, half), F32),
        ),
        in_specs=[scalars, whole, whole],
        out_specs=(whole, whole),
        compiler_params=limit,
    )(row_index.reshape(1) % 2, total, other)
    return (
        input_grad.reshape(height, pairs * lanes),
        first.reshape(3, 3, channels, half),
        second.reshape(3, 3, mids, half),
    )


def solution(mesh):
    return jax.shard_map(
        shards,
        mesh=mesh,
        in_specs=(
            P(("groups", "rows"), "tiles"),
            P(),
            P(),
            P(None, None, None, "chan"),
            P(("groups", "rows"), "tiles", "chan"),
            P(("groups", "rows"), "tiles"),
            P(("groups", "rows"), "tiles", None),
        ),
        out_specs=(
            P(("groups", "rows"), "tiles"),
            P("groups", None, None, "chan"),
            P("groups", None, None, "chan"),
        ),
        check_vma=False,
    )
```

profile of v0, /device:TPU:0, one launch (start us, length us, event | category | flops | bytes accessed | tf_op | source)
XLA Modules:
  0.0 43.2 jit_solution(7828222345005704911)
XLA Ops:
  1.3 0.6 %copy-done.5 = s32[1,1,16]{2,1,0:T(1,128)S(1)} copy-done((s32[1,1,16]{2,1,0:T(1,128)S(1)}, s32[1,1,16]{2,1,0:T(1,128)}, u32[]{:S(2)}) %copy-start.5) | copy-done | bytes 88
  2.4 1.1 %broadcast_select_fusion.2 = bf16[12,48,64]{2,1,0:T(8,128)(2,1)S(1)} fusion(bf16[12,48,64]{2,1,0:T(8,128)(2,1)} %param.11, pred[12,48]{1,0:T(8,128)(4,1)S(1)} %gt.26), kind=kLoop, calls=%fused_computation.13 | loop fusion | flops 36864 | bytes 148032 | tf_op jit(solution)/shard_map/jit(_where)/select_n | solution.py:195
  3.5 0.5 %collective-permute-start = (bf16[12,48,64]{2,1,0:T(8,128)(2,1)S(1)}, bf16[12,48,64]{2,1,0:T(8,128)(2,1)S(1)}, u32[]{:S(2)}, u32[]{:S(2)}) collective-permute-start(bf16[12,48,64]{2,1,0:T(8,128)(2,1)S(1)} %broadcast_select_fusion.2), channel_id=1, source_target_pairs={{0,1},{1,0},{2,3},{3,2},{4,5},{5,4},{6,7},{7,6},{8,9},{9,8},{10,11... | collective-permute-start | bytes 221192 | tf_op jit(solution)/shard_map/ppermute | solution.py:40
  4.5 0.9 %slice-done = bf16[3,2,64,128]{3,2,1,0:T(8,128)(2,1)S(1)} async-done(((bf16[3,3,64,128]{3,2,1,0:T(8,128)(2,1)}), bf16[3,2,64,128]{3,2,1,0:T(8,128)(2,1)S(1)}, s32[]{:S(2)}) %slice-start) | async-done | bytes 98328 | tf_op jit(solution)/shard_map/slice | solution.py:223
  5.4 0.9 %copy-done.1 = bf16[12,48,64]{2,1,0:T(8,128)(2,1)S(1)} copy-done((bf16[12,48,64]{2,1,0:T(8,128)(2,1)S(1)}, bf16[12,48,64]{2,1,0:T(8,128)(2,1)}, u32[]{:S(2)}) %copy-start.1) | copy-done | bytes 73752
  6.2 0.1 broadcast_select_fusion.4
  6.4 0.1 fusion.5
  6.5 3.0 %collective-permute-start.1 = (bf16[5,48,128]{2,1,0:T(8,128)(2,1)S(1)}, bf16[5,48,128]{2,1,0:T(8,128)(2,1)S(1)}, u32[]{:S(2)}, u32[]{:S(2)}) collective-permute-start(bf16[5,48,128]{2,1,0:T(8,128)(2,1)S(1)} %fusion.5), channel_id=1, source_target_pairs={{0,2},{2,0},{1,3},{3,1},{4,6},{6,4},{5,7},{7,5},{8,10},{10,8},{9,1... | collective-permute-start | bytes 184328 | tf_op jit(solution)/shard_map/ppermute | solution.py:31
  9.5 2.2 %collective-permute-done.1 = bf16[5,48,128]{2,1,0:T(8,128)(2,1)S(1)} collective-permute-done((bf16[5,48,128]{2,1,0:T(8,128)(2,1)S(1)}, bf16[5,48,128]{2,1,0:T(8,128)(2,1)S(1)}, u32[]{:S(2)}, u32[]{:S(2)}) %collective-permute-start.1) | collective-permute-done | bytes 61472 | tf_op jit(solution)/shard_map/ppermute | solution.py:31
  11.8 0.2 pad_maximum_fusion.1
  12.1 0.1 copy.27
  12.3 2.1 %collective-permute-start.2 = (bf16[100,128]{1,0:T(8,128)(2,1)S(1)}, bf16[100,128]{1,0:T(8,128)(2,1)S(1)}, u32[]{:S(2)}, u32[]{:S(2)}) collective-permute-start(bf16[100,128]{1,0:T(8,128)(2,1)S(1)} %get-tuple-element.34), channel_id=1, source_target_pairs={{0,4},{4,0},{8,12},{12,8},{1,5},{5,1},{9,13},{13,9},{2,6},{6,2},{1... | collective-permute-start | bytes 76808 | tf_op jit(solution)/shard_map/ppermute | solution.py:31
  14.4 0.7 %collective-permute-start.3 = (bf16[100,128]{1,0:T(8,128)(2,1)S(1)}, bf16[100,128]{1,0:T(8,128)(2,1)S(1)}, u32[]{:S(2)}, u32[]{:S(2)}) collective-permute-start(bf16[100,128]{1,0:T(8,128)(2,1)S(1)} %get-tuple-element.35), channel_id=1, source_target_pairs={{4,8},{8,4},{5,9},{9,5},{6,10},{10,6},{7,11},{11,7},{20,24},{24,20... | collective-permute-start | bytes 76808 | tf_op jit(solution)/shard_map/ppermute | solution.py:35
  15.2 0.3 copy.30
  15.5 0.8 %collective-permute-done.2 = bf16[100,128]{1,0:T(8,128)(2,1)S(1)} collective-permute-done((bf16[100,128]{1,0:T(8,128)(2,1)S(1)}, bf16[100,128]{1,0:T(8,128)(2,1)S(1)}, u32[]{:S(2)}, u32[]{:S(2)}) %collective-permute-start.2) | collective-permute-done | bytes 25632 | tf_op jit(solution)/shard_map/ppermute | solution.py:31
  16.4 0.1 pad_maximum_fusion.2.u_ref
  16.5 0.2 pad_maximum_fusion.a_ref
  16.7 0.6 %copy-done = f32[128]{0:T(128)S(1)} copy-done((f32[128]{0:T(128)S(1)}, f32[128]{0:T(128)}, u32[]{:S(2)}) %copy-start) | copy-done | bytes 536
  17.4 2.2 %shard_map.94 = (bf16[12,2,48,128]{3,2,1,0:T(8,128)(2,1)S(1)}, bf16[2,432,128]{2,1,0:T(8,128)(2,1)S(1)}) custom-call(s32[3]{0:T(128)S(1)} %pad_add_fusion.flags, bf16[14,2,64,128]{3,2,1,0:T(8,128)(2,1)S(1)} %pad_maximum_fusion.a_ref, bf16[18,64,128]{2,1,0:T(8,128)(2,1)S(1)} %pad_maximum_fusion.2.u_ref, bf16[384,256]{1,0:T(8,128)(2,1)S(1)} %pad_maximum_fusion.3.wa_ref, ...), custom_call_target="tpu_custom_call" | custom-call | tf_op jit(solution)/shard_map/pallas_call | solution.py:237
  19.6 2.0 %collective-permute-start.5 = (bf16[432,128]{1,0:T(8,128)(2,1)S(1)}, bf16[432,128]{1,0:T(8,128)(2,1)S(1)}, u32[]{:S(2)}, u32[]{:S(2)}) collective-permute-start(bf16[432,128]{1,0:T(8,128)(2,1)S(1)} %select_bitcast_fusion), channel_id=1, source_target_pairs={{0,2},{2,0},{1,3},{3,1},{4,6},{6,4},{5,7},{7,5},{8,10},{10,8},{9,1... | collective-permute-start | bytes 331784 | tf_op jit(solution)/shard_map/ppermute | solution.py:252
  21.6 2.8 %collective-permute-done.5 = bf16[432,128]{1,0:T(8,128)(2,1)S(1)} collective-permute-done((bf16[432,128]{1,0:T(8,128)(2,1)S(1)}, bf16[432,128]{1,0:T(8,128)(2,1)S(1)}, u32[]{:S(2)}, u32[]{:S(2)}) %collective-permute-start.5) | collective-permute-done | bytes 110624 | tf_op jit(solution)/shard_map/ppermute | solution.py:252
  24.4 4.1 %collective-permute-start.8 = (bf16[432,128]{1,0:T(8,128)(2,1)S(1)}, bf16[432,128]{1,0:T(8,128)(2,1)S(1)}, u32[]{:S(2)}, u32[]{:S(2)}) collective-permute-start(bf16[432,128]{1,0:T(8,128)(2,1)S(1)} %fusion), channel_id=1, source_target_pairs={{0,12},{4,8},{8,4},{12,0},{1,13},{5,9},{9,5},{13,1},{2,14},{6,10},... | collective-permute-start | bytes 331784 | tf_op jit(solution)/shard_map/ppermute | solution.py:259
  28.5 2.5 %collective-permute-start.7 = (bf16[432,128]{1,0:T(8,128)(2,1)S(1)}, bf16[432,128]{1,0:T(8,128)(2,1)S(1)}, u32[]{:S(2)}, u32[]{:S(2)}) collective-permute-start(bf16[432,128]{1,0:T(8,128)(2,1)S(1)} %fusion), channel_id=1, source_target_pairs={{0,8},{4,12},{8,0},{12,4},{1,9},{5,13},{9,1},{13,5},{2,10},{6,14},... | collective-permute-start | bytes 331784 | tf_op jit(solution)/shard_map/ppermute | solution.py:259
  31.1 0.5 %collective-permute-start.6 = (bf16[432,128]{1,0:T(8,128)(2,1)S(1)}, bf16[432,128]{1,0:T(8,128)(2,1)S(1)}, u32[]{:S(2)}, u32[]{:S(2)}) collective-permute-start(bf16[432,128]{1,0:T(8,128)(2,1)S(1)} %fusion), channel_id=1, source_target_pairs={{0,4},{4,0},{8,12},{12,8},{1,5},{5,1},{9,13},{13,9},{2,6},{6,2},{1... | collective-permute-start | bytes 331784 | tf_op jit(solution)/shard_map/ppermute | solution.py:259
  31.6 0.6 %collective-permute-done.8 = bf16[432,128]{1,0:T(8,128)(2,1)S(1)} collective-permute-done((bf16[432,128]{1,0:T(8,128)(2,1)S(1)}, bf16[432,128]{1,0:T(8,128)(2,1)S(1)}, u32[]{:S(2)}, u32[]{:S(2)}) %collective-permute-start.8) | collective-permute-done | bytes 110624 | tf_op jit(solution)/shard_map/ppermute | solution.py:259
  32.2 3.2 %collective-permute-done.7 = bf16[432,128]{1,0:T(8,128)(2,1)S(1)} collective-permute-done((bf16[432,128]{1,0:T(8,128)(2,1)S(1)}, bf16[432,128]{1,0:T(8,128)(2,1)S(1)}, u32[]{:S(2)}, u32[]{:S(2)}) %collective-permute-start.7) | collective-permute-done | bytes 110624 | tf_op jit(solution)/shard_map/ppermute | solution.py:259
  35.4 1.1 %collective-permute-done.6 = bf16[432,128]{1,0:T(8,128)(2,1)S(1)} collective-permute-done((bf16[432,128]{1,0:T(8,128)(2,1)S(1)}, bf16[432,128]{1,0:T(8,128)(2,1)S(1)}, u32[]{:S(2)}, u32[]{:S(2)}) %collective-permute-start.6) | collective-permute-done | bytes 110624 | tf_op jit(solution)/shard_map/ppermute | solution.py:259
  36.6 1.6 %collective-permute-start.9 = (bf16[432,128]{1,0:T(8,128)(2,1)S(1)}, bf16[432,128]{1,0:T(8,128)(2,1)S(1)}, u32[]{:S(2)}, u32[]{:S(2)}) collective-permute-start(bf16[432,128]{1,0:T(8,128)(2,1)S(1)} %add_convert_fusion.own_ref), channel_id=1, source_target_pairs={{0,2},{2,0},{1,3},{3,1},{4,6},{6,4},{5,7},{7,5},{8,10},{10,8},{9,1... | collective-permute-start | bytes 331784 | tf_op jit(solution)/shard_map/ppermute | solution.py:268
  38.1 0.8 %copy.42 = bf16[3,8,48,128]{3,1,2,0:T(8,128)(2,1)} copy(bf16[3,8,48,128]{3,2,1,0:T(8,128)(2,1)S(1)} %bitcast.55) | data formatting | bytes 589824
  38.9 2.5 %collective-permute-done.9.other_ref = bf16[432,128]{1,0:T(8,128)(2,1)S(1)} collective-permute-done((bf16[432,128]{1,0:T(8,128)(2,1)S(1)}, bf16[432,128]{1,0:T(8,128)(2,1)S(1)}, u32[]{:S(2)}, u32[]{:S(2)}) %collective-permute-start.9) | collective-permute-done | bytes 110624 | tf_op jit(solution)/shard_map/ppermute | solution.py:268
  41.4 0.9 %shard_map.95 = (f32[9,64,64]{2,1,0:T(8,128)}, f32[9,128,64]{2,1,0:T(8,128)S(1)}) custom-call(s32[1]{0:T(128)S(6)} %select_n.117.flags, bf16[432,128]{1,0:T(8,128)(2,1)S(1)} %add_convert_fusion.own_ref, bf16[432,128]{1,0:T(8,128)(2,1)S(1)} %collective-permute-done.9.other_ref), custom_call_target="tpu_custom_call" | custom-call | tf_op jit(solution)/shard_map/pallas_call | solution.py:273
  42.3 0.9 %copy.31 = f32[3,3,128,64]{2,3,1,0:T(8,128)} copy(f32[3,3,128,64]{3,2,1,0:T(8,128)S(1)} %bitcast.54) | data formatting | bytes 589824
  (56 shorter events, 1.4 us)
Async XLA Ops:
  1.3 0.7 %copy-start.5 = (s32[1,1,16]{2,1,0:T(1,128)S(1)}, s32[1,1,16]{2,1,0:T(1,128)}, u32[]{:S(2)}) copy-start(s32[1,1,16]{2,1,0:T(1,128)} %param.13) | copy-start | bytes 196
  2.3 1.8 %copy-start.4 = (bf16[3,3,128,64]{2,3,1,0:T(8,128)(2,1)S(1)}, bf16[3,3,128,64]{2,3,1,0:T(8,128)(2,1)}, u32[]{:S(2)}) copy-start(bf16[3,3,128,64]{2,3,1,0:T(8,128)(2,1)} %param.10) | copy-start | bytes 442372
  2.3 1.8 %copy-start.3 = (bf16[3,3,64,128]{3,2,1,0:T(8,128)(2,1)S(1)}, bf16[3,3,64,128]{3,2,1,0:T(8,128)(2,1)}, u32[]{:S(2)}) copy-start(bf16[3,3,64,128]{3,2,1,0:T(8,128)(2,1)} %param.9) | copy-start | bytes 442372
  2.4 1.7 %copy-start.2 = (bf16[24,6144]{1,0:T(8,128)(2,1)S(1)}, bf16[24,6144]{1,0:T(8,128)(2,1)}, u32[]{:S(2)}) copy-start(bf16[24,6144]{1,0:T(8,128)(2,1)} %param.7) | copy-start | bytes 884740
  3.5 1.9 %collective-permute-start = (bf16[12,48,64]{2,1,0:T(8,128)(2,1)S(1)}, bf16[12,48,64]{2,1,0:T(8,128)(2,1)S(1)}, u32[]{:S(2)}, u32[]{:S(2)}) collective-permute-start(bf16[12,48,64]{2,1,0:T(8,128)(2,1)S(1)} %broadcast_select_fusion.2), channel_id=1, source_target_pairs={{0,1},{1,0},{2,3},{3,2},{4,5},{5,4},{6,7},{7,6},{8,9},{9,8},{10,11... | collective-permute-start | bytes 221192 | tf_op jit(solution)/shard_map/ppermute | solution.py:40
  4.0 11.1 %collective-permute-start.4 = (bf16[3,3,128,64]{2,3,1,0:T(8,128)(2,1)S(1)}, bf16[3,3,128,64]{2,3,1,0:T(8,128)(2,1)S(1)}, u32[]{:S(2)}, u32[]{:S(2)}) collective-permute-start(bf16[3,3,128,64]{2,3,1,0:T(8,128)(2,1)S(1)} %copy-done.4), channel_id=1, source_target_pairs={{0,1},{1,0},{2,3},{3,2},{4,5},{5,4},{6,7},{7,6},{8,9},{9,8},{10,11... | collective-permute-start | bytes 442376 | tf_op jit(solution)/shard_map/ppermute | solution.py:40
  4.4 0.9 %slice-start = ((bf16[3,3,64,128]{3,2,1,0:T(8,128)(2,1)}), bf16[3,2,64,128]{3,2,1,0:T(8,128)(2,1)S(1)}, s32[]{:S(2)}) async-start(bf16[3,3,64,128]{3,2,1,0:T(8,128)(2,1)} %param.9), calls=%async_computation | async-start | bytes 196608 | tf_op jit(solution)/shard_map/slice | solution.py:223
  5.3 0.9 %copy-start.1 = (bf16[12,48,64]{2,1,0:T(8,128)(2,1)S(1)}, bf16[12,48,64]{2,1,0:T(8,128)(2,1)}, u32[]{:S(2)}) copy-start(bf16[12,48,64]{2,1,0:T(8,128)(2,1)} %param.11) | copy-start | bytes 221188
  6.5 5.2 %collective-permute-start.1 = (bf16[5,48,128]{2,1,0:T(8,128)(2,1)S(1)}, bf16[5,48,128]{2,1,0:T(8,128)(2,1)S(1)}, u32[]{:S(2)}, u32[]{:S(2)}) collective-permute-start(bf16[5,48,128]{2,1,0:T(8,128)(2,1)S(1)} %fusion.5), channel_id=1, source_target_pairs={{0,2},{2,0},{1,3},{3,1},{4,6},{6,4},{5,7},{7,5},{8,10},{10,8},{9,1... | collective-permute-start | bytes 184328 | tf_op jit(solution)/shard_map/ppermute | solution.py:31
  12.3 3.9 %collective-permute-start.2 = (bf16[100,128]{1,0:T(8,128)(2,1)S(1)}, bf16[100,128]{1,0:T(8,128)(2,1)S(1)}, u32[]{:S(2)}, u32[]{:S(2)}) collective-permute-start(bf16[100,128]{1,0:T(8,128)(2,1)S(1)} %get-tuple-element.34), channel_id=1, source_target_pairs={{0,4},{4,0},{8,12},{12,8},{1,5},{5,1},{9,13},{13,9},{2,6},{6,2},{1... | collective-permute-start | bytes 76808 | tf_op jit(solution)/shard_map/ppermute | solution.py:31
  14.4 1.8 %collective-permute-start.3 = (bf16[100,128]{1,0:T(8,128)(2,1)S(1)}, bf16[100,128]{1,0:T(8,128)(2,1)S(1)}, u32[]{:S(2)}, u32[]{:S(2)}) collective-permute-start(bf16[100,128]{1,0:T(8,128)(2,1)S(1)} %get-tuple-element.35), channel_id=1, source_target_pairs={{4,8},{8,4},{5,9},{9,5},{6,10},{10,6},{7,11},{11,7},{20,24},{24,20... | collective-permute-start | bytes 76808 | tf_op jit(solution)/shard_map/ppermute | solution.py:35
  16.7 0.7 %copy-start = (f32[128]{0:T(128)S(1)}, f32[128]{0:T(128)}, u32[]{:S(2)}) copy-start(f32[128]{0:T(128)} %param.8) | copy-start | bytes 1540
  19.6 4.8 %collective-permute-start.5 = (bf16[432,128]{1,0:T(8,128)(2,1)S(1)}, bf16[432,128]{1,0:T(8,128)(2,1)S(1)}, u32[]{:S(2)}, u32[]{:S(2)}) collective-permute-start(bf16[432,128]{1,0:T(8,128)(2,1)S(1)} %select_bitcast_fusion), channel_id=1, source_target_pairs={{0,2},{2,0},{1,3},{3,1},{4,6},{6,4},{5,7},{7,5},{8,10},{10,8},{9,1... | collective-permute-start | bytes 331784 | tf_op jit(solution)/shard_map/ppermute | solution.py:252
  24.4 7.7 %collective-permute-start.8 = (bf16[432,128]{1,0:T(8,128)(2,1)S(1)}, bf16[432,128]{1,0:T(8,128)(2,1)S(1)}, u32[]{:S(2)}, u32[]{:S(2)}) collective-permute-start(bf16[432,128]{1,0:T(8,128)(2,1)S(1)} %fusion), channel_id=1, source_target_pairs={{0,12},{4,8},{8,4},{12,0},{1,13},{5,9},{9,5},{13,1},{2,14},{6,10},... | collective-permute-start | bytes 331784 | tf_op jit(solution)/shard_map/ppermute | solution.py:259
  28.5 6.8 %collective-permute-start.7 = (bf16[432,128]{1,0:T(8,128)(2,1)S(1)}, bf16[432,128]{1,0:T(8,128)(2,1)S(1)}, u32[]{:S(2)}, u32[]{:S(2)}) collective-permute-start(bf16[432,128]{1,0:T(8,128)(2,1)S(1)} %fusion), channel_id=1, source_target_pairs={{0,8},{4,12},{8,0},{12,4},{1,9},{5,13},{9,1},{13,5},{2,10},{6,14},... | collective-permute-start | bytes 331784 | tf_op jit(solution)/shard_map/ppermute | solution.py:259
  31.1 5.4 %collective-permute-start.6 = (bf16[432,128]{1,0:T(8,128)(2,1)S(1)}, bf16[432,128]{1,0:T(8,128)(2,1)S(1)}, u32[]{:S(2)}, u32[]{:S(2)}) collective-permute-start(bf16[432,128]{1,0:T(8,128)(2,1)S(1)} %fusion), channel_id=1, source_target_pairs={{0,4},{4,0},{8,12},{12,8},{1,5},{5,1},{9,13},{13,9},{2,6},{6,2},{1... | collective-permute-start | bytes 331784 | tf_op jit(solution)/shard_map/ppermute | solution.py:259
  36.6 4.8 %collective-permute-start.9 = (bf16[432,128]{1,0:T(8,128)(2,1)S(1)}, bf16[432,128]{1,0:T(8,128)(2,1)S(1)}, u32[]{:S(2)}, u32[]{:S(2)}) collective-permute-start(bf16[432,128]{1,0:T(8,128)(2,1)S(1)} %add_convert_fusion.own_ref), channel_id=1, source_target_pairs={{0,2},{2,0},{1,3},{3,1},{4,6},{6,4},{5,7},{7,5},{8,10},{10,8},{9,1... | collective-permute-start | bytes 331784 | tf_op jit(solution)/shard_map/ppermute | solution.py:268
where the time goes:
time: 43.5 us; the launch traced here: 43.2 us
  starting transfers between devices  17 us (39%)
  waiting for transfers between devices  13.2 us (30%)
  local copies, waits for them, and re-layouts  5.9 us (14%)
  Pallas kernels  3.09 us (7%)
  other arithmetic  2.39 us (5%)
  between operations  1.64 us (4%)
    ppermute x3, starting transfers between devices, shards(): lax.ppermute(total, 'tiles', swaps(4, d))  7.11 us
    ppermute x2, starting transfers between devices, neighbour_strips(): got_even = lax.ppermute(jnp.where(even, last, first), axis, swaps(size, 1))  5.09 us
    ppermute x3, waiting for transfers between devices, shards(): lax.ppermute(total, 'tiles', swaps(4, d))  4.94 us
    unnamed x16, local copies, waits for them, and re-layouts  4 us
    ppermute x2, waiting for transfers between devices, neighbour_strips(): got_even = lax.ppermute(jnp.where(even, last, first), axis, swaps(size, 1))  2.96 us
    ppermute x1, waiting for transfers between devices, shards(): got = lax.ppermute(sent, 'rows', swaps(n_rows, 1))  2.81 us
    ppermute x1, waiting for transfers between devices, shards(): other = lax.ppermute(total, 'rows', swaps(n_rows, 1))  2.47 us
    pallas_call x1, Pallas kernels, shards(): pl.pallas_call(main_kernel, out_shape=(jax.ShapeDtypeStruct((rows, 2, col...  2.17 us
  transfers between devices with their start and end apart: 10, of which 7 were waited for; matrix products, arithmetic and copies ran while one was open for 5% of the time, Pallas kernels for 0%

commit v1 on v0

--- a/solution.py
+++ b/solution.py
@@ -36,23 +36,58 @@
     return jnp.where(even, got_odd, got_even), jnp.where(even, got_even, got_odd)
 
 
-def joined_halves(own, axis_dim):
-    other = lax.ppermute(own, "chan", [(0, 1), (1, 0)])
-    low = lax.axis_index("chan") == 0
-    return jnp.concatenate(
-        [jnp.where(low, own, other), jnp.where(low, other, own)], axis=axis_dim
-    )
-
-
 def roll_columns(value, amount):
     return pltpu.roll(value, amount % SLOTS, axis=1)
 
 
-def main_kernel(flags, a_ref, u_ref, wa_ref, w2_ref, shift_ref, grad_ref, weight_ref):
+def prepare_kernel(count, order, chan, cot_hbm, w1_hbm, z_ref, wa_ref, cot, w1, tissue, sems):
+    copies = [
+        pltpu.make_async_copy(cot_hbm, cot, sems.at[0]),
+        pltpu.make_async_copy(w1_hbm, w1, sems.at[1]),
+    ]
+    for copy in copies:
+        copy.start()
+    tiles = order.shape[2]
+    for k in range(tiles):
+        tissue[order[0, 0, k]] = jnp.where(k < count[0, 0], 1, 0)
+    rows, cols, half = cot.shape
+    side = TP // 2
+    across = cols // side
+    col_id = lax.broadcasted_iota(jnp.int32, (cols, 2 * half), 0)
+    lane_id = lax.broadcasted_iota(jnp.int32, (cols, 2 * half), 1)
+    mine = (lane_id < half) == (chan[0] == 0)
+    masks = []
+    for a in range(rows // side):
+        live = jnp.zeros((cols, 2 * half), jnp.int32)
+        for b in range(across):
+            inside = (col_id >= b * side) & (col_id < (b + 1) * side)
+            live = jnp.where(inside, tissue[a * across + b], live)
+        masks.append((live > 0) & mine)
+    copies[0].wait()
+    for i in range(rows):
+        value = cot[i].astype(F32)
+        twice = jnp.concatenate([value, value], axis=1)
+        z_ref[i] = jnp.where(masks[i // side], twice, 0.0).astype(BF)
+    copies[1].wait()
+    lanes = 2 * half
+    for u in range(3):
+        low = slice(u * lanes, u * lanes + half)
+        high = slice(u * lanes + half, (u + 1) * lanes)
+        wa_ref[low, :lanes] = jnp.zeros((half, lanes), BF)
+        wa_ref[high, :lanes] = w1[u, 0]
+        wa_ref[low, lanes:] = w1[u, 1]
+        wa_ref[high, lanes:] = w1[u, 2]
+
+
+def main_kernel(
+    flags, a_ref, u_ref, wa_ref, own_w2, other_w2, shift_ref, grad_ref, weight_ref, w2_ref
+):
     rows = a_ref.shape[0] - 2
     tall = rows + 1
     own_cols = grad_ref.shape[2]
     lanes = a_ref.shape[3]
+    half = lanes // 2
+    low = flags[2] == 0
 
     def flat(value):
         return value.reshape(value.shape[0] * SLOTS, value.shape[2])
@@ -73,6 +108,13 @@
     def u_rows(count):
         return jnp.concatenate([flat(u_ref[5 - 2 * u : 5 - 2 * u + count]) for u in range(3)], axis=1)
 
+    for u in range(3):
+        for w in range(3):
+            own_w, other_w = own_w2[u, w], other_w2[u, w]
+            across = slice(w * lanes, (w + 1) * lanes)
+            w2_ref[u * lanes : u * lanes + half, across] = jnp.where(low, own_w, other_w)
+            w2_ref[u * lanes + half : (u + 1) * lanes, across] = jnp.where(low, other_w, own_w)
+
     row_id = lax.broadcasted_iota(jnp.int32, (tall, SLOTS, lanes), 0)
     col_id = lax.broadcasted_iota(jnp.int32, (tall, SLOTS, lanes), 1)
     own = (row_id < rows) & (col_id < own_cols)
@@ -103,7 +145,7 @@
         axis=1,
     )
     over_pixels = (((0,), (0,)), ((), ()))
-    second = lax.dot_general(middle_taps, u_rows(rows), over_pixels, preferred_element_type=F32)
+    second = lax.dot_general(u_rows(rows), middle_taps, over_pixels, preferred_element_type=F32)
 
     grad_own = jnp.where(own, mid_grad, 0.0)[:rows]
     grad_taps = jnp.concatenate(
@@ -111,29 +153,32 @@
     )
     first = lax.dot_general(a_rows(rows), grad_taps, over_pixels, preferred_element_type=F32)
 
-    low = flags[2] == 0
-    half = lanes // 2
-    left = lax.broadcasted_iota(jnp.int32, (48, lanes), 1) < half
+    left = lax.broadcasted_iota(jnp.int32, (half, lanes), 1) < half
+
+    def keep(block, value):
+        at = block % 7 * half
+        weight_ref[block // 7, at : at + half, :] = value.astype(BF)
+
+    def at_left(value):
+        return jnp.where(low, value, pltpu.roll(value, half, axis=1))
+
+    def at_right(value):
+        return jnp.where(low, pltpu.roll(value, half, axis=1), value)
+
+    centre = []
     for u in range(3):
+        top = u * lanes
         for w in range(3):
-            a_row = u * lanes + (0 if w == 1 else half)
-            a_col = 0 if w == 0 else lanes
-            both = jnp.concatenate(
-                [
-                    second[w * lanes : (w + 1) * lanes, u * lanes : (u + 1) * lanes],
-                    first[a_row : a_row + half, a_col : a_col + lanes],
-                ],
-                axis=0,
+            across = slice(w * lanes, (w + 1) * lanes)
+            keep(
+                u * 3 + w,
+                jnp.where(low, second[top : top + half, across], second[top + half : top + lanes, across]),
             )
-            turned = pltpu.roll(both, half, axis=1)
-            at_left = jnp.where(low, both, turned)
-            at_right = jnp.where(low, turned, both)
-            tap = u * 3 + w
-            for h in range(2):
-                packed = jnp.where(
-                    left, at_left[96 * h : 96 * h + 48], at_right[96 * h + 48 : 96 * h + 96]
-                )
-                weight_ref[h, tap * 48 : tap * 48 + 48, :] = packed.astype(BF)
+        outer = first[top + half : top + lanes]
+        keep(9 + u, jnp.where(left, at_left(outer[:, :lanes]), at_right(outer[:, lanes:])))
+        centre.append(first[top : top + half, lanes:])
+    keep(12, jnp.where(left, at_left(centre[0]), at_right(centre[1])))
+    keep(13, at_left(centre[2]))
 
     by_lanes = (((1,), (1,)), ((), ()))
     grads = flat(mid_grad).astype(BF)
@@ -152,22 +197,22 @@
 def unpack_kernel(scale, flags, own_ref, other_ref, first_ref, second_ref):
     low = flags[0] == 0
     half = first_ref.shape[2]
-    for h in range(2):
-        here = low if h == 0 else jnp.logical_not(low)
-        for tap in range(9):
-            rows = slice(tap * 48, tap * 48 + 48)
-            value = (
-                jnp.where(here, own_ref[rows, :].astype(F32), other_ref[rows, :].astype(F32)) * scale
-            )
-            for side in range(2):
-                part = value[:, side * half : (side + 1) * half]
-                start = 96 * h + 48 * side
-                to_second = max(0, min(48, 128 - start))
-                if to_second > 0:
-                    second_ref[tap, start : start + to_second, :] = part[:to_second]
-                if to_second < 48:
-                    at = start + to_second - 128
-                    first_ref[tap, at : at + 48 - to_second, :] = part[to_second:]
+
+    def block(number):
+        here = low if number < 7 else jnp.logical_not(low)
+        rows = slice(number % 7 * half, number % 7 * half + half)
+        return jnp.where(here, own_ref[rows, :].astype(F32), other_ref[rows, :].astype(F32)) * scale
+
+    for tap in range(9):
+        second_ref[tap] = block(tap)
+    for u in range(3):
+        value = block(9 + u)
+        first_ref[3 * u] = value[:, :half]
+        first_ref[3 * u + 2] = value[:, half:]
+    value = block(12)
+    first_ref[1] = value[:, :half]
+    first_ref[4] = value[:, half:]
+    first_ref[7] = block(13)[:, :half]
 
 
 def summed_pair(value, axis, size, distance):
@@ -187,14 +232,31 @@
     row_index, tile_index = lax.axis_index("rows"), lax.axis_index("tiles")
     chan_index = lax.axis_index("chan")
 
-    order = tile_order[0, 0]
-    ranks = jnp.arange(order.shape[0], dtype=jnp.int32)
-    hits = (order[:, None] == ranks[None, :]) & (ranks[:, None] < tissue_count[0, 0])
-    tissue = jnp.sum(hits.astype(jnp.int32), axis=0).reshape(tile_rows, tile_cols)
-    pixel_mask = jnp.repeat(jnp.repeat(tissue, out_side, axis=0), out_side, axis=1)
-    masked = jnp.where(pixel_mask[:, :, None] > 0, cotangent, jnp.zeros_like(cotangent))
-    upstream = joined_halves(masked, 2)
-    second_full = joined_halves(weight_two, 3)
+    whole = pl.BlockSpec(memory_space=pltpu.VMEM)
+    scalars = pl.BlockSpec(memory_space=pltpu.SMEM)
+    in_place = pl.BlockSpec(memory_space=pl.ANY)
+    limit = pltpu.CompilerParams(vmem_limit_bytes=48 << 20)
+    half = channels
+    placed, wa = pl.pallas_call(
+        prepare_kernel,
+        out_shape=(
+            jax.ShapeDtypeStruct((rows, cols, lanes), BF),
+            jax.ShapeDtypeStruct((3 * lanes, 2 * mids), BF),
+        ),
+        in_specs=[scalars, scalars, scalars, in_place, in_place],
+        out_specs=(whole, whole),
+        scratch_shapes=[
+            pltpu.VMEM((rows, cols, half), BF),
+            pltpu.VMEM((3, 3, channels, mids), BF),
+            pltpu.SMEM((tile_rows * tile_cols,), jnp.int32),
+            pltpu.SemaphoreType.DMA((2,)),
+        ],
+        compiler_params=limit,
+    )(tissue_count, tile_order, chan_index.reshape(1), cotangent, weight_one)
+    core_swap = [(0, 1), (1, 0)]
+    upstream = placed + lax.ppermute(placed, "chan", core_swap)
+    own_w2 = weight_two.swapaxes(2, 3)
+    other_w2 = lax.ppermute(own_w2, "chan", core_swap)
 
     picture = acts.reshape(height, pairs, lanes)
     strip = lambda a, u: jnp.concatenate([a, u], axis=0)
@@ -220,10 +282,6 @@
         tall_u, after[n_a:].reshape(n_u, 4, lanes), before[n_a:].reshape(n_u, 4, lanes)
     )
 
-    straight = weight_one[:, 1:].reshape(3, lanes, mids)
-    shifted = jnp.concatenate([jnp.zeros_like(weight_one[:, 0]), weight_one[:, 0]], axis=1)
-    wa = jnp.concatenate([shifted, straight], axis=2).reshape(3 * lanes, 2 * mids)
-    w2 = second_full.transpose(0, 3, 1, 2).reshape(3 * lanes, 3 * mids)
     flags = jnp.stack(
         [
             (row_index < n_rows - 1).astype(jnp.int32),
@@ -231,19 +289,25 @@
             chan_index,
         ]
     )
-    whole = pl.BlockSpec(memory_space=pltpu.VMEM)
-    scalars = pl.BlockSpec(memory_space=pltpu.SMEM)
-    limit = pltpu.CompilerParams(vmem_limit_bytes=48 << 20)
     input_grad, weights = pl.pallas_call(
         main_kernel,
         out_shape=(
             jax.ShapeDtypeStruct((rows, 2, cols, lanes), BF),
-            jax.ShapeDtypeStruct((2, 9 * 48, lanes), BF),
-        ),
-        in_specs=[scalars] + [whole] * 5,
+            jax.ShapeDtypeStruct((2, 7 * half, lanes), BF),
+        ),
+        in_specs=[scalars] + [whole] * 6,
         out_specs=(whole, whole),
+        scratch_shapes=[pltpu.VMEM((3 * lanes, 3 * mids), BF)],
         compiler_params=limit,
-    )(flags, full_a.reshape(rows + 2, 2, SLOTS, lanes), full_u, wa, w2, shift.reshape(1, mids))
+    )(
+        flags,
+        full_a.reshape(rows + 2, 2, SLOTS, lanes),
+        full_u,
+        wa,
+        own_w2,
+        other_w2,
+        shift.reshape(1, mids),
+    )
 
     even = row_index % 2 == 0
     if n_rows > 1:
@@ -269,12 +333,11 @@
 
     pixels = n_rows * TISS_MEAN * n_tiles * out_side * out_side
     scale = 1.0 / math.sqrt(pixels)
-    half = mids // 2
     first, second = pl.pallas_call(
         functools.partial(unpack_kernel, scale),
         out_shape=(
             jax.ShapeDtypeStruct((9, channels, half), F32),
-            jax.ShapeDtypeStruct((9, mids, half), F32),
+            jax.ShapeDtypeStruct((9, half, mids), F32),
         ),
         in_specs=[scalars, whole, whole],
         out_specs=(whole, whole),
@@ -283,7 +346,7 @@
     return (
         input_grad.reshape(height, pairs * lanes),
         first.reshape(3, 3, channels, half),
-        second.reshape(3, 3, mids, half),
+        second.reshape(3, 3, half, mids).swapaxes(2, 3),
     )
 
 

time: 43.5 us -> 43.6 us (level)
  waiting for transfers between devices: 13.2 us -> 16.1 us
  other arithmetic: 2.39 us -> 0.85 us
  local copies, waits for them, and re-layouts: 5.9 us -> 4.53 us
  Pallas kernels: 3.09 us -> 4.18 us
  starting transfers between devices: 17 us -> 16.2 us
    select_n x3 -> x0, other arithmetic: 1.27 us -> none  [the longest x1 1.1 us: shards(): jnp.where(pixel_mask[:, :, None] > 0, cotangent, jnp.zeros_like(cotangent))]
    ppermute x2, waiting for transfers between devices: 0.01 us -> 1.25 us  [the longest x1 1.25 us: shards(): upstream = placed + lax.ppermute(placed, 'chan', core_swap)]
    pallas_call x0 -> x1, Pallas kernels: none -> 1.12 us  [shards(): pl.pallas_call(prepare_kernel, out_shape=(jax.ShapeDtypeStruct((rows, col...]
    ppermute x3, waiting for transfers between devices: 4.94 us -> 5.86 us  [shards(): lax.ppermute(total, 'tiles', swaps(4, d))]
    slice x2 -> x1, local copies, waits for them, and re-layouts: 0.86 us -> 0.01 us  [shards(): upstream[:3]]
    ppermute x2, starting transfers between devices: 5.09 us -> 4.6 us  [neighbour_strips(): got_even = lax.ppermute(jnp.where(even, last, first), axis, swaps(size, 1))]
    ppermute x2, waiting for transfers between devices: 2.96 us -> 3.42 us  [neighbour_strips(): got_even = lax.ppermute(jnp.where(even, last, first), axis, swaps(size, 1))]
    unnamed x16 -> x14, local copies, waits for them, and re-layouts: 4 us -> 4.05 us
  transfers between devices with their start and end apart: 10 -> 10, of which waited for: 7 -> 7; matrix products, arithmetic and copies ran while one was open for 5% -> 5% of each run, Pallas kernels for 0% -> 3%
where the time goes in v1:
time: 43.6 us; the launch traced here: 43.4 us
  starting transfers between devices  16.2 us (37%)
  waiting for transfers between devices  16.1 us (37%)
  local copies, waits for them, and re-layouts  4.53 us (10%)
  Pallas kernels  4.18 us (10%)
  between operations  1.55 us (4%)
  other arithmetic  0.85 us (2%)
    ppermute x3, starting transfers between devices, shards(): lax.ppermute(total, 'tiles', swaps(4, d))  6.92 us
    ppermute x3, waiting for transfers between devices, shards(): lax.ppermute(total, 'tiles', swaps(4, d))  5.86 us
    ppermute x2, starting transfers between devices, neighbour_strips(): got_even = lax.ppermute(jnp.where(even, last, first), axis, swaps(size, 1))  4.6 us
    unnamed x14, local copies, waits for them, and re-layouts  4.05 us
    ppermute x2, waiting for transfers between devices, neighbour_strips(): got_even = lax.ppermute(jnp.where(even, last, first), axis, swaps(size, 1))  3.42 us
    ppermute x1, waiting for transfers between devices, shards(): got = lax.ppermute(sent, 'rows', swaps(n_rows, 1))  3.05 us
    ppermute x1, waiting for transfers between devices, shards(): other = lax.ppermute(total, 'rows', swaps(n_rows, 1))  2.51 us
    pallas_call x1, Pallas kernels, shards(): pl.pallas_call(main_kernel, out_shape=(jax.ShapeDtypeStruct((rows, 2, col...  2.17 us
  transfers between devices with their start and end apart: 10, of which 7 were waited for; matrix products, arithmetic and copies ran while one was open for 5% of the time, Pallas kernels for 3%

profile of v1, /device:TPU:0, one launch (start us, length us, event | category | flops | bytes accessed | tf_op | source)
XLA Modules:
  0.0 43.4 jit_solution(16614656138998331952)
XLA Ops:
  0.6 0.5 %collective-permute-start.4 = (bf16[3,3,64,128]{3,2,1,0:T(8,128)(2,1)}, bf16[3,3,64,128]{3,2,1,0:T(8,128)(2,1)S(1)}, u32[]{:S(2)}, u32[]{:S(2)}) collective-permute-start(bf16[3,3,64,128]{3,2,1,0:T(8,128)(2,1)} %bitcast.43), channel_id=1, source_target_pairs={{0,1},{1,0},{2,3},{3,2},{4,5},{5,4},{6,7},{7,6},{8,9},{9,8},{10,11... | collective-permute-start | bytes 442376 | tf_op jit(solution)/shard_map/ppermute | solution.py:259
  1.8 0.6 %copy-done.3 = s32[1,1,16]{2,1,0:T(1,128)S(1)} copy-done((s32[1,1,16]{2,1,0:T(1,128)S(1)}, s32[1,1,16]{2,1,0:T(1,128)}, u32[]{:S(2)}) %copy-start.3) | copy-done | bytes 88
  2.5 0.9 %copy-done = bf16[12,48,64]{2,1,0:T(8,128)(2,1)S(1)} copy-done((bf16[12,48,64]{2,1,0:T(8,128)(2,1)S(1)}, bf16[12,48,64]{2,1,0:T(8,128)(2,1)}, u32[]{:S(2)}) %copy-start) | copy-done | bytes 73752
  3.4 0.9 %copy-done.1 = bf16[3,3,64,128]{3,2,1,0:T(8,128)(2,1)S(1)} copy-done((bf16[3,3,64,128]{3,2,1,0:T(8,128)(2,1)S(1)}, bf16[3,3,64,128]{3,2,1,0:T(8,128)(2,1)}, u32[]{:S(2)}) %copy-start.1) | copy-done | bytes 147480
  4.3 1.1 %shard_map.94 = (bf16[12,48,128]{2,1,0:T(8,128)(2,1)S(1)}, bf16[384,256]{1,0:T(8,128)(2,1)S(1)}) custom-call(s32[1,1]{1,0:T(1,128)S(6)} %copy.29.count, s32[1,1,16]{2,1,0:T(1,128)S(1)} %copy-done.3, s32[1]{0:T(128)} %bitcast.2.chan, bf16[12,48,64]{2,1,0:T(8,128)(2,1)S(1)} %copy-done, bf16[3,3,64,128]{3,2,1,0:T(8,128)(2,1)S(1)} %copy-done.1), custom_call_target="tpu_custom_call" | custom-call | tf_op jit(solution)/shard_map/pallas_call | solution.py:240
  5.4 0.1 collective-permute-start
  5.6 1.2 %collective-permute-done = bf16[12,48,128]{2,1,0:T(8,128)(2,1)S(1)} collective-permute-done((bf16[12,48,128]{2,1,0:T(8,128)(2,1)S(1)}, bf16[12,48,128]{2,1,0:T(8,128)(2,1)S(1)}, u32[]{:S(2)}, u32[]{:S(2)}) %collective-permute-start) | collective-permute-done | bytes 147488 | tf_op jit(solution)/shard_map/ppermute | solution.py:257
  6.9 2.7 %collective-permute-start.1 = (bf16[5,48,128]{2,1,0:T(8,128)(2,1)S(1)}, bf16[5,48,128]{2,1,0:T(8,128)(2,1)S(1)}, u32[]{:S(2)}, u32[]{:S(2)}) collective-permute-start(bf16[5,48,128]{2,1,0:T(8,128)(2,1)S(1)} %maximum_select_fusion), channel_id=1, source_target_pairs={{0,2},{2,0},{1,3},{3,1},{4,6},{6,4},{5,7},{7,5},{8,10},{10,8},{9,1... | collective-permute-start | bytes 184328 | tf_op jit(solution)/shard_map/ppermute | solution.py:31
  9.7 2.4 %collective-permute-done.1 = bf16[5,48,128]{2,1,0:T(8,128)(2,1)S(1)} collective-permute-done((bf16[5,48,128]{2,1,0:T(8,128)(2,1)S(1)}, bf16[5,48,128]{2,1,0:T(8,128)(2,1)S(1)}, u32[]{:S(2)}, u32[]{:S(2)}) %collective-permute-start.1) | collective-permute-done | bytes 61472 | tf_op jit(solution)/shard_map/ppermute | solution.py:31
  12.3 0.2 pad_maximum_fusion.1
  12.6 1.9 %collective-permute-start.2 = (bf16[100,128]{1,0:T(8,128)(2,1)S(1)}, bf16[100,128]{1,0:T(8,128)(2,1)S(1)}, u32[]{:S(2)}, u32[]{:S(2)}) collective-permute-start(bf16[100,128]{1,0:T(8,128)(2,1)S(1)} %get-tuple-element.27), channel_id=1, source_target_pairs={{0,4},{4,0},{8,12},{12,8},{1,5},{5,1},{9,13},{13,9},{2,6},{6,2},{1... | collective-permute-start | bytes 76808 | tf_op jit(solution)/shard_map/ppermute | solution.py:31
  14.4 0.7 %collective-permute-start.3 = (bf16[100,128]{1,0:T(8,128)(2,1)S(1)}, bf16[100,128]{1,0:T(8,128)(2,1)S(1)}, u32[]{:S(2)}, u32[]{:S(2)}) collective-permute-start(bf16[100,128]{1,0:T(8,128)(2,1)S(1)} %get-tuple-element.28), channel_id=1, source_target_pairs={{4,8},{8,4},{5,9},{9,5},{6,10},{10,6},{7,11},{11,7},{20,24},{24,20... | collective-permute-start | bytes 76808 | tf_op jit(solution)/shard_map/ppermute | solution.py:35
  15.1 0.1 pad_add_fusion.flags
  15.2 0.1 pad.8.clone
  15.3 0.1 pad.4.clone
  15.3 0.1 copy.17
  15.5 1.0 %collective-permute-done.2 = bf16[100,128]{1,0:T(8,128)(2,1)S(1)} collective-permute-done((bf16[100,128]{1,0:T(8,128)(2,1)S(1)}, bf16[100,128]{1,0:T(8,128)(2,1)S(1)}, u32[]{:S(2)}, u32[]{:S(2)}) %collective-permute-start.2) | collective-permute-done | bytes 25632 | tf_op jit(solution)/shard_map/ppermute | solution.py:31
  16.6 0.2 pad_maximum_fusion.a_ref
  16.8 0.1 pad_maximum_fusion.2.u_ref
  17.0 0.7 %copy-done.2 = bf16[3,3,128,64]{2,3,1,0:T(8,128)(2,1)S(1)} copy-done((bf16[3,3,128,64]{2,3,1,0:T(8,128)(2,1)S(1)}, bf16[3,3,128,64]{2,3,1,0:T(8,128)(2,1)}, u32[]{:S(2)}) %copy-start.2) | copy-done | bytes 147480
  17.7 2.2 %shard_map.95 = (bf16[12,2,48,128]{3,2,1,0:T(8,128)(2,1)S(1)}, bf16[2,448,128]{2,1,0:T(8,128)(2,1)S(1)}) custom-call(s32[3]{0:T(128)S(1)} %pad_add_fusion.flags, bf16[14,2,64,128]{3,2,1,0:T(8,128)(2,1)S(1)} %pad_maximum_fusion.a_ref, bf16[18,64,128]{2,1,0:T(8,128)(2,1)S(1)} %pad_maximum_fusion.2.u_ref, bf16[384,256]{1,0:T(8,128)(2,1)S(1)} %get-tuple-element.10.wa_ref, ...), custom_call_target="tpu_custom_call" | custom-call | tf_op jit(solution)/shard_map/pallas_call | solution.py:292
  19.9 1.8 %collective-permute-start.5 = (bf16[448,128]{1,0:T(8,128)(2,1)S(1)}, bf16[448,128]{1,0:T(8,128)(2,1)S(1)}, u32[]{:S(2)}, u32[]{:S(2)}) collective-permute-start(bf16[448,128]{1,0:T(8,128)(2,1)S(1)} %select_bitcast_fusion), channel_id=1, source_target_pairs={{0,2},{2,0},{1,3},{3,1},{4,6},{6,4},{5,7},{7,5},{8,10},{10,8},{9,1... | collective-permute-start | bytes 344072 | tf_op jit(solution)/shard_map/ppermute | solution.py:316
  21.7 3.1 %collective-permute-done.5 = bf16[448,128]{1,0:T(8,128)(2,1)S(1)} collective-permute-done((bf16[448,128]{1,0:T(8,128)(2,1)S(1)}, bf16[448,128]{1,0:T(8,128)(2,1)S(1)}, u32[]{:S(2)}, u32[]{:S(2)}) %collective-permute-start.5) | collective-permute-done | bytes 114720 | tf_op jit(solution)/shard_map/ppermute | solution.py:316
  24.8 3.9 %collective-permute-start.8 = (bf16[448,128]{1,0:T(8,128)(2,1)S(1)}, bf16[448,128]{1,0:T(8,128)(2,1)S(1)}, u32[]{:S(2)}, u32[]{:S(2)}) collective-permute-start(bf16[448,128]{1,0:T(8,128)(2,1)S(1)} %fusion), channel_id=1, source_target_pairs={{0,12},{4,8},{8,4},{12,0},{1,13},{5,9},{9,5},{13,1},{2,14},{6,10},... | collective-permute-start | bytes 344072 | tf_op jit(solution)/shard_map/ppermute | solution.py:323
  28.7 2.5 %collective-permute-start.7 = (bf16[448,128]{1,0:T(8,128)(2,1)S(1)}, bf16[448,128]{1,0:T(8,128)(2,1)S(1)}, u32[]{:S(2)}, u32[]{:S(2)}) collective-permute-start(bf16[448,128]{1,0:T(8,128)(2,1)S(1)} %fusion), channel_id=1, source_target_pairs={{0,8},{4,12},{8,0},{12,4},{1,9},{5,13},{9,1},{13,5},{2,10},{6,14},... | collective-permute-start | bytes 344072 | tf_op jit(solution)/shard_map/ppermute | solution.py:323
  31.2 0.5 %collective-permute-start.6 = (bf16[448,128]{1,0:T(8,128)(2,1)S(1)}, bf16[448,128]{1,0:T(8,128)(2,1)S(1)}, u32[]{:S(2)}, u32[]{:S(2)}) collective-permute-start(bf16[448,128]{1,0:T(8,128)(2,1)S(1)} %fusion), channel_id=1, source_target_pairs={{0,4},{4,0},{8,12},{12,8},{1,5},{5,1},{9,13},{13,9},{2,6},{6,2},{1... | collective-permute-start | bytes 344072 | tf_op jit(solution)/shard_map/ppermute | solution.py:323
  31.7 0.3 collective-permute-done.8
  32.0 5.5 %collective-permute-done.7 = bf16[448,128]{1,0:T(8,128)(2,1)S(1)} collective-permute-done((bf16[448,128]{1,0:T(8,128)(2,1)S(1)}, bf16[448,128]{1,0:T(8,128)(2,1)S(1)}, u32[]{:S(2)}, u32[]{:S(2)}) %collective-permute-start.7) | collective-permute-done | bytes 114720 | tf_op jit(solution)/shard_map/ppermute | solution.py:323
  37.7 1.6 %collective-permute-start.9 = (bf16[448,128]{1,0:T(8,128)(2,1)S(1)}, bf16[448,128]{1,0:T(8,128)(2,1)S(1)}, u32[]{:S(2)}, u32[]{:S(2)}) collective-permute-start(bf16[448,128]{1,0:T(8,128)(2,1)S(1)} %add_convert_fusion.own_ref), channel_id=1, source_target_pairs={{0,2},{2,0},{1,3},{3,1},{4,6},{6,4},{5,7},{7,5},{8,10},{10,8},{9,1... | collective-permute-start | bytes 344072 | tf_op jit(solution)/shard_map/ppermute | solution.py:332
  39.2 0.8 %copy.28 = bf16[3,8,48,128]{3,1,2,0:T(8,128)(2,1)} copy(bf16[3,8,48,128]{3,2,1,0:T(8,128)(2,1)S(1)} %bitcast.42) | data formatting | bytes 589824
  40.0 2.5 %collective-permute-done.9.other_ref = bf16[448,128]{1,0:T(8,128)(2,1)S(1)} collective-permute-done((bf16[448,128]{1,0:T(8,128)(2,1)S(1)}, bf16[448,128]{1,0:T(8,128)(2,1)S(1)}, u32[]{:S(2)}, u32[]{:S(2)}) %collective-permute-start.9) | collective-permute-done | bytes 114720 | tf_op jit(solution)/shard_map/ppermute | solution.py:332
  42.5 0.9 %shard_map.96 = (f32[9,64,64]{2,1,0:T(8,128)}, f32[9,64,128]{2,1,0:T(8,128)}) custom-call(s32[1]{0:T(128)S(6)} %select_n.82.flags, bf16[448,128]{1,0:T(8,128)(2,1)S(1)} %add_convert_fusion.own_ref, bf16[448,128]{1,0:T(8,128)(2,1)S(1)} %collective-permute-done.9.other_ref), custom_call_target="tpu_custom_call" | custom-call | tf_op jit(solution)/shard_map/pallas_call | solution.py:336
  (39 shorter events, 0.5 us)
Async XLA Ops:
  0.6 16.3 %collective-permute-start.4 = (bf16[3,3,64,128]{3,2,1,0:T(8,128)(2,1)}, bf16[3,3,64,128]{3,2,1,0:T(8,128)(2,1)S(1)}, u32[]{:S(2)}, u32[]{:S(2)}) collective-permute-start(bf16[3,3,64,128]{3,2,1,0:T(8,128)(2,1)} %bitcast.43), channel_id=1, source_target_pairs={{0,1},{1,0},{2,3},{3,2},{4,5},{5,4},{6,7},{7,6},{8,9},{9,8},{10,11... | collective-permute-start | bytes 442376 | tf_op jit(solution)/shard_map/ppermute | solution.py:259
  1.8 0.7 %copy-start.3 = (s32[1,1,16]{2,1,0:T(1,128)S(1)}, s32[1,1,16]{2,1,0:T(1,128)}, u32[]{:S(2)}) copy-start(s32[1,1,16]{2,1,0:T(1,128)} %order.1) | copy-start | bytes 196
  2.5 0.9 %copy-start = (bf16[12,48,64]{2,1,0:T(8,128)(2,1)S(1)}, bf16[12,48,64]{2,1,0:T(8,128)(2,1)}, u32[]{:S(2)}) copy-start(bf16[12,48,64]{2,1,0:T(8,128)(2,1)} %cot_hbm.1) | copy-start | bytes 221188
  3.4 0.9 %copy-start.1 = (bf16[3,3,64,128]{3,2,1,0:T(8,128)(2,1)S(1)}, bf16[3,3,64,128]{3,2,1,0:T(8,128)(2,1)}, u32[]{:S(2)}) copy-start(bf16[3,3,64,128]{3,2,1,0:T(8,128)(2,1)} %w1_hbm.1) | copy-start | bytes 442372
  4.3 1.3 %copy-start.5 = (bf16[24,6144]{1,0:T(8,128)(2,1)S(1)}, bf16[24,6144]{1,0:T(8,128)(2,1)}, u32[]{:S(2)}) copy-start(bf16[24,6144]{1,0:T(8,128)(2,1)} %param.7) | copy-start | bytes 884740
  5.4 1.4 %collective-permute-start = (bf16[12,48,128]{2,1,0:T(8,128)(2,1)S(1)}, bf16[12,48,128]{2,1,0:T(8,128)(2,1)S(1)}, u32[]{:S(2)}, u32[]{:S(2)}) collective-permute-start(bf16[12,48,128]{2,1,0:T(8,128)(2,1)S(1)} %get-tuple-element.9), channel_id=1, source_target_pairs={{0,1},{1,0},{2,3},{3,2},{4,5},{5,4},{6,7},{7,6},{8,9},{9,8},{10,11... | collective-permute-start | bytes 442376 | tf_op jit(solution)/shard_map/ppermute | solution.py:257
  6.9 5.2 %collective-permute-start.1 = (bf16[5,48,128]{2,1,0:T(8,128)(2,1)S(1)}, bf16[5,48,128]{2,1,0:T(8,128)(2,1)S(1)}, u32[]{:S(2)}, u32[]{:S(2)}) collective-permute-start(bf16[5,48,128]{2,1,0:T(8,128)(2,1)S(1)} %maximum_select_fusion), channel_id=1, source_target_pairs={{0,2},{2,0},{1,3},{3,1},{4,6},{6,4},{5,7},{7,5},{8,10},{10,8},{9,1... | collective-permute-start | bytes 184328 | tf_op jit(solution)/shard_map/ppermute | solution.py:31
  12.6 3.9 %collective-permute-start.2 = (bf16[100,128]{1,0:T(8,128)(2,1)S(1)}, bf16[100,128]{1,0:T(8,128)(2,1)S(1)}, u32[]{:S(2)}, u32[]{:S(2)}) collective-permute-start(bf16[100,128]{1,0:T(8,128)(2,1)S(1)} %get-tuple-element.27), channel_id=1, source_target_pairs={{0,4},{4,0},{8,12},{12,8},{1,5},{5,1},{9,13},{13,9},{2,6},{6,2},{1... | collective-permute-start | bytes 76808 | tf_op jit(solution)/shard_map/ppermute | solution.py:31
  14.4 2.0 %collective-permute-start.3 = (bf16[100,128]{1,0:T(8,128)(2,1)S(1)}, bf16[100,128]{1,0:T(8,128)(2,1)S(1)}, u32[]{:S(2)}, u32[]{:S(2)}) collective-permute-start(bf16[100,128]{1,0:T(8,128)(2,1)S(1)} %get-tuple-element.28), channel_id=1, source_target_pairs={{4,8},{8,4},{5,9},{9,5},{6,10},{10,6},{7,11},{11,7},{20,24},{24,20... | collective-permute-start | bytes 76808 | tf_op jit(solution)/shard_map/ppermute | solution.py:35
  16.8 0.9 %copy-start.2 = (bf16[3,3,128,64]{2,3,1,0:T(8,128)(2,1)S(1)}, bf16[3,3,128,64]{2,3,1,0:T(8,128)(2,1)}, u32[]{:S(2)}) copy-start(bf16[3,3,128,64]{2,3,1,0:T(8,128)(2,1)} %param.10) | copy-start | bytes 442372
  16.9 0.7 %copy-start.4 = (f32[128]{0:T(128)S(1)}, f32[128]{0:T(128)}, u32[]{:S(2)}) copy-start(f32[128]{0:T(128)} %param.8) | copy-start | bytes 1540
  19.9 4.9 %collective-permute-start.5 = (bf16[448,128]{1,0:T(8,128)(2,1)S(1)}, bf16[448,128]{1,0:T(8,128)(2,1)S(1)}, u32[]{:S(2)}, u32[]{:S(2)}) collective-permute-start(bf16[448,128]{1,0:T(8,128)(2,1)S(1)} %select_bitcast_fusion), channel_id=1, source_target_pairs={{0,2},{2,0},{1,3},{3,1},{4,6},{6,4},{5,7},{7,5},{8,10},{10,8},{9,1... | collective-permute-start | bytes 344072 | tf_op jit(solution)/shard_map/ppermute | solution.py:316
  24.8 7.2 %collective-permute-start.8 = (bf16[448,128]{1,0:T(8,128)(2,1)S(1)}, bf16[448,128]{1,0:T(8,128)(2,1)S(1)}, u32[]{:S(2)}, u32[]{:S(2)}) collective-permute-start(bf16[448,128]{1,0:T(8,128)(2,1)S(1)} %fusion), channel_id=1, source_target_pairs={{0,12},{4,8},{8,4},{12,0},{1,13},{5,9},{9,5},{13,1},{2,14},{6,10},... | collective-permute-start | bytes 344072 | tf_op jit(solution)/shard_map/ppermute | solution.py:323
  28.7 8.9 %collective-permute-start.7 = (bf16[448,128]{1,0:T(8,128)(2,1)S(1)}, bf16[448,128]{1,0:T(8,128)(2,1)S(1)}, u32[]{:S(2)}, u32[]{:S(2)}) collective-permute-start(bf16[448,128]{1,0:T(8,128)(2,1)S(1)} %fusion), channel_id=1, source_target_pairs={{0,8},{4,12},{8,0},{12,4},{1,9},{5,13},{9,1},{13,5},{2,10},{6,14},... | collective-permute-start | bytes 344072 | tf_op jit(solution)/shard_map/ppermute | solution.py:323
  31.2 6.4 %collective-permute-start.6 = (bf16[448,128]{1,0:T(8,128)(2,1)S(1)}, bf16[448,128]{1,0:T(8,128)(2,1)S(1)}, u32[]{:S(2)}, u32[]{:S(2)}) collective-permute-start(bf16[448,128]{1,0:T(8,128)(2,1)S(1)} %fusion), channel_id=1, source_target_pairs={{0,4},{4,0},{8,12},{12,8},{1,5},{5,1},{9,13},{13,9},{2,6},{6,2},{1... | collective-permute-start | bytes 344072 | tf_op jit(solution)/shard_map/ppermute | solution.py:323
  37.7 4.9 %collective-permute-start.9 = (bf16[448,128]{1,0:T(8,128)(2,1)S(1)}, bf16[448,128]{1,0:T(8,128)(2,1)S(1)}, u32[]{:S(2)}, u32[]{:S(2)}) collective-permute-start(bf16[448,128]{1,0:T(8,128)(2,1)S(1)} %add_convert_fusion.own_ref), channel_id=1, source_target_pairs={{0,2},{2,0},{1,3},{3,1},{4,6},{6,4},{5,7},{7,5},{8,10},{10,8},{9,1... | collective-permute-start | bytes 344072 | tf_op jit(solution)/shard_map/ppermute | solution.py:332

commit v2 on v1

--- a/solution.py
+++ b/solution.py
@@ -23,16 +23,23 @@
     return [p for i in range(1, size - 1, 2) for p in ((i, i + 1), (i + 1, i))]
 
 
-def neighbour_strips(first, last, axis):
+def permuted(value, axis, pairs, crossing):
+    if not crossing:
+        return lax.ppermute(value, axis, pairs)
+    both = [(2 * i + c, 2 * j + 1 - c) for i, j in pairs for c in range(2)]
+    return lax.ppermute(value, (axis, "chan"), both)
+
+
+def neighbour_strips(first, last, axis, crossing=False):
     size = lax.axis_size(axis)
     even = lax.axis_index(axis) % 2 == 0
     if size == 1:
         return jnp.zeros_like(first), jnp.zeros_like(first)
-    got_even = lax.ppermute(jnp.where(even, last, first), axis, swaps(size, 1))
+    got_even = permuted(jnp.where(even, last, first), axis, swaps(size, 1), crossing)
     if size == 2:
         got_odd = jnp.zeros_like(first)
     else:
-        got_odd = lax.ppermute(jnp.where(even, first, last), axis, odd_swaps(size))
+        got_odd = permuted(jnp.where(even, first, last), axis, odd_swaps(size), crossing)
     return jnp.where(even, got_odd, got_even), jnp.where(even, got_even, got_odd)
 
 
@@ -40,13 +47,35 @@
     return pltpu.roll(value, amount % SLOTS, axis=1)
 
 
-def prepare_kernel(count, order, chan, cot_hbm, w1_hbm, z_ref, wa_ref, cot, w1, tissue, sems):
-    copies = [
-        pltpu.make_async_copy(cot_hbm, cot, sems.at[0]),
-        pltpu.make_async_copy(w1_hbm, w1, sems.at[1]),
+def prepare_kernel(
+    chan,
+    count,
+    order_hbm,
+    cot_hbm,
+    w1_hbm,
+    w2_hbm,
+    shift_hbm,
+    z_ref,
+    wa_ref,
+    w2_ref,
+    shift_ref,
+    cot,
+    w1,
+    order,
+    tissue,
+    sems,
+):
+    pairs = [
+        (order_hbm, order),
+        (cot_hbm, cot),
+        (w1_hbm, w1),
+        (w2_hbm, w2_ref),
+        (shift_hbm, shift_ref),
     ]
+    copies = [pltpu.make_async_copy(a, b, sems.at[i]) for i, (a, b) in enumerate(pairs)]
     for copy in copies:
         copy.start()
+    copies[0].wait()
     tiles = order.shape[2]
     for k in range(tiles):
         tissue[order[0, 0, k]] = jnp.where(k < count[0, 0], 1, 0)
@@ -63,12 +92,12 @@
             inside = (col_id >= b * side) & (col_id < (b + 1) * side)
             live = jnp.where(inside, tissue[a * across + b], live)
         masks.append((live > 0) & mine)
-    copies[0].wait()
+    copies[1].wait()
     for i in range(rows):
         value = cot[i].astype(F32)
         twice = jnp.concatenate([value, value], axis=1)
         z_ref[i] = jnp.where(masks[i // side], twice, 0.0).astype(BF)
-    copies[1].wait()
+    copies[2].wait()
     lanes = 2 * half
     for u in range(3):
         low = slice(u * lanes, u * lanes + half)
@@ -77,6 +106,8 @@
         wa_ref[high, :lanes] = w1[u, 0]
         wa_ref[low, lanes:] = w1[u, 1]
         wa_ref[high, lanes:] = w1[u, 2]
+    copies[3].wait()
+    copies[4].wait()
 
 
 def main_kernel(
@@ -234,37 +265,53 @@
 
     whole = pl.BlockSpec(memory_space=pltpu.VMEM)
     scalars = pl.BlockSpec(memory_space=pltpu.SMEM)
-    in_place = pl.BlockSpec(memory_space=pl.ANY)
+    in_hbm = pl.BlockSpec(memory_space=pltpu.HBM)
     limit = pltpu.CompilerParams(vmem_limit_bytes=48 << 20)
     half = channels
-    placed, wa = pl.pallas_call(
+    placed, wa, own_w2, shift_row = pl.pallas_call(
         prepare_kernel,
         out_shape=(
             jax.ShapeDtypeStruct((rows, cols, lanes), BF),
             jax.ShapeDtypeStruct((3 * lanes, 2 * mids), BF),
-        ),
-        in_specs=[scalars, scalars, scalars, in_place, in_place],
-        out_specs=(whole, whole),
+            jax.ShapeDtypeStruct((3, 3, half, mids), BF),
+            jax.ShapeDtypeStruct((1, mids), F32),
+        ),
+        in_specs=[scalars] * 2 + [in_hbm] * 5,
+        out_specs=(whole,) * 4,
         scratch_shapes=[
             pltpu.VMEM((rows, cols, half), BF),
             pltpu.VMEM((3, 3, channels, mids), BF),
+            pltpu.SMEM((1, 1, tile_rows * tile_cols), jnp.int32),
             pltpu.SMEM((tile_rows * tile_cols,), jnp.int32),
-            pltpu.SemaphoreType.DMA((2,)),
+            pltpu.SemaphoreType.DMA((5,)),
         ],
         compiler_params=limit,
-    )(tissue_count, tile_order, chan_index.reshape(1), cotangent, weight_one)
-    core_swap = [(0, 1), (1, 0)]
-    upstream = placed + lax.ppermute(placed, "chan", core_swap)
-    own_w2 = weight_two.swapaxes(2, 3)
-    other_w2 = lax.ppermute(own_w2, "chan", core_swap)
+    )(
+        chan_index.reshape(1),
+        tissue_count,
+        *(
+            pltpu.with_memory_space_constraint(value, pltpu.HBM)
+            for value in (
+                tile_order,
+                cotangent,
+                weight_one,
+                weight_two.swapaxes(2, 3),
+                shift.reshape(1, mids),
+            )
+        ),
+    )
 
     picture = acts.reshape(height, pairs, lanes)
     strip = lambda a, u: jnp.concatenate([a, u], axis=0)
     before, after = neighbour_strips(
-        strip(picture[:2], upstream[:3]), strip(picture[height - 2 :], upstream[rows - 3 :]), "rows"
-    )
+        strip(picture[:2], placed[:3]), strip(picture[height - 2 :], placed[rows - 3 :]), "rows"
+    )
+    before_x, after_x = neighbour_strips(placed[:3], placed[rows - 3 :], "rows", crossing=True)
+    core_swap = [(0, 1), (1, 0)]
+    upstream = placed + lax.ppermute(placed, "chan", core_swap)
+    other_w2 = lax.ppermute(own_w2, "chan", core_swap)
     tall_a = jnp.concatenate([before[:2], picture, after[:2]], axis=0)
-    tall_u = jnp.concatenate([before[2:], upstream, after[2:]], axis=0)
+    tall_u = jnp.concatenate([before[2:] + before_x, upstream, after[2:] + after_x], axis=0)
 
     n_a, n_u = tall_a.shape[0], tall_u.shape[0]
     side = lambda a, u: jnp.concatenate([a.reshape(n_a, lanes), u.reshape(4 * n_u, lanes)], axis=0)
@@ -306,7 +353,7 @@
         wa,
         own_w2,
         other_w2,
-        shift.reshape(1, mids),
+        shift_row,
     )
 
     even = row_index % 2 == 0

time: 43.6 us -> 39.8 us (0.913)
  local copies, waits for them, and re-layouts: 4.53 us -> 1.31 us
  starting transfers between devices: 16.2 us -> 14.4 us
  waiting for transfers between devices: 16.1 us -> 17.4 us
    unnamed x14 -> x4, local copies, waits for them, and re-layouts: 4.05 us -> 0.84 us
    ppermute x3 -> x4, waiting for transfers between devices: 3.43 us -> 5.24 us  [the longest x3 5.24 us: permuted(): return lax.ppermute(value, axis, pairs)]
    ppermute x1, waiting for transfers between devices: 1.25 us -> 0.01 us  [shards(): upstream = placed + lax.ppermute(placed, 'chan', core_swap)]
    ppermute x1, waiting for transfers between devices: 3.05 us -> 4.15 us  [shards(): got = lax.ppermute(sent, 'rows', swaps(n_rows, 1))]
    ppermute x1, starting transfers between devices: 1.81 us -> 0.7 us  [shards(): got = lax.ppermute(sent, 'rows', swaps(n_rows, 1))]
    ppermute x3, waiting for transfers between devices: 5.86 us -> 5.2 us  [shards(): lax.ppermute(total, 'tiles', swaps(4, d))]
    ppermute x3 -> x4, starting transfers between devices: 5.25 us -> 5.03 us  [the longest x1 2.67 us: permuted(): return lax.ppermute(value, (axis, 'chan'), both)]
  transfers between devices with their start and end apart: 10 -> 11, of which waited for: 7 -> 7; matrix products, arithmetic and copies ran while one was open for 5% -> 5% of each run, Pallas kernels for 3% -> 0%
where the time goes in v2:
time: 39.8 us; the launch traced here: 39.7 us
  waiting for transfers between devices  17.4 us (44%)
  starting transfers between devices  14.4 us (36%)
  Pallas kernels  4.21 us (11%)
  between operations  1.54 us (4%)
  local copies, waits for them, and re-layouts  1.31 us (3%)
  other arithmetic  0.88 us (2%)
    ppermute x3, starting transfers between devices, shards(): lax.ppermute(total, 'tiles', swaps(4, d))  6.67 us
    ppermute x3, waiting for transfers between devices, permuted(): return lax.ppermute(value, axis, pairs)  5.24 us
    ppermute x3, waiting for transfers between devices, shards(): lax.ppermute(total, 'tiles', swaps(4, d))  5.2 us
    ppermute x1, waiting for transfers between devices, shards(): got = lax.ppermute(sent, 'rows', swaps(n_rows, 1))  4.15 us
    ppermute x1, waiting for transfers between devices, shards(): other = lax.ppermute(total, 'rows', swaps(n_rows, 1))  2.76 us
    ppermute x1, starting transfers between devices, permuted(): return lax.ppermute(value, (axis, 'chan'), both)  2.67 us
    ppermute x3, starting transfers between devices, permuted(): return lax.ppermute(value, axis, pairs)  2.36 us
    pallas_call x1, Pallas kernels, shards(): pl.pallas_call(main_kernel, out_shape=(jax.ShapeDtypeStruct((rows, 2, col...  2.18 us
  transfers between devices with their start and end apart: 11, of which 7 were waited for; matrix products, arithmetic and copies ran while one was open for 5% of the time, Pallas kernels for 0%

profile of v2, /device:TPU:0, one launch (start us, length us, event | category | flops | bytes accessed | tf_op | source)
XLA Modules:
  0.0 39.7 jit_solution(17185322942236663436)
XLA Ops:
  1.3 1.1 %shard_map.94 = (bf16[12,48,128]{2,1,0:T(8,128)(2,1)S(1)}, bf16[384,256]{1,0:T(8,128)(2,1)S(1)}, bf16[3,3,64,128]{3,2,1,0:T(8,128)(2,1)S(1)}, f32[1,128]{1,0:T(1,128)S(1)}) custom-call(s32[1]{0:T(128)} %bitcast.2.chan, s32[1,1]{1,0:T(1,128)S(6)} %copy.29.count, s32[1,1,16]{2,1,0:T(1,128)} %order_hbm.1, bf16[12,48,64]{2,1,0:T(8,128)(2,1)} %cot_hbm.1, ...), custom_call_target="tpu_custom_call" | custom-call | tf_op jit(solution)/shard_map/pallas_call | solution.py:271
  2.4 0.5 %collective-permute-start.2 = (bf16[12,48,128]{2,1,0:T(8,128)(2,1)S(1)}, bf16[12,48,128]{2,1,0:T(8,128)(2,1)S(1)}, u32[]{:S(2)}, u32[]{:S(2)}) collective-permute-start(bf16[12,48,128]{2,1,0:T(8,128)(2,1)S(1)} %get-tuple-element.11), channel_id=1, source_target_pairs={{0,1},{1,0},{2,3},{3,2},{4,5},{5,4},{6,7},{7,6},{8,9},{9,8},{10,11... | collective-permute-start | bytes 442376 | tf_op jit(solution)/shard_map/ppermute | solution.py:311
  3.0 2.7 %collective-permute-start.1 = (bf16[3,48,128]{2,1,0:T(8,128)(2,1)S(1)}, bf16[3,48,128]{2,1,0:T(8,128)(2,1)S(1)}, u32[]{:S(2)}, u32[]{:S(2)}) collective-permute-start(bf16[3,48,128]{2,1,0:T(8,128)(2,1)S(1)} %get-tuple-element.25), channel_id=1, source_target_pairs={{0,3},{1,2},{2,1},{3,0},{4,7},{5,6},{6,5},{7,4},{8,11},{9,10},{10,... | collective-permute-start | bytes 110600 | tf_op jit(solution)/shard_map/ppermute | solution.py:30
  5.7 0.1 collective-permute-start
  5.8 0.1 collective-permute-start.5
  5.9 0.1 copy_bitcast_fusion.1
  6.0 4.0 %collective-permute-done = bf16[5,48,128]{2,1,0:T(8,128)(2,1)S(1)} collective-permute-done((bf16[5,48,128]{2,1,0:T(8,128)(2,1)S(1)}, bf16[5,48,128]{2,1,0:T(8,128)(2,1)S(1)}, u32[]{:S(2)}, u32[]{:S(2)}) %collective-permute-start) | collective-permute-done | bytes 61472 | tf_op jit(solution)/shard_map/ppermute | solution.py:28
  10.1 0.2 pad_maximum_fusion.1
  10.3 0.0 collective-permute-done.1
  10.5 1.6 %collective-permute-start.3 = (bf16[100,128]{1,0:T(8,128)(2,1)S(1)}, bf16[100,128]{1,0:T(8,128)(2,1)S(1)}, u32[]{:S(2)}, u32[]{:S(2)}) collective-permute-start(bf16[100,128]{1,0:T(8,128)(2,1)S(1)} %get-tuple-element.32), channel_id=1, source_target_pairs={{0,4},{4,0},{8,12},{12,8},{1,5},{5,1},{9,13},{13,9},{2,6},{6,2},{1... | collective-permute-start | bytes 76808 | tf_op jit(solution)/shard_map/ppermute | solution.py:28
  12.1 0.7 %collective-permute-start.4 = (bf16[100,128]{1,0:T(8,128)(2,1)S(1)}, bf16[100,128]{1,0:T(8,128)(2,1)S(1)}, u32[]{:S(2)}, u32[]{:S(2)}) collective-permute-start(bf16[100,128]{1,0:T(8,128)(2,1)S(1)} %get-tuple-element.33), channel_id=1, source_target_pairs={{4,8},{8,4},{5,9},{9,5},{6,10},{10,6},{7,11},{11,7},{20,24},{24,20... | collective-permute-start | bytes 76808 | tf_op jit(solution)/shard_map/ppermute | solution.py:28
  12.8 0.1 pad_add_fusion.flags
  12.9 0.1 pad.4.clone
  12.9 0.1 pad.8.clone
  13.0 0.1 copy.17
  13.2 1.2 %collective-permute-done.3 = bf16[100,128]{1,0:T(8,128)(2,1)S(1)} collective-permute-done((bf16[100,128]{1,0:T(8,128)(2,1)S(1)}, bf16[100,128]{1,0:T(8,128)(2,1)S(1)}, u32[]{:S(2)}, u32[]{:S(2)}) %collective-permute-start.3) | collective-permute-done | bytes 25632 | tf_op jit(solution)/shard_map/ppermute | solution.py:28
  14.5 0.2 pad_maximum_fusion.a_ref
  14.7 0.1 pad_maximum_fusion.2.u_ref
  14.9 2.2 %shard_map.95 = (bf16[12,2,48,128]{3,2,1,0:T(8,128)(2,1)S(1)}, bf16[2,448,128]{2,1,0:T(8,128)(2,1)S(1)}) custom-call(s32[3]{0:T(128)S(1)} %pad_add_fusion.flags, bf16[14,2,64,128]{3,2,1,0:T(8,128)(2,1)S(1)} %pad_maximum_fusion.a_ref, bf16[18,64,128]{2,1,0:T(8,128)(2,1)S(1)} %pad_maximum_fusion.2.u_ref, bf16[384,256]{1,0:T(8,128)(2,1)S(1)} %get-tuple-element.12.wa_ref, ...), custom_call_target="tpu_custom_call" | custom-call | tf_op jit(solution)/shard_map/pallas_call | solution.py:339
  17.1 0.7 %collective-permute-start.6 = (bf16[448,128]{1,0:T(8,128)(2,1)S(1)}, bf16[448,128]{1,0:T(8,128)(2,1)S(1)}, u32[]{:S(2)}, u32[]{:S(2)}) collective-permute-start(bf16[448,128]{1,0:T(8,128)(2,1)S(1)} %select_bitcast_fusion), channel_id=1, source_target_pairs={{0,2},{2,0},{1,3},{3,1},{4,6},{6,4},{5,7},{7,5},{8,10},{10,8},{9,1... | collective-permute-start | bytes 344072 | tf_op jit(solution)/shard_map/ppermute | solution.py:363
  17.8 4.2 %collective-permute-done.6 = bf16[448,128]{1,0:T(8,128)(2,1)S(1)} collective-permute-done((bf16[448,128]{1,0:T(8,128)(2,1)S(1)}, bf16[448,128]{1,0:T(8,128)(2,1)S(1)}, u32[]{:S(2)}, u32[]{:S(2)}) %collective-permute-start.6) | collective-permute-done | bytes 114720 | tf_op jit(solution)/shard_map/ppermute | solution.py:363
  22.0 3.7 %collective-permute-start.9 = (bf16[448,128]{1,0:T(8,128)(2,1)S(1)}, bf16[448,128]{1,0:T(8,128)(2,1)S(1)}, u32[]{:S(2)}, u32[]{:S(2)}) collective-permute-start(bf16[448,128]{1,0:T(8,128)(2,1)S(1)} %fusion), channel_id=1, source_target_pairs={{0,12},{4,8},{8,4},{12,0},{1,13},{5,9},{9,5},{13,1},{2,14},{6,10},... | collective-permute-start | bytes 344072 | tf_op jit(solution)/shard_map/ppermute | solution.py:370
  25.6 2.5 %collective-permute-start.8 = (bf16[448,128]{1,0:T(8,128)(2,1)S(1)}, bf16[448,128]{1,0:T(8,128)(2,1)S(1)}, u32[]{:S(2)}, u32[]{:S(2)}) collective-permute-start(bf16[448,128]{1,0:T(8,128)(2,1)S(1)} %fusion), channel_id=1, source_target_pairs={{0,8},{4,12},{8,0},{12,4},{1,9},{5,13},{9,1},{13,5},{2,10},{6,14},... | collective-permute-start | bytes 344072 | tf_op jit(solution)/shard_map/ppermute | solution.py:370
  28.2 0.5 %collective-permute-start.7 = (bf16[448,128]{1,0:T(8,128)(2,1)S(1)}, bf16[448,128]{1,0:T(8,128)(2,1)S(1)}, u32[]{:S(2)}, u32[]{:S(2)}) collective-permute-start(bf16[448,128]{1,0:T(8,128)(2,1)S(1)} %fusion), channel_id=1, source_target_pairs={{0,4},{4,0},{8,12},{12,8},{1,5},{5,1},{9,13},{13,9},{2,6},{6,2},{1... | collective-permute-start | bytes 344072 | tf_op jit(solution)/shard_map/ppermute | solution.py:370
  28.6 1.1 %collective-permute-done.9 = bf16[448,128]{1,0:T(8,128)(2,1)S(1)} collective-permute-done((bf16[448,128]{1,0:T(8,128)(2,1)S(1)}, bf16[448,128]{1,0:T(8,128)(2,1)S(1)}, u32[]{:S(2)}, u32[]{:S(2)}) %collective-permute-start.9) | collective-permute-done | bytes 114720 | tf_op jit(solution)/shard_map/ppermute | solution.py:370
  29.8 3.0 %collective-permute-done.8 = bf16[448,128]{1,0:T(8,128)(2,1)S(1)} collective-permute-done((bf16[448,128]{1,0:T(8,128)(2,1)S(1)}, bf16[448,128]{1,0:T(8,128)(2,1)S(1)}, u32[]{:S(2)}, u32[]{:S(2)}) %collective-permute-start.8) | collective-permute-done | bytes 114720 | tf_op jit(solution)/shard_map/ppermute | solution.py:370
  32.7 1.1 %collective-permute-done.7 = bf16[448,128]{1,0:T(8,128)(2,1)S(1)} collective-permute-done((bf16[448,128]{1,0:T(8,128)(2,1)S(1)}, bf16[448,128]{1,0:T(8,128)(2,1)S(1)}, u32[]{:S(2)}, u32[]{:S(2)}) %collective-permute-start.7) | collective-permute-done | bytes 114720 | tf_op jit(solution)/shard_map/ppermute | solution.py:370
  33.8 0.1 add_convert_fusion.own_ref
  33.9 1.3 %collective-permute-start.10 = (bf16[448,128]{1,0:T(8,128)(2,1)S(1)}, bf16[448,128]{1,0:T(8,128)(2,1)S(1)}, u32[]{:S(2)}, u32[]{:S(2)}) collective-permute-start(bf16[448,128]{1,0:T(8,128)(2,1)S(1)} %add_convert_fusion.own_ref), channel_id=1, source_target_pairs={{0,2},{2,0},{1,3},{3,1},{4,6},{6,4},{5,7},{7,5},{8,10},{10,8},{9,1... | collective-permute-start | bytes 344072 | tf_op jit(solution)/shard_map/ppermute | solution.py:379
  35.2 0.8 %copy.28 = bf16[3,8,48,128]{3,1,2,0:T(8,128)(2,1)} copy(bf16[3,8,48,128]{3,2,1,0:T(8,128)(2,1)S(1)} %bitcast.42) | data formatting | bytes 589824
  36.0 2.8 %collective-permute-done.10.other_ref = bf16[448,128]{1,0:T(8,128)(2,1)S(1)} collective-permute-done((bf16[448,128]{1,0:T(8,128)(2,1)S(1)}, bf16[448,128]{1,0:T(8,128)(2,1)S(1)}, u32[]{:S(2)}, u32[]{:S(2)}) %collective-permute-start.10) | collective-permute-done | bytes 114720 | tf_op jit(solution)/shard_map/ppermute | solution.py:379
  38.8 0.9 %shard_map.96 = (f32[9,64,64]{2,1,0:T(8,128)}, f32[9,64,128]{2,1,0:T(8,128)}) custom-call(s32[1]{0:T(128)S(6)} %select_n.104.flags, bf16[448,128]{1,0:T(8,128)(2,1)S(1)} %add_convert_fusion.own_ref, bf16[448,128]{1,0:T(8,128)(2,1)S(1)} %collective-permute-done.10.other_ref), custom_call_target="tpu_custom_call" | custom-call | tf_op jit(solution)/shard_map/pallas_call | solution.py:383
  (30 shorter events, 0.4 us)
Async XLA Ops:
  1.3 4.4 %copy-start = (bf16[24,6144]{1,0:T(8,128)(2,1)S(1)}, bf16[24,6144]{1,0:T(8,128)(2,1)}, u32[]{:S(2)}) copy-start(bf16[24,6144]{1,0:T(8,128)(2,1)} %param.7) | copy-start | bytes 884740
  2.4 7.9 %collective-permute-start.2 = (bf16[12,48,128]{2,1,0:T(8,128)(2,1)S(1)}, bf16[12,48,128]{2,1,0:T(8,128)(2,1)S(1)}, u32[]{:S(2)}, u32[]{:S(2)}) collective-permute-start(bf16[12,48,128]{2,1,0:T(8,128)(2,1)S(1)} %get-tuple-element.11), channel_id=1, source_target_pairs={{0,1},{1,0},{2,3},{3,2},{4,5},{5,4},{6,7},{7,6},{8,9},{9,8},{10,11... | collective-permute-start | bytes 442376 | tf_op jit(solution)/shard_map/ppermute | solution.py:311
  3.0 7.3 %collective-permute-start.1 = (bf16[3,48,128]{2,1,0:T(8,128)(2,1)S(1)}, bf16[3,48,128]{2,1,0:T(8,128)(2,1)S(1)}, u32[]{:S(2)}, u32[]{:S(2)}) collective-permute-start(bf16[3,48,128]{2,1,0:T(8,128)(2,1)S(1)} %get-tuple-element.25), channel_id=1, source_target_pairs={{0,3},{1,2},{2,1},{3,0},{4,7},{5,6},{6,5},{7,4},{8,11},{9,10},{10,... | collective-permute-start | bytes 110600 | tf_op jit(solution)/shard_map/ppermute | solution.py:30
  5.7 4.3 %collective-permute-start = (bf16[5,48,128]{2,1,0:T(8,128)(2,1)S(1)}, bf16[5,48,128]{2,1,0:T(8,128)(2,1)S(1)}, u32[]{:S(2)}, u32[]{:S(2)}) collective-permute-start(bf16[5,48,128]{2,1,0:T(8,128)(2,1)S(1)} %maximum_select_fusion), channel_id=1, source_target_pairs={{0,2},{2,0},{1,3},{3,1},{4,6},{6,4},{5,7},{7,5},{8,10},{10,8},{9,1... | collective-permute-start | bytes 184328 | tf_op jit(solution)/shard_map/ppermute | solution.py:28
  5.8 9.0 %collective-permute-start.5 = (bf16[3,3,64,128]{3,2,1,0:T(8,128)(2,1)S(1)}, bf16[3,3,64,128]{3,2,1,0:T(8,128)(2,1)S(1)}, u32[]{:S(2)}, u32[]{:S(2)}) collective-permute-start(bf16[3,3,64,128]{3,2,1,0:T(8,128)(2,1)S(1)} %get-tuple-element.13.own_w2), channel_id=1, source_target_pairs={{0,1},{1,0},{2,3},{3,2},{4,5},{5,4},{6,7},{7,6},{8,9},{9,8},{10,11... | collective-permute-start | bytes 442376 | tf_op jit(solution)/shard_map/ppermute | solution.py:312
  10.5 3.9 %collective-permute-start.3 = (bf16[100,128]{1,0:T(8,128)(2,1)S(1)}, bf16[100,128]{1,0:T(8,128)(2,1)S(1)}, u32[]{:S(2)}, u32[]{:S(2)}) collective-permute-start(bf16[100,128]{1,0:T(8,128)(2,1)S(1)} %get-tuple-element.32), channel_id=1, source_target_pairs={{0,4},{4,0},{8,12},{12,8},{1,5},{5,1},{9,13},{13,9},{2,6},{6,2},{1... | collective-permute-start | bytes 76808 | tf_op jit(solution)/shard_map/ppermute | solution.py:28
  12.1 2.3 %collective-permute-start.4 = (bf16[100,128]{1,0:T(8,128)(2,1)S(1)}, bf16[100,128]{1,0:T(8,128)(2,1)S(1)}, u32[]{:S(2)}, u32[]{:S(2)}) collective-permute-start(bf16[100,128]{1,0:T(8,128)(2,1)S(1)} %get-tuple-element.33), channel_id=1, source_target_pairs={{4,8},{8,4},{5,9},{9,5},{6,10},{10,6},{7,11},{11,7},{20,24},{24,20... | collective-permute-start | bytes 76808 | tf_op jit(solution)/shard_map/ppermute | solution.py:28
  17.1 4.9 %collective-permute-start.6 = (bf16[448,128]{1,0:T(8,128)(2,1)S(1)}, bf16[448,128]{1,0:T(8,128)(2,1)S(1)}, u32[]{:S(2)}, u32[]{:S(2)}) collective-permute-start(bf16[448,128]{1,0:T(8,128)(2,1)S(1)} %select_bitcast_fusion), channel_id=1, source_target_pairs={{0,2},{2,0},{1,3},{3,1},{4,6},{6,4},{5,7},{7,5},{8,10},{10,8},{9,1... | collective-permute-start | bytes 344072 | tf_op jit(solution)/shard_map/ppermute | solution.py:363
  22.0 7.8 %collective-permute-start.9 = (bf16[448,128]{1,0:T(8,128)(2,1)S(1)}, bf16[448,128]{1,0:T(8,128)(2,1)S(1)}, u32[]{:S(2)}, u32[]{:S(2)}) collective-permute-start(bf16[448,128]{1,0:T(8,128)(2,1)S(1)} %fusion), channel_id=1, source_target_pairs={{0,12},{4,8},{8,4},{12,0},{1,13},{5,9},{9,5},{13,1},{2,14},{6,10},... | collective-permute-start | bytes 344072 | tf_op jit(solution)/shard_map/ppermute | solution.py:370
  25.6 7.1 %collective-permute-start.8 = (bf16[448,128]{1,0:T(8,128)(2,1)S(1)}, bf16[448,128]{1,0:T(8,128)(2,1)S(1)}, u32[]{:S(2)}, u32[]{:S(2)}) collective-permute-start(bf16[448,128]{1,0:T(8,128)(2,1)S(1)} %fusion), channel_id=1, source_target_pairs={{0,8},{4,12},{8,0},{12,4},{1,9},{5,13},{9,1},{13,5},{2,10},{6,14},... | collective-permute-start | bytes 344072 | tf_op jit(solution)/shard_map/ppermute | solution.py:370
  28.2 5.7 %collective-permute-start.7 = (bf16[448,128]{1,0:T(8,128)(2,1)S(1)}, bf16[448,128]{1,0:T(8,128)(2,1)S(1)}, u32[]{:S(2)}, u32[]{:S(2)}) collective-permute-start(bf16[448,128]{1,0:T(8,128)(2,1)S(1)} %fusion), channel_id=1, source_target_pairs={{0,4},{4,0},{8,12},{12,8},{1,5},{5,1},{9,13},{13,9},{2,6},{6,2},{1... | collective-permute-start | bytes 344072 | tf_op jit(solution)/shard_map/ppermute | solution.py:370
  33.9 4.9 %collective-permute-start.10 = (bf16[448,128]{1,0:T(8,128)(2,1)S(1)}, bf16[448,128]{1,0:T(8,128)(2,1)S(1)}, u32[]{:S(2)}, u32[]{:S(2)}) collective-permute-start(bf16[448,128]{1,0:T(8,128)(2,1)S(1)} %add_convert_fusion.own_ref), channel_id=1, source_target_pairs={{0,2},{2,0},{1,3},{3,1},{4,6},{6,4},{5,7},{7,5},{8,10},{10,8},{9,1... | collective-permute-start | bytes 344072 | tf_op jit(solution)/shard_map/ppermute | solution.py:379

commit v3 on v2

--- a/solution.py
+++ b/solution.py
@@ -19,28 +19,51 @@
     return [(i, i ^ distance) for i in range(size) if (i ^ distance) < size]
 
 
-def odd_swaps(size):
-    return [p for i in range(1, size - 1, 2) for p in ((i, i + 1), (i + 1, i))]
-
-
-def permuted(value, axis, pairs, crossing):
-    if not crossing:
-        return lax.ppermute(value, axis, pairs)
-    both = [(2 * i + c, 2 * j + 1 - c) for i, j in pairs for c in range(2)]
-    return lax.ppermute(value, (axis, "chan"), both)
-
-
-def neighbour_strips(first, last, axis, crossing=False):
-    size = lax.axis_size(axis)
-    even = lax.axis_index(axis) % 2 == 0
+def core_swapped(value):
+    return lax.ppermute(value, "chan", [(0, 1), (1, 0)])
+
+
+def shared_pairs(axis, n_tiles, n_rows):
+    sizes = (n_tiles, n_rows)
+    along = ("tiles", "rows").index(axis)
+    size = sizes[along]
+    pairs = []
+    for t in range(n_tiles):
+        for r in range(n_rows):
+            for core in range(2):
+                place, partner = [t, r], [t, r]
+                if core == 0:
+                    partner[along] = place[along] ^ 1
+                else:
+                    partner[along] = ((place[along] + 1) ^ 1) - 1
+                if not 0 <= partner[along] < size:
+                    partner[along] = place[along]
+                    partner[1 - along] = place[1 - along] ^ 1
+                    if partner[1 - along] >= sizes[1 - along]:
+                        continue
+                code = lambda p: (p[0] * n_rows + p[1]) * 2 + core
+                pairs.append((code(place), code(partner)))
+    return pairs
+
+
+def neighbour_strips(first, last, axis):
+    size, index = lax.axis_size(axis), lax.axis_index(axis)
+    even = index % 2 == 0
+    none = jnp.zeros_like(first)
     if size == 1:
-        return jnp.zeros_like(first), jnp.zeros_like(first)
-    got_even = permuted(jnp.where(even, last, first), axis, swaps(size, 1), crossing)
+        return none, none
+    to_even, to_odd = jnp.where(even, last, first), jnp.where(even, first, last)
     if size == 2:
-        got_odd = jnp.zeros_like(first)
-    else:
-        got_odd = permuted(jnp.where(even, first, last), axis, odd_swaps(size), crossing)
-    return jnp.where(even, got_odd, got_even), jnp.where(even, got_even, got_odd)
+        got = lax.ppermute(to_even, axis, swaps(size, 1))
+        return jnp.where(even, none, got), jnp.where(even, got, none)
+    low = lax.axis_index("chan") == 0
+    pairs = shared_pairs(axis, lax.axis_size("tiles"), lax.axis_size("rows"))
+    got = lax.ppermute(jnp.where(low, to_even, to_odd), ("tiles", "rows", "chan"), pairs)
+    other = core_swapped(got)
+    own_first = low == even
+    before = jnp.where(index == 0, none, jnp.where(own_first, other, got))
+    after = jnp.where(index == size - 1, none, jnp.where(own_first, got, other))
+    return before, after
 
 
 def roll_columns(value, amount):
@@ -110,21 +133,23 @@
     copies[4].wait()
 
 
+def flat(value):
+    return value.reshape(value.shape[0] * SLOTS, value.shape[2])
+
+
+def image(value):
+    return value.reshape(value.shape[0] // SLOTS, SLOTS, value.shape[1])
+
+
 def main_kernel(
-    flags, a_ref, u_ref, wa_ref, own_w2, other_w2, shift_ref, grad_ref, weight_ref, w2_ref
+    flags, a_ref, u_ref, wa_ref, own_w2, other_w2, shift_ref, mid_ref, weight_ref, w2_ref
 ):
     rows = a_ref.shape[0] - 2
     tall = rows + 1
-    own_cols = grad_ref.shape[2]
+    own_cols = flags[4]
     lanes = a_ref.shape[3]
     half = lanes // 2
     low = flags[2] == 0
-
-    def flat(value):
-        return value.reshape(value.shape[0] * SLOTS, value.shape[2])
-
-    def image(value):
-        return value.reshape(value.shape[0] // SLOTS, SLOTS, value.shape[1])
 
     def a_rows(count):
         return jnp.concatenate(
@@ -165,6 +190,7 @@
         + roll_columns(image(mid_part[:, 2 * lanes :]), 2)
     )
     mid_grad = jnp.where((middle > 0) & valid, mid_raw, 0.0)
+    mid_ref[...] = mid_grad.astype(BF)
 
     middle_own = jnp.where(own, middle, 0.0)[:rows]
     middle_taps = jnp.concatenate(
@@ -186,9 +212,16 @@
 
     left = lax.broadcasted_iota(jnp.int32, (half, lanes), 1) < half
 
+    part = weight_ref.shape[1]
+    me = flags[3]
+
     def keep(block, value):
-        at = block % 7 * half
-        weight_ref[block // 7, at : at + half, :] = value.astype(BF)
+        done = 0
+        while done < half:
+            number, at = divmod(block * half + done, part)
+            count = min(part - at, half - done)
+            weight_ref[number ^ me, at : at + count, :] = value[done : done + count].astype(BF)
+            done += count
 
     def at_left(value):
         return jnp.where(low, value, pltpu.roll(value, half, axis=1))
@@ -211,8 +244,13 @@
     keep(12, jnp.where(left, at_left(centre[0]), at_right(centre[1])))
     keep(13, at_left(centre[2]))
 
+
+def input_kernel(mid_ref, wa_ref, grad_ref):
+    rows, own_cols, lanes = grad_ref.shape[0], grad_ref.shape[2], grad_ref.shape[3]
+    tall = rows + 1
     by_lanes = (((1,), (1,)), ((), ()))
-    grads = flat(mid_grad).astype(BF)
+    grads = flat(mid_ref[...])
+    wa = wa_ref[...]
     straight = lax.dot_general(grads, wa[:, lanes:], by_lanes, preferred_element_type=F32)
     shifted = lax.dot_general(grads, wa[:, :lanes], by_lanes, preferred_element_type=F32)
 
@@ -225,14 +263,20 @@
     grad_ref[:, 1] = (below[:rows, :own_cols] + above[1:tall, :own_cols]).astype(BF)
 
 
-def unpack_kernel(scale, flags, own_ref, other_ref, first_ref, second_ref):
-    low = flags[0] == 0
+def unpack_kernel(scale, flags, piece_0, piece_1, piece_2, piece_3, first_ref, second_ref, all_ref):
     half = first_ref.shape[2]
+    part = piece_0.shape[0]
+    for distance, piece in enumerate((piece_0, piece_1, piece_2, piece_3)):
+        all_ref[flags[0] ^ distance] = piece[...]
 
     def block(number):
-        here = low if number < 7 else jnp.logical_not(low)
-        rows = slice(number % 7 * half, number % 7 * half + half)
-        return jnp.where(here, own_ref[rows, :].astype(F32), other_ref[rows, :].astype(F32)) * scale
+        done, values = 0, []
+        while done < half:
+            which, at = divmod(number * half + done, part)
+            count = min(part - at, half - done)
+            values.append(all_ref[which, at : at + count, :].astype(F32) * scale)
+            done += count
+        return values[0] if len(values) == 1 else jnp.concatenate(values, axis=0)
 
     for tap in range(9):
         second_ref[tap] = block(tap)
@@ -302,16 +346,22 @@
     )
 
     picture = acts.reshape(height, pairs, lanes)
+    edges = jnp.stack([placed[:3], placed[rows - 3 :]])
+    if n_rows == 2:
+        edge = jnp.where(row_index == 0, edges[1], edges[0])
+        edge = edge + core_swapped(edge)
+        first_u, last_u = edge, edge
+    else:
+        edges = edges + core_swapped(edges)
+        first_u, last_u = edges[0], edges[1]
     strip = lambda a, u: jnp.concatenate([a, u], axis=0)
     before, after = neighbour_strips(
-        strip(picture[:2], placed[:3]), strip(picture[height - 2 :], placed[rows - 3 :]), "rows"
-    )
-    before_x, after_x = neighbour_strips(placed[:3], placed[rows - 3 :], "rows", crossing=True)
-    core_swap = [(0, 1), (1, 0)]
-    upstream = placed + lax.ppermute(placed, "chan", core_swap)
-    other_w2 = lax.ppermute(own_w2, "chan", core_swap)
+        strip(picture[:2], first_u), strip(picture[height - 2 :], last_u), "rows"
+    )
+    upstream = placed + core_swapped(placed)
+    other_w2 = core_swapped(own_w2)
     tall_a = jnp.concatenate([before[:2], picture, after[:2]], axis=0)
-    tall_u = jnp.concatenate([before[2:] + before_x, upstream, after[2:] + after_x], axis=0)
+    tall_u = jnp.concatenate([before[2:], upstream, after[2:]], axis=0)
 
     n_a, n_u = tall_a.shape[0], tall_u.shape[0]
     side = lambda a, u: jnp.concatenate([a.reshape(n_a, lanes), u.reshape(4 * n_u, lanes)], axis=0)
@@ -329,18 +379,22 @@
         tall_u, after[n_a:].reshape(n_u, 4, lanes), before[n_a:].reshape(n_u, 4, lanes)
     )
 
+    quarter = tile_index % 2 * 2 + row_index % 2
     flags = jnp.stack(
         [
             (row_index < n_rows - 1).astype(jnp.int32),
             (tile_index < n_tiles - 1).astype(jnp.int32),
             chan_index,
+            quarter,
+            jnp.int32(cols),
         ]
     )
-    input_grad, weights = pl.pallas_call(
+    part = 14 * half // 4
+    mid_grad, weights = pl.pallas_call(
         main_kernel,
         out_shape=(
-            jax.ShapeDtypeStruct((rows, 2, cols, lanes), BF),
-            jax.ShapeDtypeStruct((2, 7 * half, lanes), BF),
+            jax.ShapeDtypeStruct((rows + 1, SLOTS, lanes), BF),
+            jax.ShapeDtypeStruct((4, part, lanes), BF),
         ),
         in_specs=[scalars] + [whole] * 6,
         out_specs=(whole, whole),
@@ -355,28 +409,41 @@
         other_w2,
         shift_row,
     )
-
-    even = row_index % 2 == 0
-    if n_rows > 1:
-        kept = jnp.where(even, weights[0], weights[1])
-        sent = jnp.where(even, weights[1], weights[0])
-        got = lax.ppermute(sent, "rows", swaps(n_rows, 1))
-        total = (kept.astype(F32) + got.astype(F32)).astype(BF)
+    input_grad = pl.pallas_call(
+        input_kernel,
+        out_shape=jax.ShapeDtypeStruct((rows, 2, cols, lanes), BF),
+        in_specs=[whole, whole],
+        out_specs=whole,
+        compiler_params=limit,
+    )(mid_grad, wa)
+
+    def from_block(values):
+        return [
+            lax.ppermute(
+                value,
+                ("tiles", "rows"),
+                [
+                    (t * n_rows + r, (t ^ (d >> 1)) * n_rows + (r ^ (d & 1)))
+                    for t in range(n_tiles)
+                    for r in range(n_rows)
+                ],
+            )
+            for d, value in enumerate(values, 1)
+        ]
+
+    one, two, three = from_block([weights[1], weights[2], weights[3]])
+    total = (
+        (weights[0].astype(F32) + one.astype(F32)) + (two.astype(F32) + three.astype(F32))
+    ).astype(BF)
     distance = 2
     while distance < n_rows:
         total = summed_pair(total, "rows", n_rows, distance)
         distance *= 2
-    if n_tiles == 4:
-        one, two, three = (lax.ppermute(total, "tiles", swaps(4, d)) for d in (1, 2, 3))
-        total = (
-            (total.astype(F32) + one.astype(F32)) + (two.astype(F32) + three.astype(F32))
-        ).astype(BF)
-    else:
-        distance = 1
-        while distance < n_tiles:
-            total = summed_pair(total, "tiles", n_tiles, distance)
-            distance *= 2
-    other = lax.ppermute(total, "rows", swaps(n_rows, 1))
+    distance = 2
+    while distance < n_tiles:
+        total = summed_pair(total, "tiles", n_tiles, distance)
+        distance *= 2
+    pieces = [total] + from_block([total] * 3)
 
     pixels = n_rows * TISS_MEAN * n_tiles * out_side * out_side
     scale = 1.0 / math.sqrt(pixels)
@@ -386,10 +453,11 @@
             jax.ShapeDtypeStruct((9, channels, half), F32),
             jax.ShapeDtypeStruct((9, half, mids), F32),
         ),
-        in_specs=[scalars, whole, whole],
+        in_specs=[scalars] + [whole] * 4,
         out_specs=(whole, whole),
+        scratch_shapes=[pltpu.VMEM((4, part, lanes), BF)],
         compiler_params=limit,
-    )(row_index.reshape(1) % 2, total, other)
+    )(quarter.reshape(1), *pieces)
     return (
         input_grad.reshape(height, pairs * lanes),
         first.reshape(3, 3, channels, half),

time: 39.8 us -> 39.1 us (0.982)
  waiting for transfers between devices: 17.4 us -> 15.2 us
  starting transfers between devices: 14.4 us -> 15.6 us
    ppermute x11 -> x13, waiting for transfers between devices: 17.4 us -> 15.2 us  [the longest x6 6.86 us: from_block(): lax.ppermute(value, ('tiles', 'rows'), [(t * n_rows + r, (t ^ d >> 1) * n...]
    ppermute x11 -> x13, starting transfers between devices: 14.4 us -> 15.6 us  [the longest x6 7.18 us: from_block(): lax.ppermute(value, ('tiles', 'rows'), [(t * n_rows + r, (t ^ d >> 1) * n...]
    pallas_call x1 -> x2, Pallas kernels: 2.18 us -> 2.43 us  [the longest x1 1.94 us: shards(): pl.pallas_call(main_kernel, out_shape=(jax.ShapeDtypeStruct((rows + 1, SL...]
  transfers between devices with their start and end apart: 11 -> 13, of which waited for: 7 -> 11; matrix products, arithmetic and copies ran while one was open for 5% -> 5% of each run, Pallas kernels for 0% -> 1%
where the time goes in v3:
time: 39.1 us; the launch traced here: 38.9 us
  starting transfers between devices  15.6 us (40%)
  waiting for transfers between devices  15.2 us (39%)
  Pallas kernels  4.41 us (11%)
  between operations  1.6 us (4%)
  local copies, waits for them, and re-layouts  1.41 us (4%)
  other arithmetic  0.72 us (2%)
    ppermute x6, starting transfers between devices, from_block(): lax.ppermute(value, ('tiles', 'rows'), [(t * n_rows + r, (t ^ d >> 1) * n...  7.18 us
    ppermute x6, waiting for transfers between devices, from_block(): lax.ppermute(value, ('tiles', 'rows'), [(t * n_rows + r, (t ^ d >> 1) * n...  6.86 us
    ppermute x1, starting transfers between devices, neighbour_strips(): got = lax.ppermute(to_even, axis, swaps(size, 1))  2.71 us
    ppermute x1, starting transfers between devices, summed_pair(): got = lax.ppermute(value, axis, swaps(size, distance))  2.65 us
    ppermute x1, waiting for transfers between devices, summed_pair(): got = lax.ppermute(value, axis, swaps(size, distance))  2.5 us
    ppermute x1, waiting for transfers between devices, neighbour_strips(): got = lax.ppermute(to_even, axis, swaps(size, 1))  2.44 us
    ppermute x1, waiting for transfers between devices, neighbour_strips(): lax.ppermute(jnp.where(low, to_even, to_odd), ('tiles', 'rows', 'chan'),...  2.02 us
    pallas_call x1, Pallas kernels, shards(): pl.pallas_call(main_kernel, out_shape=(jax.ShapeDtypeStruct((rows + 1, SL...  1.94 us
  transfers between devices with their start and end apart: 13, of which 11 were waited for; matrix products, arithmetic and copies ran while one was open for 5% of the time, Pallas kernels for 1%

profile of v3, /device:TPU:0, one launch (start us, length us, event | category | flops | bytes accessed | tf_op | source)
XLA Modules:
  0.0 38.9 jit_solution(3503619114119538713)
XLA Ops:
  1.3 1.1 %shard_map.94 = (bf16[12,48,128]{2,1,0:T(8,128)(2,1)S(1)}, bf16[384,256]{1,0:T(8,128)(2,1)S(1)}, bf16[3,3,64,128]{3,2,1,0:T(8,128)(2,1)S(1)}, f32[1,128]{1,0:T(1,128)S(1)}) custom-call(s32[1]{0:T(128)} %bitcast.2.chan, s32[1,1]{1,0:T(1,128)S(6)} %copy.29.count, s32[1,1,16]{2,1,0:T(1,128)} %order_hbm.1, bf16[12,48,64]{2,1,0:T(8,128)(2,1)} %cot_hbm.1, ...), custom_call_target="tpu_custom_call" | custom-call | tf_op jit(solution)/shard_map/pallas_call | solution.py:315
  2.4 0.5 %collective-permute-start.2 = (bf16[12,48,128]{2,1,0:T(8,128)(2,1)S(1)}, bf16[12,48,128]{2,1,0:T(8,128)(2,1)S(1)}, u32[]{:S(2)}, u32[]{:S(2)}) collective-permute-start(bf16[12,48,128]{2,1,0:T(8,128)(2,1)S(1)} %get-tuple-element.11), channel_id=1, source_target_pairs={{0,1},{1,0},{2,3},{3,2},{4,5},{5,4},{6,7},{7,6},{8,9},{9,8},{10,11... | collective-permute-start | bytes 442376 | tf_op jit(solution)/shard_map/ppermute | solution.py:23
  3.0 0.1 collective-permute-start
  3.2 1.1 %collective-permute-done = bf16[3,48,128]{2,1,0:T(8,128)(2,1)S(1)} collective-permute-done((bf16[3,48,128]{2,1,0:T(8,128)(2,1)S(1)}, bf16[3,48,128]{2,1,0:T(8,128)(2,1)S(1)}, u32[]{:S(2)}, u32[]{:S(2)}) %collective-permute-start) | collective-permute-done | bytes 36896 | tf_op jit(solution)/shard_map/ppermute | solution.py:23
  4.3 2.7 %collective-permute-start.1 = (bf16[5,48,128]{2,1,0:T(8,128)(2,1)S(1)}, bf16[5,48,128]{2,1,0:T(8,128)(2,1)S(1)}, u32[]{:S(2)}, u32[]{:S(2)}) collective-permute-start(bf16[5,48,128]{2,1,0:T(8,128)(2,1)S(1)} %fusion.2), channel_id=1, source_target_pairs={{0,2},{2,0},{1,3},{3,1},{4,6},{6,4},{5,7},{7,5},{8,10},{10,8},{9,1... | collective-permute-start | bytes 184328 | tf_op jit(solution)/shard_map/ppermute | solution.py:57
  7.1 2.4 %collective-permute-done.1 = bf16[5,48,128]{2,1,0:T(8,128)(2,1)S(1)} collective-permute-done((bf16[5,48,128]{2,1,0:T(8,128)(2,1)S(1)}, bf16[5,48,128]{2,1,0:T(8,128)(2,1)S(1)}, u32[]{:S(2)}, u32[]{:S(2)}) %collective-permute-start.1) | collective-permute-done | bytes 61472 | tf_op jit(solution)/shard_map/ppermute | solution.py:57
  9.6 0.2 pad_maximum_fusion.1
  10.0 1.9 %collective-permute-start.3 = (bf16[100,128]{1,0:T(8,128)(2,1)S(1)}, bf16[100,128]{1,0:T(8,128)(2,1)S(1)}, u32[]{:S(2)}, u32[]{:S(2)}) collective-permute-start(bf16[100,128]{1,0:T(8,128)(2,1)S(1)} %select_select_fusion.2), channel_id=1, source_target_pairs={{0,4},{1,3},{2,6},{3,1},{4,0},{5,9},{6,2},{7,11},{8,12},{9,5},{10,... | collective-permute-start | bytes 76808 | tf_op jit(solution)/shard_map/ppermute | solution.py:61
  11.9 2.0 %collective-permute-done.3 = bf16[100,128]{1,0:T(8,128)(2,1)S(1)} collective-permute-done((bf16[100,128]{1,0:T(8,128)(2,1)S(1)}, bf16[100,128]{1,0:T(8,128)(2,1)S(1)}, u32[]{:S(2)}, u32[]{:S(2)}) %collective-permute-start.3) | collective-permute-done | bytes 25632 | tf_op jit(solution)/shard_map/ppermute | solution.py:61
  13.9 0.5 %collective-permute-start.5 = (bf16[3,3,64,128]{3,2,1,0:T(8,128)(2,1)S(1)}, bf16[3,3,64,128]{3,2,1,0:T(8,128)(2,1)S(1)}, u32[]{:S(2)}, u32[]{:S(2)}) collective-permute-start(bf16[3,3,64,128]{3,2,1,0:T(8,128)(2,1)S(1)} %get-tuple-element.13.own_w2), channel_id=1, source_target_pairs={{0,1},{1,0},{2,3},{3,2},{4,5},{5,4},{6,7},{7,6},{8,9},{9,8},{10,11... | collective-permute-start | bytes 442376 | tf_op jit(solution)/shard_map/ppermute | solution.py:23
  14.6 0.1 stack.27.flags
  14.6 0.1 copy.17
  14.8 0.3 collective-permute-done.4
  15.2 0.2 pad_maximum_fusion.a_ref
  15.4 0.1 pad_maximum_fusion.2.u_ref
  15.5 1.9 %shard_map.95 = (bf16[13,64,128]{2,1,0:T(8,128)(2,1)S(1)}, bf16[4,224,128]{2,1,0:T(8,128)(2,1)S(1)}) custom-call(s32[5]{0:T(128)S(1)} %stack.27.flags, bf16[14,2,64,128]{3,2,1,0:T(8,128)(2,1)S(1)} %pad_maximum_fusion.a_ref, bf16[18,64,128]{2,1,0:T(8,128)(2,1)S(1)} %pad_maximum_fusion.2.u_ref, bf16[384,256]{1,0:T(8,128)(2,1)S(1)} %get-tuple-element.12.wa_ref, ...), custom_call_target="tpu_custom_call" | custom-call | tf_op jit(solution)/shard_map/pallas_call | solution.py:393
  17.5 1.8 %collective-permute-start.6 = (bf16[224,128]{1,0:T(8,128)(2,1)S(1)}, bf16[224,128]{1,0:T(8,128)(2,1)S(1)}, u32[]{:S(2)}, u32[]{:S(2)}) collective-permute-start(bf16[224,128]{1,0:T(8,128)(2,1)S(1)} %get-tuple-element.23), channel_id=1, source_target_pairs={{0,2},{2,0},{4,6},{6,4},{8,10},{10,8},{12,14},{14,12},{1,3},{3,1},... | collective-permute-start | bytes 172040 | tf_op jit(solution)/shard_map/ppermute | solution.py:422
  19.3 1.5 %collective-permute-start.8 = (bf16[224,128]{1,0:T(8,128)(2,1)S(1)}, bf16[224,128]{1,0:T(8,128)(2,1)S(1)}, u32[]{:S(2)}, u32[]{:S(2)}) collective-permute-start(bf16[224,128]{1,0:T(8,128)(2,1)S(1)} %get-tuple-element.24), channel_id=1, source_target_pairs={{0,6},{2,4},{4,2},{6,0},{8,14},{10,12},{12,10},{14,8},{1,7},{3,5},... | collective-permute-start | bytes 172040 | tf_op jit(solution)/shard_map/ppermute | solution.py:422
  20.9 0.2 collective-permute-start.7
  21.1 0.7 %collective-permute-done.6 = bf16[224,128]{1,0:T(8,128)(2,1)S(1)} collective-permute-done((bf16[224,128]{1,0:T(8,128)(2,1)S(1)}, bf16[224,128]{1,0:T(8,128)(2,1)S(1)}, u32[]{:S(2)}, u32[]{:S(2)}) %collective-permute-start.6) | collective-permute-done | bytes 57376 | tf_op jit(solution)/shard_map/ppermute | solution.py:422
  21.7 3.0 %collective-permute-done.8 = bf16[224,128]{1,0:T(8,128)(2,1)S(1)} collective-permute-done((bf16[224,128]{1,0:T(8,128)(2,1)S(1)}, bf16[224,128]{1,0:T(8,128)(2,1)S(1)}, u32[]{:S(2)}, u32[]{:S(2)}) %collective-permute-start.8) | collective-permute-done | bytes 57376 | tf_op jit(solution)/shard_map/ppermute | solution.py:422
  24.7 0.3 collective-permute-done.7
  25.1 2.7 %collective-permute-start.9 = (bf16[224,128]{1,0:T(8,128)(2,1)S(1)}, bf16[224,128]{1,0:T(8,128)(2,1)S(1)}, u32[]{:S(2)}, u32[]{:S(2)}) collective-permute-start(bf16[224,128]{1,0:T(8,128)(2,1)S(1)} %fusion.1), channel_id=1, source_target_pairs={{0,8},{4,12},{8,0},{12,4},{1,9},{5,13},{9,1},{13,5},{2,10},{6,14},... | collective-permute-start | bytes 172040 | tf_op jit(solution)/shard_map/ppermute | solution.py:294
  27.7 2.5 %collective-permute-done.9 = bf16[224,128]{1,0:T(8,128)(2,1)S(1)} collective-permute-done((bf16[224,128]{1,0:T(8,128)(2,1)S(1)}, bf16[224,128]{1,0:T(8,128)(2,1)S(1)}, u32[]{:S(2)}, u32[]{:S(2)}) %collective-permute-start.9) | collective-permute-done | bytes 57376 | tf_op jit(solution)/shard_map/ppermute | solution.py:294
  30.2 1.9 %collective-permute-start.12 = (bf16[224,128]{1,0:T(8,128)(2,1)S(1)}, bf16[224,128]{1,0:T(8,128)(2,1)S(1)}, u32[]{:S(2)}, u32[]{:S(2)}) collective-permute-start(bf16[224,128]{1,0:T(8,128)(2,1)S(1)} %add_convert_fusion.piece_0), channel_id=1, source_target_pairs={{0,6},{2,4},{4,2},{6,0},{8,14},{10,12},{12,10},{14,8},{1,7},{3,5},... | collective-permute-start | bytes 172040 | tf_op jit(solution)/shard_map/ppermute | solution.py:422
  32.1 1.7 %collective-permute-start.11 = (bf16[224,128]{1,0:T(8,128)(2,1)S(1)}, bf16[224,128]{1,0:T(8,128)(2,1)S(1)}, u32[]{:S(2)}, u32[]{:S(2)}) collective-permute-start(bf16[224,128]{1,0:T(8,128)(2,1)S(1)} %add_convert_fusion.piece_0), channel_id=1, source_target_pairs={{0,4},{2,6},{4,0},{6,2},{8,12},{10,14},{12,8},{14,10},{1,5},{3,7},... | collective-permute-start | bytes 172040 | tf_op jit(solution)/shard_map/ppermute | solution.py:422
  33.9 0.5 %shard_map.96 = bf16[12,2,48,128]{3,2,1,0:T(8,128)(2,1)S(1)} custom-call(bf16[13,64,128]{2,1,0:T(8,128)(2,1)S(1)} %get-tuple-element.15.mid_ref, bf16[384,256]{1,0:T(8,128)(2,1)S(1)} %get-tuple-element.12.wa_ref), custom_call_target="tpu_custom_call" | custom-call | tf_op jit(solution)/shard_map/pallas_call | solution.py:412
  34.4 0.8 %copy.28 = bf16[3,8,48,128]{3,1,2,0:T(8,128)(2,1)} copy(bf16[3,8,48,128]{3,2,1,0:T(8,128)(2,1)S(1)} %bitcast.46) | data formatting | bytes 589824
  35.2 0.2 collective-permute-done.12.piece_3
  35.4 1.2 %collective-permute-done.11.piece_2 = bf16[224,128]{1,0:T(8,128)(2,1)S(1)} collective-permute-done((bf16[224,128]{1,0:T(8,128)(2,1)S(1)}, bf16[224,128]{1,0:T(8,128)(2,1)S(1)}, u32[]{:S(2)}, u32[]{:S(2)}) %collective-permute-start.11) | collective-permute-done | bytes 57376 | tf_op jit(solution)/shard_map/ppermute | solution.py:422
  36.6 1.4 %collective-permute-done.10.piece_1 = bf16[224,128]{1,0:T(8,128)(2,1)S(1)} collective-permute-done((bf16[224,128]{1,0:T(8,128)(2,1)S(1)}, bf16[224,128]{1,0:T(8,128)(2,1)S(1)}, u32[]{:S(2)}, u32[]{:S(2)}) %collective-permute-start.10) | collective-permute-done | bytes 57376 | tf_op jit(solution)/shard_map/ppermute | solution.py:422
  38.0 0.9 %shard_map.97 = (f32[9,64,64]{2,1,0:T(8,128)}, f32[9,64,128]{2,1,0:T(8,128)}) custom-call(s32[1]{0:T(128)} %bitcast.3.flags, bf16[224,128]{1,0:T(8,128)(2,1)S(1)} %add_convert_fusion.piece_0, bf16[224,128]{1,0:T(8,128)(2,1)S(1)} %collective-permute-done.10.piece_1, bf16[224,128]{1,0:T(8,128)(2,1)S(1)} %collective-permute-done.11.piece_2, ...), custom_call_target="tpu_custom_call" | custom-call | tf_op jit(solution)/shard_map/pallas_call | solution.py:450
  (37 shorter events, 0.6 us)
Async XLA Ops:
  0.6 2.5 %copy-start = (bf16[24,6144]{1,0:T(8,128)(2,1)S(1)}, bf16[24,6144]{1,0:T(8,128)(2,1)}, u32[]{:S(2)}) copy-start(bf16[24,6144]{1,0:T(8,128)(2,1)} %param.7) | copy-start | bytes 884740
  2.4 7.4 %collective-permute-start.2 = (bf16[12,48,128]{2,1,0:T(8,128)(2,1)S(1)}, bf16[12,48,128]{2,1,0:T(8,128)(2,1)S(1)}, u32[]{:S(2)}, u32[]{:S(2)}) collective-permute-start(bf16[12,48,128]{2,1,0:T(8,128)(2,1)S(1)} %get-tuple-element.11), channel_id=1, source_target_pairs={{0,1},{1,0},{2,3},{3,2},{4,5},{5,4},{6,7},{7,6},{8,9},{9,8},{10,11... | collective-permute-start | bytes 442376 | tf_op jit(solution)/shard_map/ppermute | solution.py:23
  3.0 1.3 %collective-permute-start = (bf16[3,48,128]{2,1,0:T(8,128)(2,1)S(1)}, bf16[3,48,128]{2,1,0:T(8,128)(2,1)S(1)}, u32[]{:S(2)}, u32[]{:S(2)}) collective-permute-start(bf16[3,48,128]{2,1,0:T(8,128)(2,1)S(1)} %slice_select_fusion), channel_id=1, source_target_pairs={{0,1},{1,0},{2,3},{3,2},{4,5},{5,4},{6,7},{7,6},{8,9},{9,8},{10,11... | collective-permute-start | bytes 110600 | tf_op jit(solution)/shard_map/ppermute | solution.py:23
  4.3 5.2 %collective-permute-start.1 = (bf16[5,48,128]{2,1,0:T(8,128)(2,1)S(1)}, bf16[5,48,128]{2,1,0:T(8,128)(2,1)S(1)}, u32[]{:S(2)}, u32[]{:S(2)}) collective-permute-start(bf16[5,48,128]{2,1,0:T(8,128)(2,1)S(1)} %fusion.2), channel_id=1, source_target_pairs={{0,2},{2,0},{1,3},{3,1},{4,6},{6,4},{5,7},{7,5},{8,10},{10,8},{9,1... | collective-permute-start | bytes 184328 | tf_op jit(solution)/shard_map/ppermute | solution.py:57
  10.0 3.9 %collective-permute-start.3 = (bf16[100,128]{1,0:T(8,128)(2,1)S(1)}, bf16[100,128]{1,0:T(8,128)(2,1)S(1)}, u32[]{:S(2)}, u32[]{:S(2)}) collective-permute-start(bf16[100,128]{1,0:T(8,128)(2,1)S(1)} %select_select_fusion.2), channel_id=1, source_target_pairs={{0,4},{1,3},{2,6},{3,1},{4,0},{5,9},{6,2},{7,11},{8,12},{9,5},{10,... | collective-permute-start | bytes 76808 | tf_op jit(solution)/shard_map/ppermute | solution.py:61
  13.9 1.2 %collective-permute-start.4 = (bf16[100,128]{1,0:T(8,128)(2,1)S(1)}, bf16[100,128]{1,0:T(8,128)(2,1)S(1)}, u32[]{:S(2)}, u32[]{:S(2)}) collective-permute-start(bf16[100,128]{1,0:T(8,128)(2,1)S(1)} %collective-permute-done.3), channel_id=1, source_target_pairs={{0,1},{1,0},{2,3},{3,2},{4,5},{5,4},{6,7},{7,6},{8,9},{9,8},{10,11... | collective-permute-start | bytes 76808 | tf_op jit(solution)/shard_map/ppermute | solution.py:23
  13.9 1.6 %collective-permute-start.5 = (bf16[3,3,64,128]{3,2,1,0:T(8,128)(2,1)S(1)}, bf16[3,3,64,128]{3,2,1,0:T(8,128)(2,1)S(1)}, u32[]{:S(2)}, u32[]{:S(2)}) collective-permute-start(bf16[3,3,64,128]{3,2,1,0:T(8,128)(2,1)S(1)} %get-tuple-element.13.own_w2), channel_id=1, source_target_pairs={{0,1},{1,0},{2,3},{3,2},{4,5},{5,4},{6,7},{7,6},{8,9},{9,8},{10,11... | collective-permute-start | bytes 442376 | tf_op jit(solution)/shard_map/ppermute | solution.py:23
  17.5 4.2 %collective-permute-start.6 = (bf16[224,128]{1,0:T(8,128)(2,1)S(1)}, bf16[224,128]{1,0:T(8,128)(2,1)S(1)}, u32[]{:S(2)}, u32[]{:S(2)}) collective-permute-start(bf16[224,128]{1,0:T(8,128)(2,1)S(1)} %get-tuple-element.23), channel_id=1, source_target_pairs={{0,2},{2,0},{4,6},{6,4},{8,10},{10,8},{12,14},{14,12},{1,3},{3,1},... | collective-permute-start | bytes 172040 | tf_op jit(solution)/shard_map/ppermute | solution.py:422
  19.3 5.4 %collective-permute-start.8 = (bf16[224,128]{1,0:T(8,128)(2,1)S(1)}, bf16[224,128]{1,0:T(8,128)(2,1)S(1)}, u32[]{:S(2)}, u32[]{:S(2)}) collective-permute-start(bf16[224,128]{1,0:T(8,128)(2,1)S(1)} %get-tuple-element.24), channel_id=1, source_target_pairs={{0,6},{2,4},{4,2},{6,0},{8,14},{10,12},{12,10},{14,8},{1,7},{3,5},... | collective-permute-start | bytes 172040 | tf_op jit(solution)/shard_map/ppermute | solution.py:422
  20.9 4.2 %collective-permute-start.7 = (bf16[224,128]{1,0:T(8,128)(2,1)S(1)}, bf16[224,128]{1,0:T(8,128)(2,1)S(1)}, u32[]{:S(2)}, u32[]{:S(2)}) collective-permute-start(bf16[224,128]{1,0:T(8,128)(2,1)S(1)} %get-tuple-element.25), channel_id=1, source_target_pairs={{0,4},{2,6},{4,0},{6,2},{8,12},{10,14},{12,8},{14,10},{1,5},{3,7},... | collective-permute-start | bytes 172040 | tf_op jit(solution)/shard_map/ppermute | solution.py:422
  25.1 5.2 %collective-permute-start.9 = (bf16[224,128]{1,0:T(8,128)(2,1)S(1)}, bf16[224,128]{1,0:T(8,128)(2,1)S(1)}, u32[]{:S(2)}, u32[]{:S(2)}) collective-permute-start(bf16[224,128]{1,0:T(8,128)(2,1)S(1)} %fusion.1), channel_id=1, source_target_pairs={{0,8},{4,12},{8,0},{12,4},{1,9},{5,13},{9,1},{13,5},{2,10},{6,14},... | collective-permute-start | bytes 172040 | tf_op jit(solution)/shard_map/ppermute | solution.py:294
  30.2 5.1 %collective-permute-start.12 = (bf16[224,128]{1,0:T(8,128)(2,1)S(1)}, bf16[224,128]{1,0:T(8,128)(2,1)S(1)}, u32[]{:S(2)}, u32[]{:S(2)}) collective-permute-start(bf16[224,128]{1,0:T(8,128)(2,1)S(1)} %add_convert_fusion.piece_0), channel_id=1, source_target_pairs={{0,6},{2,4},{4,2},{6,0},{8,14},{10,12},{12,10},{14,8},{1,7},{3,5},... | collective-permute-start | bytes 172040 | tf_op jit(solution)/shard_map/ppermute | solution.py:422
  32.1 4.5 %collective-permute-start.11 = (bf16[224,128]{1,0:T(8,128)(2,1)S(1)}, bf16[224,128]{1,0:T(8,128)(2,1)S(1)}, u32[]{:S(2)}, u32[]{:S(2)}) collective-permute-start(bf16[224,128]{1,0:T(8,128)(2,1)S(1)} %add_convert_fusion.piece_0), channel_id=1, source_target_pairs={{0,4},{2,6},{4,0},{6,2},{8,12},{10,14},{12,8},{14,10},{1,5},{3,7},... | collective-permute-start | bytes 172040 | tf_op jit(solution)/shard_map/ppermute | solution.py:422
  33.9 4.2 %collective-permute-start.10 = (bf16[224,128]{1,0:T(8,128)(2,1)S(1)}, bf16[224,128]{1,0:T(8,128)(2,1)S(1)}, u32[]{:S(2)}, u32[]{:S(2)}) collective-permute-start(bf16[224,128]{1,0:T(8,128)(2,1)S(1)} %add_convert_fusion.piece_0), channel_id=1, source_target_pairs={{0,2},{2,0},{4,6},{6,4},{8,10},{10,8},{12,14},{14,12},{1,3},{3,1},... | collective-permute-start | bytes 172040 | tf_op jit(solution)/shard_map/ppermute | solution.py:422

commit v4 on v3

--- a/solution.py
+++ b/solution.py
@@ -46,23 +46,28 @@
     return pairs
 
 
-def neighbour_strips(first, last, axis):
-    size, index = lax.axis_size(axis), lax.axis_index(axis)
-    even = index % 2 == 0
-    none = jnp.zeros_like(first)
+def sends_last(axis):
+    even = lax.axis_index(axis) % 2 == 0
+    return even if lax.axis_size(axis) <= 2 else (lax.axis_index("chan") == 0) == even
+
+
+def traded(value, axis):
+    size = lax.axis_size(axis)
     if size == 1:
-        return none, none
-    to_even, to_odd = jnp.where(even, last, first), jnp.where(even, first, last)
+        return jnp.zeros_like(value), jnp.zeros_like(value)
     if size == 2:
-        got = lax.ppermute(to_even, axis, swaps(size, 1))
-        return jnp.where(even, none, got), jnp.where(even, got, none)
-    low = lax.axis_index("chan") == 0
+        got = lax.ppermute(value, axis, swaps(size, 1))
+        return got, got
     pairs = shared_pairs(axis, lax.axis_size("tiles"), lax.axis_size("rows"))
-    got = lax.ppermute(jnp.where(low, to_even, to_odd), ("tiles", "rows", "chan"), pairs)
-    other = core_swapped(got)
-    own_first = low == even
-    before = jnp.where(index == 0, none, jnp.where(own_first, other, got))
-    after = jnp.where(index == size - 1, none, jnp.where(own_first, got, other))
+    got = lax.ppermute(value, ("tiles", "rows", "chan"), pairs)
+    return got, core_swapped(got)
+
+
+def before_and_after(got, other, axis):
+    index, none = lax.axis_index(axis), jnp.zeros_like(got)
+    last = sends_last(axis)
+    before = jnp.where(index == 0, none, jnp.where(last, other, got))
+    after = jnp.where(index == lax.axis_size(axis) - 1, none, jnp.where(last, got, other))
     return before, after
 
 
@@ -71,23 +76,25 @@
 
 
 def prepare_kernel(
-    chan,
-    count,
+    n_rows,
+    count_ref,
     order_hbm,
     cot_hbm,
     w1_hbm,
     w2_hbm,
     shift_hbm,
-    z_ref,
+    near_ref,
+    edge_ref,
+    w2_ref,
     wa_ref,
-    w2_ref,
     shift_ref,
     cot,
     w1,
     order,
-    tissue,
+    rank,
     sems,
 ):
+    rows, cols, half = cot.shape
     pairs = [
         (order_hbm, order),
         (cot_hbm, cot),
@@ -99,27 +106,37 @@
     for copy in copies:
         copy.start()
     copies[0].wait()
-    tiles = order.shape[2]
-    for k in range(tiles):
-        tissue[order[0, 0, k]] = jnp.where(k < count[0, 0], 1, 0)
-    rows, cols, half = cot.shape
+    for k in range(order.shape[2]):
+        rank[order[0, 0, k]] = k
     side = TP // 2
     across = cols // side
     col_id = lax.broadcasted_iota(jnp.int32, (cols, 2 * half), 0)
     lane_id = lax.broadcasted_iota(jnp.int32, (cols, 2 * half), 1)
-    mine = (lane_id < half) == (chan[0] == 0)
+    mine = (lane_id < half) == (lax.axis_index("chan") == 0)
     masks = []
     for a in range(rows // side):
-        live = jnp.zeros((cols, 2 * half), jnp.int32)
+        place = jnp.zeros((cols, 2 * half), jnp.int32)
         for b in range(across):
             inside = (col_id >= b * side) & (col_id < (b + 1) * side)
-            live = jnp.where(inside, tissue[a * across + b], live)
-        masks.append((live > 0) & mine)
+            place = jnp.where(inside, rank[a * across + b], place)
+        masks.append((place < count_ref[0:1, :]) & mine)
     copies[1].wait()
+    lower = lax.axis_index("rows") % 2 == 0
+    kept = []
     for i in range(rows):
         value = cot[i].astype(F32)
         twice = jnp.concatenate([value, value], axis=1)
-        z_ref[i] = jnp.where(masks[i // side], twice, 0.0).astype(BF)
+        placed = jnp.where(masks[i // side], twice, 0.0)
+        near_ref[i] = placed.astype(BF)
+        kept.append(placed)
+    for i in range(3):
+        top, bottom = kept[i], kept[rows - 3 + i]
+        at = slice(i * cols, (i + 1) * cols)
+        if n_rows == 2:
+            edge_ref[0, at, :] = jnp.where(lower, bottom, top).astype(BF)
+        else:
+            edge_ref[0, at, :] = top.astype(BF)
+            edge_ref[1, at, :] = bottom.astype(BF)
     copies[2].wait()
     lanes = 2 * half
     for u in range(3):
@@ -141,15 +158,70 @@
     return value.reshape(value.shape[0] // SLOTS, SLOTS, value.shape[1])
 
 
+def block_place():
+    return lax.axis_index("tiles") % 2 * 2 + lax.axis_index("rows") % 2
+
+
 def main_kernel(
-    flags, a_ref, u_ref, wa_ref, own_w2, other_w2, shift_ref, mid_ref, weight_ref, w2_ref
+    n_tiles,
+    n_rows,
+    picture_ref,
+    near_ref,
+    far_ref,
+    own_w2_ref,
+    other_w2_ref,
+    before_ref,
+    after_ref,
+    got_ref,
+    got_other_ref,
+    wa_ref,
+    shift_ref,
+    mid_ref,
+    weight_ref,
+    a_ref,
+    u_ref,
+    w2_ref,
 ):
-    rows = a_ref.shape[0] - 2
+    rows = u_ref.shape[0] - 6
+    height, own_cols, lanes = picture_ref.shape
     tall = rows + 1
-    own_cols = flags[4]
-    lanes = a_ref.shape[3]
     half = lanes // 2
-    low = flags[2] == 0
+    row_index, tile_index = lax.axis_index("rows"), lax.axis_index("tiles")
+    low = lax.axis_index("chan") == 0
+
+    a_ref[0, :, :own_cols] = before_ref[:2]
+    a_ref[rows + 1, :, :own_cols] = after_ref[:2]
+    u_ref[:3, :own_cols] = before_ref[2:]
+    u_ref[rows + 3 :, :own_cols] = after_ref[2:]
+    for i in range(rows):
+        a_ref[i + 1, :, :own_cols] = picture_ref[2 * i : 2 * i + 2]
+        u_ref[i + 3, :own_cols] = near_ref[i] + far_ref[i]
+    got, shared = got_ref[...].astype(F32), got_other_ref[...].astype(F32)
+    mine_after = tile_index % 2 == 0
+    if n_tiles > 2:
+        mine_after = low == mine_after
+        left_strip, right_strip = jnp.where(mine_after, shared, got), jnp.where(mine_after, got, shared)
+    else:
+        left_strip = right_strip = got
+    left_strip = jnp.where(tile_index == 0, 0.0, left_strip)
+    right_strip = jnp.where(tile_index == n_tiles - 1, 0.0, right_strip)
+
+    def edge(at, count):
+        fill = jnp.zeros((SLOTS - own_cols - 2 * count, lanes), F32)
+        value = [right_strip[at : at + count], fill, left_strip[at : at + count]]
+        return jnp.concatenate(value, axis=0).astype(BF)
+
+    own_u, halo_a, halo_u = height, height + 4 * rows, height + 4 * rows + 4
+    for i in range(height):
+        a_ref[i // 2 + 1, i % 2, own_cols:] = edge(i, 1)
+    for i in range(2):
+        a_ref[0, i, own_cols:] = edge(halo_a + i, 1)
+        a_ref[rows + 1, i, own_cols:] = edge(halo_a + 2 + i, 1)
+    for i in range(rows):
+        u_ref[i + 3, own_cols:] = edge(own_u + 4 * i, 4)
+    for i in range(3):
+        u_ref[i, own_cols:] = edge(halo_u + 4 * i, 4)
+        u_ref[rows + 3 + i, own_cols:] = edge(halo_u + 12 + 4 * i, 4)
 
     def a_rows(count):
         return jnp.concatenate(
@@ -166,7 +238,8 @@
 
     for u in range(3):
         for w in range(3):
-            own_w, other_w = own_w2[u, w], other_w2[u, w]
+            at = slice((u * 3 + w) * half, (u * 3 + w + 1) * half)
+            own_w, other_w = own_w2_ref[at, :], other_w2_ref[at, :]
             across = slice(w * lanes, (w + 1) * lanes)
             w2_ref[u * lanes : u * lanes + half, across] = jnp.where(low, own_w, other_w)
             w2_ref[u * lanes + half : (u + 1) * lanes, across] = jnp.where(low, other_w, own_w)
@@ -174,8 +247,8 @@
     row_id = lax.broadcasted_iota(jnp.int32, (tall, SLOTS, lanes), 0)
     col_id = lax.broadcasted_iota(jnp.int32, (tall, SLOTS, lanes), 1)
     own = (row_id < rows) & (col_id < own_cols)
-    last_row = rows + flags[0]
-    last_col = own_cols + flags[1]
+    last_row = rows + jnp.where(row_index < n_rows - 1, 1, 0)
+    last_col = own_cols + jnp.where(tile_index < n_tiles - 1, 1, 0)
     valid = (row_id < last_row) & (col_id < last_col)
 
     wa = wa_ref[...]
@@ -213,7 +286,7 @@
     left = lax.broadcasted_iota(jnp.int32, (half, lanes), 1) < half
 
     part = weight_ref.shape[1]
-    me = flags[3]
+    me = block_place()
 
     def keep(block, value):
         done = 0
@@ -263,11 +336,12 @@
     grad_ref[:, 1] = (below[:rows, :own_cols] + above[1:tall, :own_cols]).astype(BF)
 
 
-def unpack_kernel(scale, flags, piece_0, piece_1, piece_2, piece_3, first_ref, second_ref, all_ref):
+def unpack_kernel(scale, piece_0, piece_1, piece_2, piece_3, first_ref, second_ref, all_ref):
     half = first_ref.shape[2]
     part = piece_0.shape[0]
+    me = block_place()
     for distance, piece in enumerate((piece_0, piece_1, piece_2, piece_3)):
-        all_ref[flags[0] ^ distance] = piece[...]
+        all_ref[me ^ distance] = piece[...]
 
     def block(number):
         done, values = 0, []
@@ -304,24 +378,23 @@
     tile_rows, tile_cols = height // TP, 2 * pairs // TP
     out_side = TP // 2
     n_rows, n_tiles = lax.axis_size("rows"), lax.axis_size("tiles")
-    row_index, tile_index = lax.axis_index("rows"), lax.axis_index("tiles")
-    chan_index = lax.axis_index("chan")
 
     whole = pl.BlockSpec(memory_space=pltpu.VMEM)
-    scalars = pl.BlockSpec(memory_space=pltpu.SMEM)
     in_hbm = pl.BlockSpec(memory_space=pltpu.HBM)
     limit = pltpu.CompilerParams(vmem_limit_bytes=48 << 20)
     half = channels
-    placed, wa, own_w2, shift_row = pl.pallas_call(
-        prepare_kernel,
+    n_edges = 1 if n_rows == 2 else 2
+    near, edges, own_w2, wa, shift_row = pl.pallas_call(
+        functools.partial(prepare_kernel, n_rows),
         out_shape=(
             jax.ShapeDtypeStruct((rows, cols, lanes), BF),
+            jax.ShapeDtypeStruct((n_edges, 3 * cols, lanes), BF),
+            jax.ShapeDtypeStruct((9 * half, mids), BF),
             jax.ShapeDtypeStruct((3 * lanes, 2 * mids), BF),
-            jax.ShapeDtypeStruct((3, 3, half, mids), BF),
             jax.ShapeDtypeStruct((1, mids), F32),
         ),
-        in_specs=[scalars] * 2 + [in_hbm] * 5,
-        out_specs=(whole,) * 4,
+        in_specs=[whole] + [in_hbm] * 5,
+        out_specs=(whole,) * 5,
         scratch_shapes=[
             pltpu.VMEM((rows, cols, half), BF),
             pltpu.VMEM((3, 3, channels, mids), BF),
@@ -331,84 +404,71 @@
         ],
         compiler_params=limit,
     )(
-        chan_index.reshape(1),
-        tissue_count,
+        jnp.broadcast_to(tissue_count, (8, lanes)),
         *(
             pltpu.with_memory_space_constraint(value, pltpu.HBM)
             for value in (
                 tile_order,
                 cotangent,
                 weight_one,
-                weight_two.swapaxes(2, 3),
+                weight_two.swapaxes(2, 3).reshape(9 * half, mids),
                 shift.reshape(1, mids),
             )
         ),
     )
-
-    picture = acts.reshape(height, pairs, lanes)
-    edges = jnp.stack([placed[:3], placed[rows - 3 :]])
     if n_rows == 2:
-        edge = jnp.where(row_index == 0, edges[1], edges[0])
-        edge = edge + core_swapped(edge)
-        first_u, last_u = edge, edge
+        edge_u = edges[0] + core_swapped(edges[0])
     else:
         edges = edges + core_swapped(edges)
-        first_u, last_u = edges[0], edges[1]
-    strip = lambda a, u: jnp.concatenate([a, u], axis=0)
-    before, after = neighbour_strips(
-        strip(picture[:2], first_u), strip(picture[height - 2 :], last_u), "rows"
-    )
-    upstream = placed + core_swapped(placed)
+        edge_u = jnp.where(sends_last("rows"), edges[1], edges[0])
+    picture = acts.reshape(height, pairs, lanes)
+    edge_a = jnp.where(sends_last("rows"), picture[height - 2 :], picture[:2])
+    before, after = (
+        value.reshape(5, cols, lanes)
+        for value in before_and_after(
+            *traded(jnp.concatenate([edge_a.reshape(2 * cols, lanes), edge_u], axis=0), "rows"),
+            "rows",
+        )
+    )
+    far = core_swapped(near)
+    own_w2, before = lax.optimization_barrier((own_w2, before))
     other_w2 = core_swapped(own_w2)
-    tall_a = jnp.concatenate([before[:2], picture, after[:2]], axis=0)
-    tall_u = jnp.concatenate([before[2:], upstream, after[2:]], axis=0)
-
-    n_a, n_u = tall_a.shape[0], tall_u.shape[0]
-    side = lambda a, u: jnp.concatenate([a.reshape(n_a, lanes), u.reshape(4 * n_u, lanes)], axis=0)
-    before, after = neighbour_strips(
-        side(tall_a[:, :1], tall_u[:, :4]), side(tall_a[:, cols - 1 :], tall_u[:, cols - 4 :]), "tiles"
-    )
-
-    def circular(middle, a, b):
-        gap = SLOTS - cols - a.shape[1] - b.shape[1]
-        fill = jnp.zeros((middle.shape[0], gap, lanes), BF)
-        return jnp.concatenate([middle, a, fill, b], axis=1)
-
-    full_a = circular(tall_a, after[:n_a].reshape(n_a, 1, lanes), before[:n_a].reshape(n_a, 1, lanes))
-    full_u = circular(
-        tall_u, after[n_a:].reshape(n_u, 4, lanes), before[n_a:].reshape(n_u, 4, lanes)
-    )
-
-    quarter = tile_index % 2 * 2 + row_index % 2
-    flags = jnp.stack(
-        [
-            (row_index < n_rows - 1).astype(jnp.int32),
-            (tile_index < n_tiles - 1).astype(jnp.int32),
-            chan_index,
-            quarter,
-            jnp.int32(cols),
-        ]
-    )
+
+    right = sends_last("tiles")
+    side = lambda value, count: jnp.where(
+        right, value[:, cols - count :], value[:, :count]
+    ).reshape(count * value.shape[0], lanes)
+    got, got_other = traded(
+        jnp.concatenate(
+            [
+                side(picture, 1),
+                side(near, 4) + side(far, 4),
+                side(before[:2], 1),
+                side(after[:2], 1),
+                side(before[2:], 4),
+                side(after[2:], 4),
+            ],
+            axis=0,
+        ),
+        "tiles",
+    )
+
     part = 14 * half // 4
     mid_grad, weights = pl.pallas_call(
-        main_kernel,
+        functools.partial(main_kernel, n_tiles, n_rows),
         out_shape=(
             jax.ShapeDtypeStruct((rows + 1, SLOTS, lanes), BF),
             jax.ShapeDtypeStruct((4, part, lanes), BF),
         ),
-        in_specs=[scalars] + [whole] * 6,
+        in_specs=[whole] * 11,
         out_specs=(whole, whole),
-        scratch_shapes=[pltpu.VMEM((3 * lanes, 3 * mids), BF)],
+        scratch_shapes=[
+            pltpu.VMEM((rows + 2, 2, SLOTS, lanes), BF),
+            pltpu.VMEM((rows + 6, SLOTS, lanes), BF),
+            pltpu.VMEM((3 * lanes, 3 * mids), BF),
+        ],
         compiler_params=limit,
-    )(
-        flags,
-        full_a.reshape(rows + 2, 2, SLOTS, lanes),
-        full_u,
-        wa,
-        own_w2,
-        other_w2,
-        shift_row,
-    )
+    )(picture, near, far, own_w2, other_w2, before, after, got, got_other, wa, shift_row)
     input_grad = pl.pallas_call(
         input_kernel,
         out_shape=jax.ShapeDtypeStruct((rows, 2, cols, lanes), BF),
@@ -453,11 +513,11 @@
             jax.ShapeDtypeStruct((9, channels, half), F32),
             jax.ShapeDtypeStruct((9, half, mids), F32),
         ),
-        in_specs=[scalars] + [whole] * 4,
+        in_specs=[whole] * 4,
         out_specs=(whole, whole),
         scratch_shapes=[pltpu.VMEM((4, part, lanes), BF)],
         compiler_params=limit,
-    )(quarter.reshape(1), *pieces)
+    )(*pieces)
     return (
         input_grad.reshape(height, pairs * lanes),
         first.reshape(3, 3, channels, half),

time: 39.1 us -> 37.8 us (0.967)
  Pallas kernels: 4.41 us -> 3.86 us
  other arithmetic: 0.72 us -> 0.18 us
  waiting for transfers between devices: 15.2 us -> 15.6 us
    ppermute x1, waiting for transfers between devices: 2.5 us -> 3.1 us  [summed_pair(): got = lax.ppermute(value, axis, swaps(size, distance))]
    pallas_call x2, Pallas kernels: 3.04 us -> 2.49 us  [the longest x1 1.38 us: shards(): pl.pallas_call(functools.partial(main_kernel, n_tiles, n_rows), out_shape...]
    concatenate x3 -> x1, other arithmetic: 0.52 us -> 0.01 us  [shards(): jnp.concatenate([edge_a.reshape(2 * cols, lanes), edge_u], axis=0)]
    ppermute x4, starting transfers between devices: 1.15 us -> 0.67 us  [core_swapped(): return lax.ppermute(value, 'chan', [(0, 1), (1, 0)])]
    ppermute x4, waiting for transfers between devices: 1.38 us -> 1.81 us  [core_swapped(): return lax.ppermute(value, 'chan', [(0, 1), (1, 0)])]
  transfers between devices with their start and end apart: 13 -> 13, of which waited for: 11 -> 11; matrix products, arithmetic and copies ran while one was open for 5% -> 3% of each run, Pallas kernels for 1% -> 1%
where the time goes in v4:
time: 37.8 us; the launch traced here: 37.6 us
  waiting for transfers between devices  15.6 us (41%)
  starting transfers between devices  15.4 us (41%)
  Pallas kernels  3.86 us (10%)
  between operations  1.51 us (4%)
  local copies, waits for them, and re-layouts  1.13 us (3%)
    ppermute x6, starting transfers between devices, from_block(): lax.ppermute(value, ('tiles', 'rows'), [(t * n_rows + r, (t ^ d >> 1) * n...  7.11 us
    ppermute x6, waiting for transfers between devices, from_block(): lax.ppermute(value, ('tiles', 'rows'), [(t * n_rows + r, (t ^ d >> 1) * n...  6.48 us
    ppermute x1, waiting for transfers between devices, summed_pair(): got = lax.ppermute(value, axis, swaps(size, distance))  3.1 us
    ppermute x1, starting transfers between devices, traded(): got = lax.ppermute(value, axis, swaps(size, 1))  2.9 us
    ppermute x1, starting transfers between devices, summed_pair(): got = lax.ppermute(value, axis, swaps(size, distance))  2.65 us
    ppermute x1, waiting for transfers between devices, traded(): got = lax.ppermute(value, axis, swaps(size, 1))  2.32 us
    ppermute x1, starting transfers between devices, traded(): got = lax.ppermute(value, ('tiles', 'rows', 'chan'), pairs)  2.04 us
    ppermute x1, waiting for transfers between devices, traded(): got = lax.ppermute(value, ('tiles', 'rows', 'chan'), pairs)  1.87 us
  transfers between devices with their start and end apart: 13, of which 11 were waited for; matrix products, arithmetic and copies ran while one was open for 3% of the time, Pallas kernels for 1%

profile of v4, /device:TPU:0, one launch (start us, length us, event | category | flops | bytes accessed | tf_op | source)
XLA Modules:
  0.0 37.6 jit_solution(15328902679583339068)
XLA Ops:
  1.3 1.1 %shard_map.94 = (bf16[12,48,128]{2,1,0:T(8,128)(2,1)S(1)}, bf16[1,144,128]{2,1,0:T(8,128)(2,1)S(1)}, bf16[576,128]{1,0:T(8,128)(2,1)S(1)}, bf16[384,256]{1,0:T(8,128)(2,1)S(1)}, f32[1,128]{1,0:T(1,128)S(1)}) custom-call(s32[8,128]{1,0:T(8,128)S(1)} %broadcast_in_dim.11.count_ref, s32[1,1,16]{2,1,0:T(1,128)} %order_hbm.1, bf16[12,48,64]{2,1,0:T(8,128)(2,1)} %cot_hbm.1, ...), custom_call_target="tpu_custom_call" | custom-call | tf_op jit(solution)/shard_map/pallas_call | solution.py:387
  2.5 0.5 %collective-permute-start.1 = (bf16[144,128]{1,0:T(8,128)(2,1)S(1)}, bf16[144,128]{1,0:T(8,128)(2,1)S(1)}, u32[]{:S(2)}, u32[]{:S(2)}) collective-permute-start(bf16[144,128]{1,0:T(8,128)(2,1)S(1)} %bitcast.46), channel_id=1, source_target_pairs={{0,1},{1,0},{2,3},{3,2},{4,5},{5,4},{6,7},{7,6},{8,9},{9,8},{10,11... | collective-permute-start | bytes 110600 | tf_op jit(solution)/shard_map/ppermute | solution.py:23
  3.0 0.1 collective-permute-start
  3.2 0.6 %collective-permute-done.1 = bf16[144,128]{1,0:T(8,128)(2,1)S(1)} collective-permute-done((bf16[144,128]{1,0:T(8,128)(2,1)S(1)}, bf16[144,128]{1,0:T(8,128)(2,1)S(1)}, u32[]{:S(2)}, u32[]{:S(2)}) %collective-permute-start.1) | collective-permute-done | bytes 36896 | tf_op jit(solution)/shard_map/ppermute | solution.py:23
  3.9 2.9 %collective-permute-start.2 = (bf16[240,128]{1,0:T(8,128)(2,1)S(1)}, bf16[240,128]{1,0:T(8,128)(2,1)S(1)}, u32[]{:S(2)}, u32[]{:S(2)}) collective-permute-start(bf16[240,128]{1,0:T(8,128)(2,1)S(1)} %pad_maximum_fusion), channel_id=1, source_target_pairs={{0,2},{2,0},{1,3},{3,1},{4,6},{6,4},{5,7},{7,5},{8,10},{10,8},{9,1... | collective-permute-start | bytes 184328 | tf_op jit(solution)/shard_map/ppermute | solution.py:59
  6.8 2.3 %collective-permute-done.2 = bf16[240,128]{1,0:T(8,128)(2,1)S(1)} collective-permute-done((bf16[240,128]{1,0:T(8,128)(2,1)S(1)}, bf16[240,128]{1,0:T(8,128)(2,1)S(1)}, u32[]{:S(2)}, u32[]{:S(2)}) %collective-permute-start.2) | collective-permute-done | bytes 61472 | tf_op jit(solution)/shard_map/ppermute | solution.py:59
  9.2 0.1 collective-permute-start.3
  9.3 0.0 collective-permute-done.far_ref
  9.4 0.2 concatenate.7
  9.5 2.0 %collective-permute-start.4 = (bf16[100,128]{1,0:T(8,128)(2,1)S(1)}, bf16[100,128]{1,0:T(8,128)(2,1)S(1)}, u32[]{:S(2)}, u32[]{:S(2)}) collective-permute-start(bf16[100,128]{1,0:T(8,128)(2,1)S(1)} %concatenate.7), channel_id=1, source_target_pairs={{0,4},{1,3},{2,6},{3,1},{4,0},{5,9},{6,2},{7,11},{8,12},{9,5},{10,... | collective-permute-start | bytes 76808 | tf_op jit(solution)/shard_map/ppermute | solution.py:62
  11.6 1.9 %collective-permute-done.4.got_ref = bf16[100,128]{1,0:T(8,128)(2,1)S(1)} collective-permute-done((bf16[100,128]{1,0:T(8,128)(2,1)S(1)}, bf16[100,128]{1,0:T(8,128)(2,1)S(1)}, u32[]{:S(2)}, u32[]{:S(2)}) %collective-permute-start.4) | collective-permute-done | bytes 25632 | tf_op jit(solution)/shard_map/ppermute | solution.py:62
  13.4 0.0 collective-permute-start.5
  13.4 1.2 %collective-permute-done.5.got_other_ref = bf16[100,128]{1,0:T(8,128)(2,1)S(1)} collective-permute-done((bf16[100,128]{1,0:T(8,128)(2,1)S(1)}, bf16[100,128]{1,0:T(8,128)(2,1)S(1)}, u32[]{:S(2)}, u32[]{:S(2)}) %collective-permute-start.5) | collective-permute-done | bytes 25632 | tf_op jit(solution)/shard_map/ppermute | solution.py:23
  14.6 0.0 collective-permute-done.3.other_w2_ref
  14.6 1.4 %shard_map.95 = (bf16[13,64,128]{2,1,0:T(8,128)(2,1)S(1)}, bf16[4,224,128]{2,1,0:T(8,128)(2,1)S(1)}) custom-call(bf16[24,48,128]{2,1,0:T(8,128)(2,1)S(1)} %bitcast.40, bf16[12,48,128]{2,1,0:T(8,128)(2,1)S(1)} %get-tuple-element.14.near_ref, bf16[12,48,128]{2,1,0:T(8,128)(2,1)S(1)} %collective-permute-done.far_ref, ...), custom_call_target="tpu_custom_call" | custom-call | tf_op jit(solution)/shard_map/pallas_call | solution.py:457
  16.1 2.0 %collective-permute-start.6 = (bf16[224,128]{1,0:T(8,128)(2,1)S(1)}, bf16[224,128]{1,0:T(8,128)(2,1)S(1)}, u32[]{:S(2)}, u32[]{:S(2)}) collective-permute-start(bf16[224,128]{1,0:T(8,128)(2,1)S(1)} %get-tuple-element.27), channel_id=1, source_target_pairs={{0,2},{2,0},{4,6},{6,4},{8,10},{10,8},{12,14},{14,12},{1,3},{3,1},... | collective-permute-start | bytes 172040 | tf_op jit(solution)/shard_map/ppermute | solution.py:482
  18.0 1.5 %collective-permute-start.8 = (bf16[224,128]{1,0:T(8,128)(2,1)S(1)}, bf16[224,128]{1,0:T(8,128)(2,1)S(1)}, u32[]{:S(2)}, u32[]{:S(2)}) collective-permute-start(bf16[224,128]{1,0:T(8,128)(2,1)S(1)} %get-tuple-element.28), channel_id=1, source_target_pairs={{0,6},{2,4},{4,2},{6,0},{8,14},{10,12},{12,10},{14,8},{1,7},{3,5},... | collective-permute-start | bytes 172040 | tf_op jit(solution)/shard_map/ppermute | solution.py:482
  19.6 0.1 collective-permute-start.7
  19.6 0.9 %collective-permute-done.6 = bf16[224,128]{1,0:T(8,128)(2,1)S(1)} collective-permute-done((bf16[224,128]{1,0:T(8,128)(2,1)S(1)}, bf16[224,128]{1,0:T(8,128)(2,1)S(1)}, u32[]{:S(2)}, u32[]{:S(2)}) %collective-permute-start.6) | collective-permute-done | bytes 57376 | tf_op jit(solution)/shard_map/ppermute | solution.py:482
  20.5 3.0 %collective-permute-done.8 = bf16[224,128]{1,0:T(8,128)(2,1)S(1)} collective-permute-done((bf16[224,128]{1,0:T(8,128)(2,1)S(1)}, bf16[224,128]{1,0:T(8,128)(2,1)S(1)}, u32[]{:S(2)}, u32[]{:S(2)}) %collective-permute-start.8) | collective-permute-done | bytes 57376 | tf_op jit(solution)/shard_map/ppermute | solution.py:482
  23.5 0.2 collective-permute-done.7
  23.8 2.7 %collective-permute-start.9 = (bf16[224,128]{1,0:T(8,128)(2,1)S(1)}, bf16[224,128]{1,0:T(8,128)(2,1)S(1)}, u32[]{:S(2)}, u32[]{:S(2)}) collective-permute-start(bf16[224,128]{1,0:T(8,128)(2,1)S(1)} %fusion.1), channel_id=1, source_target_pairs={{0,8},{4,12},{8,0},{12,4},{1,9},{5,13},{9,1},{13,5},{2,10},{6,14},... | collective-permute-start | bytes 172040 | tf_op jit(solution)/shard_map/ppermute | solution.py:368
  26.4 3.1 %collective-permute-done.9 = bf16[224,128]{1,0:T(8,128)(2,1)S(1)} collective-permute-done((bf16[224,128]{1,0:T(8,128)(2,1)S(1)}, bf16[224,128]{1,0:T(8,128)(2,1)S(1)}, u32[]{:S(2)}, u32[]{:S(2)}) %collective-permute-start.9) | collective-permute-done | bytes 57376 | tf_op jit(solution)/shard_map/ppermute | solution.py:368
  29.6 1.2 %collective-permute-start.12 = (bf16[224,128]{1,0:T(8,128)(2,1)S(1)}, bf16[224,128]{1,0:T(8,128)(2,1)S(1)}, u32[]{:S(2)}, u32[]{:S(2)}) collective-permute-start(bf16[224,128]{1,0:T(8,128)(2,1)S(1)} %add_convert_fusion.piece_0), channel_id=1, source_target_pairs={{0,6},{2,4},{4,2},{6,0},{8,14},{10,12},{12,10},{14,8},{1,7},{3,5},... | collective-permute-start | bytes 172040 | tf_op jit(solution)/shard_map/ppermute | solution.py:482
  30.8 1.8 %collective-permute-start.11 = (bf16[224,128]{1,0:T(8,128)(2,1)S(1)}, bf16[224,128]{1,0:T(8,128)(2,1)S(1)}, u32[]{:S(2)}, u32[]{:S(2)}) collective-permute-start(bf16[224,128]{1,0:T(8,128)(2,1)S(1)} %add_convert_fusion.piece_0), channel_id=1, source_target_pairs={{0,4},{2,6},{4,0},{6,2},{8,12},{10,14},{12,8},{14,10},{1,5},{3,7},... | collective-permute-start | bytes 172040 | tf_op jit(solution)/shard_map/ppermute | solution.py:482
  32.6 0.5 %collective-permute-start.10 = (bf16[224,128]{1,0:T(8,128)(2,1)S(1)}, bf16[224,128]{1,0:T(8,128)(2,1)S(1)}, u32[]{:S(2)}, u32[]{:S(2)}) collective-permute-start(bf16[224,128]{1,0:T(8,128)(2,1)S(1)} %add_convert_fusion.piece_0), channel_id=1, source_target_pairs={{0,2},{2,0},{4,6},{6,4},{8,10},{10,8},{12,14},{14,12},{1,3},{3,1},... | collective-permute-start | bytes 172040 | tf_op jit(solution)/shard_map/ppermute | solution.py:482
  33.1 0.5 %shard_map.96 = bf16[12,2,48,128]{3,2,1,0:T(8,128)(2,1)S(1)} custom-call(bf16[13,64,128]{2,1,0:T(8,128)(2,1)S(1)} %get-tuple-element.21.mid_ref, bf16[384,256]{1,0:T(8,128)(2,1)S(1)} %get-tuple-element.19.wa_ref), custom_call_target="tpu_custom_call" | custom-call | tf_op jit(solution)/shard_map/pallas_call | solution.py:472
  33.6 0.8 %copy.33 = bf16[3,8,48,128]{3,1,2,0:T(8,128)(2,1)} copy(bf16[3,8,48,128]{3,2,1,0:T(8,128)(2,1)S(1)} %bitcast.41) | data formatting | bytes 589824
  34.4 0.3 collective-permute-done.12.piece_3
  34.7 0.6 %collective-permute-done.11.piece_2 = bf16[224,128]{1,0:T(8,128)(2,1)S(1)} collective-permute-done((bf16[224,128]{1,0:T(8,128)(2,1)S(1)}, bf16[224,128]{1,0:T(8,128)(2,1)S(1)}, u32[]{:S(2)}, u32[]{:S(2)}) %collective-permute-start.11) | collective-permute-done | bytes 57376 | tf_op jit(solution)/shard_map/ppermute | solution.py:482
  35.3 1.4 %collective-permute-done.10.piece_1 = bf16[224,128]{1,0:T(8,128)(2,1)S(1)} collective-permute-done((bf16[224,128]{1,0:T(8,128)(2,1)S(1)}, bf16[224,128]{1,0:T(8,128)(2,1)S(1)}, u32[]{:S(2)}, u32[]{:S(2)}) %collective-permute-start.10) | collective-permute-done | bytes 57376 | tf_op jit(solution)/shard_map/ppermute | solution.py:482
  36.7 0.9 %shard_map.97 = (f32[9,64,64]{2,1,0:T(8,128)}, f32[9,64,128]{2,1,0:T(8,128)}) custom-call(bf16[224,128]{1,0:T(8,128)(2,1)S(1)} %add_convert_fusion.piece_0, bf16[224,128]{1,0:T(8,128)(2,1)S(1)} %collective-permute-done.10.piece_1, bf16[224,128]{1,0:T(8,128)(2,1)S(1)} %collective-permute-done.11.piece_2, bf16[224,128]{1,0:T(8,128)(2,1)S(1)} %collective-permute-done.12.piece_3), custom_call_target="tpu_custom_call" | custom-call | tf_op jit(solution)/shard_map/pallas_call | solution.py:510
  (24 shorter events, 0.4 us)
Async XLA Ops:
  0.6 2.4 %copy-start = (bf16[24,6144]{1,0:T(8,128)(2,1)S(1)}, bf16[24,6144]{1,0:T(8,128)(2,1)}, u32[]{:S(2)}) copy-start(bf16[24,6144]{1,0:T(8,128)(2,1)} %param.7) | copy-start | bytes 884740
  2.5 1.4 %collective-permute-start.1 = (bf16[144,128]{1,0:T(8,128)(2,1)S(1)}, bf16[144,128]{1,0:T(8,128)(2,1)S(1)}, u32[]{:S(2)}, u32[]{:S(2)}) collective-permute-start(bf16[144,128]{1,0:T(8,128)(2,1)S(1)} %bitcast.46), channel_id=1, source_target_pairs={{0,1},{1,0},{2,3},{3,2},{4,5},{5,4},{6,7},{7,6},{8,9},{9,8},{10,11... | collective-permute-start | bytes 110600 | tf_op jit(solution)/shard_map/ppermute | solution.py:23
  3.0 6.4 %collective-permute-start = (bf16[12,48,128]{2,1,0:T(8,128)(2,1)S(1)}, bf16[12,48,128]{2,1,0:T(8,128)(2,1)S(1)}, u32[]{:S(2)}, u32[]{:S(2)}) collective-permute-start(bf16[12,48,128]{2,1,0:T(8,128)(2,1)S(1)} %get-tuple-element.14.near_ref), channel_id=1, source_target_pairs={{0,1},{1,0},{2,3},{3,2},{4,5},{5,4},{6,7},{7,6},{8,9},{9,8},{10,11... | collective-permute-start | bytes 442376 | tf_op jit(solution)/shard_map/ppermute | solution.py:23
  3.9 5.2 %collective-permute-start.2 = (bf16[240,128]{1,0:T(8,128)(2,1)S(1)}, bf16[240,128]{1,0:T(8,128)(2,1)S(1)}, u32[]{:S(2)}, u32[]{:S(2)}) collective-permute-start(bf16[240,128]{1,0:T(8,128)(2,1)S(1)} %pad_maximum_fusion), channel_id=1, source_target_pairs={{0,2},{2,0},{1,3},{3,1},{4,6},{6,4},{5,7},{7,5},{8,10},{10,8},{9,1... | collective-permute-start | bytes 184328 | tf_op jit(solution)/shard_map/ppermute | solution.py:59
  9.2 5.4 %collective-permute-start.3 = (bf16[576,128]{1,0:T(8,128)(2,1)S(1)}, bf16[576,128]{1,0:T(8,128)(2,1)S(1)}, u32[]{:S(2)}, u32[]{:S(2)}) collective-permute-start(bf16[576,128]{1,0:T(8,128)(2,1)S(1)} %get-tuple-element.17.own_w2_ref), channel_id=1, source_target_pairs={{0,1},{1,0},{2,3},{3,2},{4,5},{5,4},{6,7},{7,6},{8,9},{9,8},{10,11... | collective-permute-start | bytes 442376 | tf_op jit(solution)/shard_map/ppermute | solution.py:23
  9.5 3.9 %collective-permute-start.4 = (bf16[100,128]{1,0:T(8,128)(2,1)S(1)}, bf16[100,128]{1,0:T(8,128)(2,1)S(1)}, u32[]{:S(2)}, u32[]{:S(2)}) collective-permute-start(bf16[100,128]{1,0:T(8,128)(2,1)S(1)} %concatenate.7), channel_id=1, source_target_pairs={{0,4},{1,3},{2,6},{3,1},{4,0},{5,9},{6,2},{7,11},{8,12},{9,5},{10,... | collective-permute-start | bytes 76808 | tf_op jit(solution)/shard_map/ppermute | solution.py:62
  13.4 1.2 %collective-permute-start.5 = (bf16[100,128]{1,0:T(8,128)(2,1)S(1)}, bf16[100,128]{1,0:T(8,128)(2,1)S(1)}, u32[]{:S(2)}, u32[]{:S(2)}) collective-permute-start(bf16[100,128]{1,0:T(8,128)(2,1)S(1)} %collective-permute-done.4.got_ref), channel_id=1, source_target_pairs={{0,1},{1,0},{2,3},{3,2},{4,5},{5,4},{6,7},{7,6},{8,9},{9,8},{10,11... | collective-permute-start | bytes 76808 | tf_op jit(solution)/shard_map/ppermute | solution.py:23
  16.1 4.4 %collective-permute-start.6 = (bf16[224,128]{1,0:T(8,128)(2,1)S(1)}, bf16[224,128]{1,0:T(8,128)(2,1)S(1)}, u32[]{:S(2)}, u32[]{:S(2)}) collective-permute-start(bf16[224,128]{1,0:T(8,128)(2,1)S(1)} %get-tuple-element.27), channel_id=1, source_target_pairs={{0,2},{2,0},{4,6},{6,4},{8,10},{10,8},{12,14},{14,12},{1,3},{3,1},... | collective-permute-start | bytes 172040 | tf_op jit(solution)/shard_map/ppermute | solution.py:482
  18.0 5.5 %collective-permute-start.8 = (bf16[224,128]{1,0:T(8,128)(2,1)S(1)}, bf16[224,128]{1,0:T(8,128)(2,1)S(1)}, u32[]{:S(2)}, u32[]{:S(2)}) collective-permute-start(bf16[224,128]{1,0:T(8,128)(2,1)S(1)} %get-tuple-element.28), channel_id=1, source_target_pairs={{0,6},{2,4},{4,2},{6,0},{8,14},{10,12},{12,10},{14,8},{1,7},{3,5},... | collective-permute-start | bytes 172040 | tf_op jit(solution)/shard_map/ppermute | solution.py:482
  19.6 4.2 %collective-permute-start.7 = (bf16[224,128]{1,0:T(8,128)(2,1)S(1)}, bf16[224,128]{1,0:T(8,128)(2,1)S(1)}, u32[]{:S(2)}, u32[]{:S(2)}) collective-permute-start(bf16[224,128]{1,0:T(8,128)(2,1)S(1)} %get-tuple-element.29), channel_id=1, source_target_pairs={{0,4},{2,6},{4,0},{6,2},{8,12},{10,14},{12,8},{14,10},{1,5},{3,7},... | collective-permute-start | bytes 172040 | tf_op jit(solution)/shard_map/ppermute | solution.py:482
  23.8 5.8 %collective-permute-start.9 = (bf16[224,128]{1,0:T(8,128)(2,1)S(1)}, bf16[224,128]{1,0:T(8,128)(2,1)S(1)}, u32[]{:S(2)}, u32[]{:S(2)}) collective-permute-start(bf16[224,128]{1,0:T(8,128)(2,1)S(1)} %fusion.1), channel_id=1, source_target_pairs={{0,8},{4,12},{8,0},{12,4},{1,9},{5,13},{9,1},{13,5},{2,10},{6,14},... | collective-permute-start | bytes 172040 | tf_op jit(solution)/shard_map/ppermute | solution.py:368
  29.6 5.1 %collective-permute-start.12 = (bf16[224,128]{1,0:T(8,128)(2,1)S(1)}, bf16[224,128]{1,0:T(8,128)(2,1)S(1)}, u32[]{:S(2)}, u32[]{:S(2)}) collective-permute-start(bf16[224,128]{1,0:T(8,128)(2,1)S(1)} %add_convert_fusion.piece_0), channel_id=1, source_target_pairs={{0,6},{2,4},{4,2},{6,0},{8,14},{10,12},{12,10},{14,8},{1,7},{3,5},... | collective-permute-start | bytes 172040 | tf_op jit(solution)/shard_map/ppermute | solution.py:482
  30.8 4.5 %collective-permute-start.11 = (bf16[224,128]{1,0:T(8,128)(2,1)S(1)}, bf16[224,128]{1,0:T(8,128)(2,1)S(1)}, u32[]{:S(2)}, u32[]{:S(2)}) collective-permute-start(bf16[224,128]{1,0:T(8,128)(2,1)S(1)} %add_convert_fusion.piece_0), channel_id=1, source_target_pairs={{0,4},{2,6},{4,0},{6,2},{8,12},{10,14},{12,8},{14,10},{1,5},{3,7},... | collective-permute-start | bytes 172040 | tf_op jit(solution)/shard_map/ppermute | solution.py:482
  32.6 4.2 %collective-permute-start.10 = (bf16[224,128]{1,0:T(8,128)(2,1)S(1)}, bf16[224,128]{1,0:T(8,128)(2,1)S(1)}, u32[]{:S(2)}, u32[]{:S(2)}) collective-permute-start(bf16[224,128]{1,0:T(8,128)(2,1)S(1)} %add_convert_fusion.piece_0), channel_id=1, source_target_pairs={{0,2},{2,0},{4,6},{6,4},{8,10},{10,8},{12,14},{14,12},{1,3},{3,1},... | collective-permute-start | bytes 172040 | tf_op jit(solution)/shard_map/ppermute | solution.py:482

commit v5 on v4

--- a/solution.py
+++ b/solution.py
@@ -77,7 +77,6 @@
 
 def prepare_kernel(
     n_rows,
-    count_ref,
     order_hbm,
     cot_hbm,
     w1_hbm,
@@ -85,6 +84,7 @@
     shift_hbm,
     near_ref,
     edge_ref,
+    place_ref,
     w2_ref,
     wa_ref,
     shift_ref,
@@ -113,20 +113,18 @@
     col_id = lax.broadcasted_iota(jnp.int32, (cols, 2 * half), 0)
     lane_id = lax.broadcasted_iota(jnp.int32, (cols, 2 * half), 1)
     mine = (lane_id < half) == (lax.axis_index("chan") == 0)
-    masks = []
     for a in range(rows // side):
         place = jnp.zeros((cols, 2 * half), jnp.int32)
         for b in range(across):
             inside = (col_id >= b * side) & (col_id < (b + 1) * side)
             place = jnp.where(inside, rank[a * across + b], place)
-        masks.append((place < count_ref[0:1, :]) & mine)
+        place_ref[a] = place
     copies[1].wait()
     lower = lax.axis_index("rows") % 2 == 0
     kept = []
     for i in range(rows):
         value = cot[i].astype(F32)
-        twice = jnp.concatenate([value, value], axis=1)
-        placed = jnp.where(masks[i // side], twice, 0.0)
+        placed = jnp.where(mine, jnp.concatenate([value, value], axis=1), 0.0)
         near_ref[i] = placed.astype(BF)
         kept.append(placed)
     for i in range(3):
@@ -384,17 +382,18 @@
     limit = pltpu.CompilerParams(vmem_limit_bytes=48 << 20)
     half = channels
     n_edges = 1 if n_rows == 2 else 2
-    near, edges, own_w2, wa, shift_row = pl.pallas_call(
+    near, edges, place, own_w2, wa, shift_row = pl.pallas_call(
         functools.partial(prepare_kernel, n_rows),
         out_shape=(
             jax.ShapeDtypeStruct((rows, cols, lanes), BF),
             jax.ShapeDtypeStruct((n_edges, 3 * cols, lanes), BF),
+            jax.ShapeDtypeStruct((tile_rows, cols, lanes), jnp.int32),
             jax.ShapeDtypeStruct((9 * half, mids), BF),
             jax.ShapeDtypeStruct((3 * lanes, 2 * mids), BF),
             jax.ShapeDtypeStruct((1, mids), F32),
         ),
-        in_specs=[whole] + [in_hbm] * 5,
-        out_specs=(whole,) * 5,
+        in_specs=[in_hbm] * 5,
+        out_specs=(whole,) * 6,
         scratch_shapes=[
             pltpu.VMEM((rows, cols, half), BF),
             pltpu.VMEM((3, 3, channels, mids), BF),
@@ -404,7 +403,6 @@
         ],
         compiler_params=limit,
     )(
-        jnp.broadcast_to(tissue_count, (8, lanes)),
         *(
             pltpu.with_memory_space_constraint(value, pltpu.HBM)
             for value in (
@@ -416,19 +414,23 @@
             )
         ),
     )
-    if n_rows == 2:
-        edge_u = edges[0] + core_swapped(edges[0])
-    else:
-        edges = edges + core_swapped(edges)
-        edge_u = jnp.where(sends_last("rows"), edges[1], edges[0])
+    other_edges = core_swapped(edges)
+    edges, tissue_count = lax.optimization_barrier((edges, tissue_count))
+    live = place < tissue_count[0, 0]
+    near = jnp.where(live[:, None], near.reshape(tile_rows, -1, cols, lanes), jnp.zeros((), BF))
+    near = near.reshape(rows, cols, lanes)
+    edges = (edges + other_edges).reshape(n_edges, 3, cols, lanes)
+    last = sends_last("rows")
+    edge_u = edges[0] if n_rows == 2 else jnp.where(last, edges[1], edges[0])
+    edge_u = jnp.where(jnp.where(last, live[-1], live[0]), edge_u, jnp.zeros((), BF))
+    edge_u = edge_u.reshape(3 * cols, lanes)
     picture = acts.reshape(height, pairs, lanes)
-    edge_a = jnp.where(sends_last("rows"), picture[height - 2 :], picture[:2])
+    edge_a = jnp.where(last, picture[height - 2 :], picture[:2])
+    strip = jnp.concatenate([edge_a.reshape(2 * cols, lanes), edge_u], axis=0)
+    strip, near = lax.optimization_barrier((strip, near))
     before, after = (
         value.reshape(5, cols, lanes)
-        for value in before_and_after(
-            *traded(jnp.concatenate([edge_a.reshape(2 * cols, lanes), edge_u], axis=0), "rows"),
-            "rows",
-        )
+        for value in before_and_after(*traded(strip, "rows"), "rows")
     )
     far = core_swapped(near)
     own_w2, before = lax.optimization_barrier((own_w2, before))

time: 37.8 us -> 37.1 us (0.981)
  waiting for transfers between devices: 15.6 us -> 15 us
    ppermute x4, waiting for transfers between devices: 1.81 us -> 1.2 us  [core_swapped(): return lax.ppermute(value, 'chan', [(0, 1), (1, 0)])]
  transfers between devices with their start and end apart: 13 -> 13, of which waited for: 11 -> 10; matrix products, arithmetic and copies ran while one was open for 3% -> 3% of each run, Pallas kernels for 1% -> 1%
where the time goes in v5:
time: 37.1 us; the launch traced here: 37 us
  starting transfers between devices  15.2 us (41%)
  waiting for transfers between devices  15 us (40%)
  Pallas kernels  3.9 us (11%)
  between operations  1.52 us (4%)
  local copies, waits for them, and re-layouts  1.13 us (3%)
    ppermute x6, starting transfers between devices, from_block(): lax.ppermute(value, ('tiles', 'rows'), [(t * n_rows + r, (t ^ d >> 1) * n...  7.11 us
    ppermute x6, waiting for transfers between devices, from_block(): lax.ppermute(value, ('tiles', 'rows'), [(t * n_rows + r, (t ^ d >> 1) * n...  6.41 us
    ppermute x1, waiting for transfers between devices, summed_pair(): got = lax.ppermute(value, axis, swaps(size, distance))  3.1 us
    ppermute x1, starting transfers between devices, traded(): got = lax.ppermute(value, axis, swaps(size, 1))  2.84 us
    ppermute x1, starting transfers between devices, summed_pair(): got = lax.ppermute(value, axis, swaps(size, distance))  2.65 us
    ppermute x1, waiting for transfers between devices, traded(): got = lax.ppermute(value, axis, swaps(size, 1))  2.38 us
    ppermute x1, starting transfers between devices, traded(): got = lax.ppermute(value, ('tiles', 'rows', 'chan'), pairs)  1.98 us
    ppermute x1, waiting for transfers between devices, traded(): got = lax.ppermute(value, ('tiles', 'rows', 'chan'), pairs)  1.93 us
  transfers between devices with their start and end apart: 13, of which 10 were waited for; matrix products, arithmetic and copies ran while one was open for 3% of the time, Pallas kernels for 1%

profile of v5, /device:TPU:0, one launch (start us, length us, event | category | flops | bytes accessed | tf_op | source)
XLA Modules:
  0.0 37.0 jit_solution(18223431634741733384)
XLA Ops:
  0.6 1.1 %shard_map.94 = (bf16[12,48,128]{2,1,0:T(8,128)(2,1)S(1)}, bf16[1,144,128]{2,1,0:T(8,128)(2,1)S(1)}, s32[2,48,128]{2,1,0:T(8,128)S(1)}, bf16[576,128]{1,0:T(8,12...) custom-call(s32[1,1,16]{2,1,0:T(1,128)} %order_hbm.1, bf16[12,48,64]{2,1,0:T(8,128)(2,1)} %cot_hbm.1, ...), custom_call_target="tpu_custom_call" | custom-call | tf_op jit(solution)/shard_map/pallas_call | solution.py:385
  1.8 0.5 %collective-permute-start = (bf16[1,144,128]{2,1,0:T(8,128)(2,1)S(1)}, bf16[1,144,128]{2,1,0:T(8,128)(2,1)S(1)}, u32[]{:S(2)}, u32[]{:S(2)}) collective-permute-start(bf16[1,144,128]{2,1,0:T(8,128)(2,1)S(1)} %get-tuple-element.22), channel_id=1, source_target_pairs={{0,1},{1,0},{2,3},{3,2},{4,5},{5,4},{6,7},{7,6},{8,9},{9,8},{10,11... | collective-permute-start | bytes 110600 | tf_op jit(solution)/shard_map/ppermute | solution.py:23
  3.2 0.0 collective-permute-done
  3.3 2.8 %collective-permute-start.2 = (bf16[240,128]{1,0:T(8,128)(2,1)S(1)}, bf16[240,128]{1,0:T(8,128)(2,1)S(1)}, u32[]{:S(2)}, u32[]{:S(2)}) collective-permute-start(bf16[240,128]{1,0:T(8,128)(2,1)S(1)} %pad_maximum_fusion), channel_id=1, source_target_pairs={{0,2},{2,0},{1,3},{3,1},{4,6},{6,4},{5,7},{7,5},{8,10},{10,8},{9,1... | collective-permute-start | bytes 184328 | tf_op jit(solution)/shard_map/ppermute | solution.py:59
  6.1 0.0 collective-permute-start.1
  6.1 2.4 %collective-permute-done.2 = bf16[240,128]{1,0:T(8,128)(2,1)S(1)} collective-permute-done((bf16[240,128]{1,0:T(8,128)(2,1)S(1)}, bf16[240,128]{1,0:T(8,128)(2,1)S(1)}, u32[]{:S(2)}, u32[]{:S(2)}) %collective-permute-start.2) | collective-permute-done | bytes 61472 | tf_op jit(solution)/shard_map/ppermute | solution.py:59
  8.6 0.1 collective-permute-start.3
  8.7 0.0 collective-permute-done.1.far_ref
  8.8 0.2 concatenate.7
  8.9 2.0 %collective-permute-start.4 = (bf16[100,128]{1,0:T(8,128)(2,1)S(1)}, bf16[100,128]{1,0:T(8,128)(2,1)S(1)}, u32[]{:S(2)}, u32[]{:S(2)}) collective-permute-start(bf16[100,128]{1,0:T(8,128)(2,1)S(1)} %concatenate.7), channel_id=1, source_target_pairs={{0,4},{1,3},{2,6},{3,1},{4,0},{5,9},{6,2},{7,11},{8,12},{9,5},{10,... | collective-permute-start | bytes 76808 | tf_op jit(solution)/shard_map/ppermute | solution.py:62
  10.9 1.9 %collective-permute-done.4.got_ref = bf16[100,128]{1,0:T(8,128)(2,1)S(1)} collective-permute-done((bf16[100,128]{1,0:T(8,128)(2,1)S(1)}, bf16[100,128]{1,0:T(8,128)(2,1)S(1)}, u32[]{:S(2)}, u32[]{:S(2)}) %collective-permute-start.4) | collective-permute-done | bytes 25632 | tf_op jit(solution)/shard_map/ppermute | solution.py:62
  12.8 0.0 collective-permute-start.5
  12.8 1.2 %collective-permute-done.5.got_other_ref = bf16[100,128]{1,0:T(8,128)(2,1)S(1)} collective-permute-done((bf16[100,128]{1,0:T(8,128)(2,1)S(1)}, bf16[100,128]{1,0:T(8,128)(2,1)S(1)}, u32[]{:S(2)}, u32[]{:S(2)}) %collective-permute-start.5) | collective-permute-done | bytes 25632 | tf_op jit(solution)/shard_map/ppermute | solution.py:23
  14.0 0.0 collective-permute-done.3.other_w2_ref
  14.0 1.4 %shard_map.95 = (bf16[13,64,128]{2,1,0:T(8,128)(2,1)S(1)}, bf16[4,224,128]{2,1,0:T(8,128)(2,1)S(1)}) custom-call(bf16[24,48,128]{2,1,0:T(8,128)(2,1)S(1)} %bitcast.46, bf16[12,48,128]{2,1,0:T(8,128)(2,1)S(1)} %bitcast_select_fusion.near_ref, bf16[12,48,128]{2,1,0:T(8,128)(2,1)S(1)} %collective-permute-done.1.far_ref, ...), custom_call_target="tpu_custom_call" | custom-call | tf_op jit(solution)/shard_map/pallas_call | solution.py:459
  15.5 1.9 %collective-permute-start.6 = (bf16[224,128]{1,0:T(8,128)(2,1)S(1)}, bf16[224,128]{1,0:T(8,128)(2,1)S(1)}, u32[]{:S(2)}, u32[]{:S(2)}) collective-permute-start(bf16[224,128]{1,0:T(8,128)(2,1)S(1)} %get-tuple-element.37), channel_id=1, source_target_pairs={{0,2},{2,0},{4,6},{6,4},{8,10},{10,8},{12,14},{14,12},{1,3},{3,1},... | collective-permute-start | bytes 172040 | tf_op jit(solution)/shard_map/ppermute | solution.py:484
  17.3 1.5 %collective-permute-start.8 = (bf16[224,128]{1,0:T(8,128)(2,1)S(1)}, bf16[224,128]{1,0:T(8,128)(2,1)S(1)}, u32[]{:S(2)}, u32[]{:S(2)}) collective-permute-start(bf16[224,128]{1,0:T(8,128)(2,1)S(1)} %get-tuple-element.38), channel_id=1, source_target_pairs={{0,6},{2,4},{4,2},{6,0},{8,14},{10,12},{12,10},{14,8},{1,7},{3,5},... | collective-permute-start | bytes 172040 | tf_op jit(solution)/shard_map/ppermute | solution.py:484
  18.9 0.1 collective-permute-start.7
  19.0 0.7 %collective-permute-done.6 = bf16[224,128]{1,0:T(8,128)(2,1)S(1)} collective-permute-done((bf16[224,128]{1,0:T(8,128)(2,1)S(1)}, bf16[224,128]{1,0:T(8,128)(2,1)S(1)}, u32[]{:S(2)}, u32[]{:S(2)}) %collective-permute-start.6) | collective-permute-done | bytes 57376 | tf_op jit(solution)/shard_map/ppermute | solution.py:484
  19.7 3.1 %collective-permute-done.8 = bf16[224,128]{1,0:T(8,128)(2,1)S(1)} collective-permute-done((bf16[224,128]{1,0:T(8,128)(2,1)S(1)}, bf16[224,128]{1,0:T(8,128)(2,1)S(1)}, u32[]{:S(2)}, u32[]{:S(2)}) %collective-permute-start.8) | collective-permute-done | bytes 57376 | tf_op jit(solution)/shard_map/ppermute | solution.py:484
  22.8 0.2 collective-permute-done.7
  23.1 2.7 %collective-permute-start.9 = (bf16[224,128]{1,0:T(8,128)(2,1)S(1)}, bf16[224,128]{1,0:T(8,128)(2,1)S(1)}, u32[]{:S(2)}, u32[]{:S(2)}) collective-permute-start(bf16[224,128]{1,0:T(8,128)(2,1)S(1)} %fusion.1), channel_id=1, source_target_pairs={{0,8},{4,12},{8,0},{12,4},{1,9},{5,13},{9,1},{13,5},{2,10},{6,14},... | collective-permute-start | bytes 172040 | tf_op jit(solution)/shard_map/ppermute | solution.py:366
  25.8 3.1 %collective-permute-done.9 = bf16[224,128]{1,0:T(8,128)(2,1)S(1)} collective-permute-done((bf16[224,128]{1,0:T(8,128)(2,1)S(1)}, bf16[224,128]{1,0:T(8,128)(2,1)S(1)}, u32[]{:S(2)}, u32[]{:S(2)}) %collective-permute-start.9) | collective-permute-done | bytes 57376 | tf_op jit(solution)/shard_map/ppermute | solution.py:366
  28.9 1.2 %collective-permute-start.12 = (bf16[224,128]{1,0:T(8,128)(2,1)S(1)}, bf16[224,128]{1,0:T(8,128)(2,1)S(1)}, u32[]{:S(2)}, u32[]{:S(2)}) collective-permute-start(bf16[224,128]{1,0:T(8,128)(2,1)S(1)} %add_convert_fusion.piece_0), channel_id=1, source_target_pairs={{0,6},{2,4},{4,2},{6,0},{8,14},{10,12},{12,10},{14,8},{1,7},{3,5},... | collective-permute-start | bytes 172040 | tf_op jit(solution)/shard_map/ppermute | solution.py:484
  30.1 1.8 %collective-permute-start.11 = (bf16[224,128]{1,0:T(8,128)(2,1)S(1)}, bf16[224,128]{1,0:T(8,128)(2,1)S(1)}, u32[]{:S(2)}, u32[]{:S(2)}) collective-permute-start(bf16[224,128]{1,0:T(8,128)(2,1)S(1)} %add_convert_fusion.piece_0), channel_id=1, source_target_pairs={{0,4},{2,6},{4,0},{6,2},{8,12},{10,14},{12,8},{14,10},{1,5},{3,7},... | collective-permute-start | bytes 172040 | tf_op jit(solution)/shard_map/ppermute | solution.py:484
  31.9 0.5 %collective-permute-start.10 = (bf16[224,128]{1,0:T(8,128)(2,1)S(1)}, bf16[224,128]{1,0:T(8,128)(2,1)S(1)}, u32[]{:S(2)}, u32[]{:S(2)}) collective-permute-start(bf16[224,128]{1,0:T(8,128)(2,1)S(1)} %add_convert_fusion.piece_0), channel_id=1, source_target_pairs={{0,2},{2,0},{4,6},{6,4},{8,10},{10,8},{12,14},{14,12},{1,3},{3,1},... | collective-permute-start | bytes 172040 | tf_op jit(solution)/shard_map/ppermute | solution.py:484
  32.4 0.5 %shard_map.96 = bf16[12,2,48,128]{3,2,1,0:T(8,128)(2,1)S(1)} custom-call(bf16[13,64,128]{2,1,0:T(8,128)(2,1)S(1)} %get-tuple-element.31.mid_ref, bf16[384,256]{1,0:T(8,128)(2,1)S(1)} %get-tuple-element.29.wa_ref), custom_call_target="tpu_custom_call" | custom-call | tf_op jit(solution)/shard_map/pallas_call | solution.py:474
  33.0 0.8 %copy.33 = bf16[3,8,48,128]{3,1,2,0:T(8,128)(2,1)} copy(bf16[3,8,48,128]{3,2,1,0:T(8,128)(2,1)S(1)} %bitcast.47) | data formatting | bytes 589824
  33.7 0.3 collective-permute-done.12.piece_3
  34.0 0.6 %collective-permute-done.11.piece_2 = bf16[224,128]{1,0:T(8,128)(2,1)S(1)} collective-permute-done((bf16[224,128]{1,0:T(8,128)(2,1)S(1)}, bf16[224,128]{1,0:T(8,128)(2,1)S(1)}, u32[]{:S(2)}, u32[]{:S(2)}) %collective-permute-start.11) | collective-permute-done | bytes 57376 | tf_op jit(solution)/shard_map/ppermute | solution.py:484
  34.7 1.4 %collective-permute-done.10.piece_1 = bf16[224,128]{1,0:T(8,128)(2,1)S(1)} collective-permute-done((bf16[224,128]{1,0:T(8,128)(2,1)S(1)}, bf16[224,128]{1,0:T(8,128)(2,1)S(1)}, u32[]{:S(2)}, u32[]{:S(2)}) %collective-permute-start.10) | collective-permute-done | bytes 57376 | tf_op jit(solution)/shard_map/ppermute | solution.py:484
  36.1 0.9 %shard_map.97 = (f32[9,64,64]{2,1,0:T(8,128)}, f32[9,64,128]{2,1,0:T(8,128)}) custom-call(bf16[224,128]{1,0:T(8,128)(2,1)S(1)} %add_convert_fusion.piece_0, bf16[224,128]{1,0:T(8,128)(2,1)S(1)} %collective-permute-done.10.piece_1, bf16[224,128]{1,0:T(8,128)(2,1)S(1)} %collective-permute-done.11.piece_2, bf16[224,128]{1,0:T(8,128)(2,1)S(1)} %collective-permute-done.12.piece_3), custom_call_target="tpu_custom_call" | custom-call | tf_op jit(solution)/shard_map/pallas_call | solution.py:512
  (26 shorter events, 0.4 us)
Async XLA Ops:
  0.6 2.3 %copy-start = (bf16[24,6144]{1,0:T(8,128)(2,1)S(1)}, bf16[24,6144]{1,0:T(8,128)(2,1)}, u32[]{:S(2)}) copy-start(bf16[24,6144]{1,0:T(8,128)(2,1)} %param.7) | copy-start | bytes 884740
  1.8 1.4 %collective-permute-start = (bf16[1,144,128]{2,1,0:T(8,128)(2,1)S(1)}, bf16[1,144,128]{2,1,0:T(8,128)(2,1)S(1)}, u32[]{:S(2)}, u32[]{:S(2)}) collective-permute-start(bf16[1,144,128]{2,1,0:T(8,128)(2,1)S(1)} %get-tuple-element.22), channel_id=1, source_target_pairs={{0,1},{1,0},{2,3},{3,2},{4,5},{5,4},{6,7},{7,6},{8,9},{9,8},{10,11... | collective-permute-start | bytes 110600 | tf_op jit(solution)/shard_map/ppermute | solution.py:23
  3.3 5.2 %collective-permute-start.2 = (bf16[240,128]{1,0:T(8,128)(2,1)S(1)}, bf16[240,128]{1,0:T(8,128)(2,1)S(1)}, u32[]{:S(2)}, u32[]{:S(2)}) collective-permute-start(bf16[240,128]{1,0:T(8,128)(2,1)S(1)} %pad_maximum_fusion), channel_id=1, source_target_pairs={{0,2},{2,0},{1,3},{3,1},{4,6},{6,4},{5,7},{7,5},{8,10},{10,8},{9,1... | collective-permute-start | bytes 184328 | tf_op jit(solution)/shard_map/ppermute | solution.py:59
  6.1 2.6 %collective-permute-start.1 = (bf16[12,48,128]{2,1,0:T(8,128)(2,1)S(1)}, bf16[12,48,128]{2,1,0:T(8,128)(2,1)S(1)}, u32[]{:S(2)}, u32[]{:S(2)}) collective-permute-start(bf16[12,48,128]{2,1,0:T(8,128)(2,1)S(1)} %bitcast_select_fusion.near_ref), channel_id=1, source_target_pairs={{0,1},{1,0},{2,3},{3,2},{4,5},{5,4},{6,7},{7,6},{8,9},{9,8},{10,11... | collective-permute-start | bytes 442376 | tf_op jit(solution)/shard_map/ppermute | solution.py:23
  8.6 5.4 %collective-permute-start.3 = (bf16[576,128]{1,0:T(8,128)(2,1)S(1)}, bf16[576,128]{1,0:T(8,128)(2,1)S(1)}, u32[]{:S(2)}, u32[]{:S(2)}) collective-permute-start(bf16[576,128]{1,0:T(8,128)(2,1)S(1)} %get-tuple-element.27.own_w2_ref), channel_id=1, source_target_pairs={{0,1},{1,0},{2,3},{3,2},{4,5},{5,4},{6,7},{7,6},{8,9},{9,8},{10,11... | collective-permute-start | bytes 442376 | tf_op jit(solution)/shard_map/ppermute | solution.py:23
  8.9 3.9 %collective-permute-start.4 = (bf16[100,128]{1,0:T(8,128)(2,1)S(1)}, bf16[100,128]{1,0:T(8,128)(2,1)S(1)}, u32[]{:S(2)}, u32[]{:S(2)}) collective-permute-start(bf16[100,128]{1,0:T(8,128)(2,1)S(1)} %concatenate.7), channel_id=1, source_target_pairs={{0,4},{1,3},{2,6},{3,1},{4,0},{5,9},{6,2},{7,11},{8,12},{9,5},{10,... | collective-permute-start | bytes 76808 | tf_op jit(solution)/shard_map/ppermute | solution.py:62
  12.8 1.2 %collective-permute-start.5 = (bf16[100,128]{1,0:T(8,128)(2,1)S(1)}, bf16[100,128]{1,0:T(8,128)(2,1)S(1)}, u32[]{:S(2)}, u32[]{:S(2)}) collective-permute-start(bf16[100,128]{1,0:T(8,128)(2,1)S(1)} %collective-permute-done.4.got_ref), channel_id=1, source_target_pairs={{0,1},{1,0},{2,3},{3,2},{4,5},{5,4},{6,7},{7,6},{8,9},{9,8},{10,11... | collective-permute-start | bytes 76808 | tf_op jit(solution)/shard_map/ppermute | solution.py:23
  15.5 4.2 %collective-permute-start.6 = (bf16[224,128]{1,0:T(8,128)(2,1)S(1)}, bf16[224,128]{1,0:T(8,128)(2,1)S(1)}, u32[]{:S(2)}, u32[]{:S(2)}) collective-permute-start(bf16[224,128]{1,0:T(8,128)(2,1)S(1)} %get-tuple-element.37), channel_id=1, source_target_pairs={{0,2},{2,0},{4,6},{6,4},{8,10},{10,8},{12,14},{14,12},{1,3},{3,1},... | collective-permute-start | bytes 172040 | tf_op jit(solution)/shard_map/ppermute | solution.py:484
  17.3 5.5 %collective-permute-start.8 = (bf16[224,128]{1,0:T(8,128)(2,1)S(1)}, bf16[224,128]{1,0:T(8,128)(2,1)S(1)}, u32[]{:S(2)}, u32[]{:S(2)}) collective-permute-start(bf16[224,128]{1,0:T(8,128)(2,1)S(1)} %get-tuple-element.38), channel_id=1, source_target_pairs={{0,6},{2,4},{4,2},{6,0},{8,14},{10,12},{12,10},{14,8},{1,7},{3,5},... | collective-permute-start | bytes 172040 | tf_op jit(solution)/shard_map/ppermute | solution.py:484
  18.9 4.2 %collective-permute-start.7 = (bf16[224,128]{1,0:T(8,128)(2,1)S(1)}, bf16[224,128]{1,0:T(8,128)(2,1)S(1)}, u32[]{:S(2)}, u32[]{:S(2)}) collective-permute-start(bf16[224,128]{1,0:T(8,128)(2,1)S(1)} %get-tuple-element.39), channel_id=1, source_target_pairs={{0,4},{2,6},{4,0},{6,2},{8,12},{10,14},{12,8},{14,10},{1,5},{3,7},... | collective-permute-start | bytes 172040 | tf_op jit(solution)/shard_map/ppermute | solution.py:484
  23.1 5.8 %collective-permute-start.9 = (bf16[224,128]{1,0:T(8,128)(2,1)S(1)}, bf16[224,128]{1,0:T(8,128)(2,1)S(1)}, u32[]{:S(2)}, u32[]{:S(2)}) collective-permute-start(bf16[224,128]{1,0:T(8,128)(2,1)S(1)} %fusion.1), channel_id=1, source_target_pairs={{0,8},{4,12},{8,0},{12,4},{1,9},{5,13},{9,1},{13,5},{2,10},{6,14},... | collective-permute-start | bytes 172040 | tf_op jit(solution)/shard_map/ppermute | solution.py:366
  28.9 5.1 %collective-permute-start.12 = (bf16[224,128]{1,0:T(8,128)(2,1)S(1)}, bf16[224,128]{1,0:T(8,128)(2,1)S(1)}, u32[]{:S(2)}, u32[]{:S(2)}) collective-permute-start(bf16[224,128]{1,0:T(8,128)(2,1)S(1)} %add_convert_fusion.piece_0), channel_id=1, source_target_pairs={{0,6},{2,4},{4,2},{6,0},{8,14},{10,12},{12,10},{14,8},{1,7},{3,5},... | collective-permute-start | bytes 172040 | tf_op jit(solution)/shard_map/ppermute | solution.py:484
  30.1 4.5 %collective-permute-start.11 = (bf16[224,128]{1,0:T(8,128)(2,1)S(1)}, bf16[224,128]{1,0:T(8,128)(2,1)S(1)}, u32[]{:S(2)}, u32[]{:S(2)}) collective-permute-start(bf16[224,128]{1,0:T(8,128)(2,1)S(1)} %add_convert_fusion.piece_0), channel_id=1, source_target_pairs={{0,4},{2,6},{4,0},{6,2},{8,12},{10,14},{12,8},{14,10},{1,5},{3,7},... | collective-permute-start | bytes 172040 | tf_op jit(solution)/shard_map/ppermute | solution.py:484
  31.9 4.2 %collective-permute-start.10 = (bf16[224,128]{1,0:T(8,128)(2,1)S(1)}, bf16[224,128]{1,0:T(8,128)(2,1)S(1)}, u32[]{:S(2)}, u32[]{:S(2)}) collective-permute-start(bf16[224,128]{1,0:T(8,128)(2,1)S(1)} %add_convert_fusion.piece_0), channel_id=1, source_target_pairs={{0,2},{2,0},{4,6},{6,4},{8,10},{10,8},{12,14},{14,12},{1,3},{3,1},... | collective-permute-start | bytes 172040 | tf_op jit(solution)/shard_map/ppermute | solution.py:484

commit v6 on v5

--- a/solution.py
+++ b/solution.py
@@ -480,18 +480,18 @@
     )(mid_grad, wa)
 
     def from_block(values):
-        return [
-            lax.ppermute(
-                value,
-                ("tiles", "rows"),
-                [
-                    (t * n_rows + r, (t ^ (d >> 1)) * n_rows + (r ^ (d & 1)))
-                    for t in range(n_tiles)
-                    for r in range(n_rows)
-                ],
-            )
-            for d, value in enumerate(values, 1)
-        ]
+        got = {}
+        for d in (1, 2, 3):
+            value = values[d - 1]
+            for other in got.values():
+                value, _ = lax.optimization_barrier((value, other[0]))
+            pairs = [
+                (t * n_rows + r, (t ^ (d >> 1)) * n_rows + (r ^ (d & 1)))
+                for t in range(n_tiles)
+                for r in range(n_rows)
+            ]
+            got[d] = (value, lax.ppermute(value, ("tiles", "rows"), pairs))
+        return [got[d][1] for d in (1, 2, 3)]
 
     one, two, three = from_block([weights[1], weights[2], weights[3]])
     total = (

time: 37.1 us -> 35.4 us (0.954)
  waiting for transfers between devices: 15 us -> 13.3 us
    ppermute x6, waiting for transfers between devices: 6.41 us -> 5.31 us  [from_block(): got[d] = (value, lax.ppermute(value, ('tiles', 'rows'), pairs))]
    ppermute x1, waiting for transfers between devices: 3.1 us -> 2.49 us  [summed_pair(): got = lax.ppermute(value, axis, swaps(size, distance))]
  transfers between devices with their start and end apart: 13 -> 13, of which waited for: 10 -> 10; matrix products, arithmetic and copies ran while one was open for 3% -> 4% of each run, Pallas kernels for 1% -> 1%
where the time goes in v6:
time: 35.4 us; the launch traced here: 35.3 us
  starting transfers between devices  15.2 us (43%)
  waiting for transfers between devices  13.3 us (38%)
  Pallas kernels  3.9 us (11%)
  between operations  1.52 us (4%)
  local copies, waits for them, and re-layouts  1.13 us (3%)
    ppermute x6, starting transfers between devices, from_block(): got[d] = (value, lax.ppermute(value, ('tiles', 'rows'), pairs))  7.11 us
    ppermute x6, waiting for transfers between devices, from_block(): got[d] = (value, lax.ppermute(value, ('tiles', 'rows'), pairs))  5.31 us
    ppermute x1, starting transfers between devices, traded(): got = lax.ppermute(value, axis, swaps(size, 1))  2.84 us
    ppermute x1, starting transfers between devices, summed_pair(): got = lax.ppermute(value, axis, swaps(size, distance))  2.65 us
    ppermute x1, waiting for transfers between devices, summed_pair(): got = lax.ppermute(value, axis, swaps(size, distance))  2.49 us
    ppermute x1, waiting for transfers between devices, traded(): got = lax.ppermute(value, axis, swaps(size, 1))  2.38 us
    ppermute x1, starting transfers between devices, traded(): got = lax.ppermute(value, ('tiles', 'rows', 'chan'), pairs)  1.98 us
    ppermute x1, waiting for transfers between devices, traded(): got = lax.ppermute(value, ('tiles', 'rows', 'chan'), pairs)  1.93 us
  transfers between devices with their start and end apart: 13, of which 10 were waited for; matrix products, arithmetic and copies ran while one was open for 4% of the time, Pallas kernels for 1%

profile of v6, /device:TPU:0, one launch (start us, length us, event | category | flops | bytes accessed | tf_op | source)
XLA Modules:
  0.0 35.3 jit_solution(4272593860524497763)
XLA Ops:
  0.6 1.1 %shard_map.94 = (bf16[12,48,128]{2,1,0:T(8,128)(2,1)S(1)}, bf16[1,144,128]{2,1,0:T(8,128)(2,1)S(1)}, s32[2,48,128]{2,1,0:T(8,128)S(1)}, bf16[576,128]{1,0:T(8,12...) custom-call(s32[1,1,16]{2,1,0:T(1,128)} %order_hbm.1, bf16[12,48,64]{2,1,0:T(8,128)(2,1)} %cot_hbm.1, ...), custom_call_target="tpu_custom_call" | custom-call | tf_op jit(solution)/shard_map/pallas_call | solution.py:385
  1.8 0.5 %collective-permute-start = (bf16[1,144,128]{2,1,0:T(8,128)(2,1)S(1)}, bf16[1,144,128]{2,1,0:T(8,128)(2,1)S(1)}, u32[]{:S(2)}, u32[]{:S(2)}) collective-permute-start(bf16[1,144,128]{2,1,0:T(8,128)(2,1)S(1)} %get-tuple-element.27), channel_id=1, source_target_pairs={{0,1},{1,0},{2,3},{3,2},{4,5},{5,4},{6,7},{7,6},{8,9},{9,8},{10,11... | collective-permute-start | bytes 110600 | tf_op jit(solution)/shard_map/ppermute | solution.py:23
  3.2 0.0 collective-permute-done
  3.3 2.8 %collective-permute-start.2 = (bf16[240,128]{1,0:T(8,128)(2,1)S(1)}, bf16[240,128]{1,0:T(8,128)(2,1)S(1)}, u32[]{:S(2)}, u32[]{:S(2)}) collective-permute-start(bf16[240,128]{1,0:T(8,128)(2,1)S(1)} %pad_maximum_fusion), channel_id=1, source_target_pairs={{0,2},{2,0},{1,3},{3,1},{4,6},{6,4},{5,7},{7,5},{8,10},{10,8},{9,1... | collective-permute-start | bytes 184328 | tf_op jit(solution)/shard_map/ppermute | solution.py:59
  6.1 0.0 collective-permute-start.1
  6.1 2.4 %collective-permute-done.2 = bf16[240,128]{1,0:T(8,128)(2,1)S(1)} collective-permute-done((bf16[240,128]{1,0:T(8,128)(2,1)S(1)}, bf16[240,128]{1,0:T(8,128)(2,1)S(1)}, u32[]{:S(2)}, u32[]{:S(2)}) %collective-permute-start.2) | collective-permute-done | bytes 61472 | tf_op jit(solution)/shard_map/ppermute | solution.py:59
  8.6 0.1 collective-permute-start.3
  8.7 0.0 collective-permute-done.1.far_ref
  8.8 0.2 concatenate.7
  8.9 2.0 %collective-permute-start.4 = (bf16[100,128]{1,0:T(8,128)(2,1)S(1)}, bf16[100,128]{1,0:T(8,128)(2,1)S(1)}, u32[]{:S(2)}, u32[]{:S(2)}) collective-permute-start(bf16[100,128]{1,0:T(8,128)(2,1)S(1)} %concatenate.7), channel_id=1, source_target_pairs={{0,4},{1,3},{2,6},{3,1},{4,0},{5,9},{6,2},{7,11},{8,12},{9,5},{10,... | collective-permute-start | bytes 76808 | tf_op jit(solution)/shard_map/ppermute | solution.py:62
  10.9 1.9 %collective-permute-done.4.got_ref = bf16[100,128]{1,0:T(8,128)(2,1)S(1)} collective-permute-done((bf16[100,128]{1,0:T(8,128)(2,1)S(1)}, bf16[100,128]{1,0:T(8,128)(2,1)S(1)}, u32[]{:S(2)}, u32[]{:S(2)}) %collective-permute-start.4) | collective-permute-done | bytes 25632 | tf_op jit(solution)/shard_map/ppermute | solution.py:62
  12.8 0.0 collective-permute-start.5
  12.8 1.2 %collective-permute-done.5.got_other_ref = bf16[100,128]{1,0:T(8,128)(2,1)S(1)} collective-permute-done((bf16[100,128]{1,0:T(8,128)(2,1)S(1)}, bf16[100,128]{1,0:T(8,128)(2,1)S(1)}, u32[]{:S(2)}, u32[]{:S(2)}) %collective-permute-start.5) | collective-permute-done | bytes 25632 | tf_op jit(solution)/shard_map/ppermute | solution.py:23
  14.0 0.0 collective-permute-done.3.other_w2_ref
  14.0 1.4 %shard_map.95 = (bf16[13,64,128]{2,1,0:T(8,128)(2,1)S(1)}, bf16[4,224,128]{2,1,0:T(8,128)(2,1)S(1)}) custom-call(bf16[24,48,128]{2,1,0:T(8,128)(2,1)S(1)} %bitcast.46, bf16[12,48,128]{2,1,0:T(8,128)(2,1)S(1)} %bitcast_select_fusion.near_ref, bf16[12,48,128]{2,1,0:T(8,128)(2,1)S(1)} %collective-permute-done.1.far_ref, ...), custom_call_target="tpu_custom_call" | custom-call | tf_op jit(solution)/shard_map/pallas_call | solution.py:459
  15.5 2.9 %collective-permute-start.8 = (bf16[224,128]{1,0:T(8,128)(2,1)S(1)}, bf16[224,128]{1,0:T(8,128)(2,1)S(1)}, u32[]{:S(2)}, u32[]{:S(2)}) collective-permute-start(bf16[224,128]{1,0:T(8,128)(2,1)S(1)} %get-tuple-element.40), channel_id=1, source_target_pairs={{0,6},{2,4},{4,2},{6,0},{8,14},{10,12},{12,10},{14,8},{1,7},{3,5},... | collective-permute-start | bytes 172040 | tf_op jit(solution)/shard_map/ppermute | solution.py:493
  18.4 0.4 %collective-permute-start.7 = (bf16[224,128]{1,0:T(8,128)(2,1)S(1)}, bf16[224,128]{1,0:T(8,128)(2,1)S(1)}, u32[]{:S(2)}, u32[]{:S(2)}) collective-permute-start(bf16[224,128]{1,0:T(8,128)(2,1)S(1)} %get-tuple-element.38), channel_id=1, source_target_pairs={{0,4},{2,6},{4,0},{6,2},{8,12},{10,14},{12,8},{14,10},{1,5},{3,7},... | collective-permute-start | bytes 172040 | tf_op jit(solution)/shard_map/ppermute | solution.py:493
  18.8 0.2 collective-permute-start.6
  19.0 1.6 %collective-permute-done.8 = bf16[224,128]{1,0:T(8,128)(2,1)S(1)} collective-permute-done((bf16[224,128]{1,0:T(8,128)(2,1)S(1)}, bf16[224,128]{1,0:T(8,128)(2,1)S(1)}, u32[]{:S(2)}, u32[]{:S(2)}) %collective-permute-start.8) | collective-permute-done | bytes 57376 | tf_op jit(solution)/shard_map/ppermute | solution.py:493
  20.6 1.9 %collective-permute-done.7 = bf16[224,128]{1,0:T(8,128)(2,1)S(1)} collective-permute-done((bf16[224,128]{1,0:T(8,128)(2,1)S(1)}, bf16[224,128]{1,0:T(8,128)(2,1)S(1)}, u32[]{:S(2)}, u32[]{:S(2)}) %collective-permute-start.7) | collective-permute-done | bytes 57376 | tf_op jit(solution)/shard_map/ppermute | solution.py:493
  22.5 0.4 %collective-permute-done.6 = bf16[224,128]{1,0:T(8,128)(2,1)S(1)} collective-permute-done((bf16[224,128]{1,0:T(8,128)(2,1)S(1)}, bf16[224,128]{1,0:T(8,128)(2,1)S(1)}, u32[]{:S(2)}, u32[]{:S(2)}) %collective-permute-start.6) | collective-permute-done | bytes 57376 | tf_op jit(solution)/shard_map/ppermute | solution.py:493
  23.0 2.7 %collective-permute-start.9 = (bf16[224,128]{1,0:T(8,128)(2,1)S(1)}, bf16[224,128]{1,0:T(8,128)(2,1)S(1)}, u32[]{:S(2)}, u32[]{:S(2)}) collective-permute-start(bf16[224,128]{1,0:T(8,128)(2,1)S(1)} %fusion.1), channel_id=1, source_target_pairs={{0,8},{4,12},{8,0},{12,4},{1,9},{5,13},{9,1},{13,5},{2,10},{6,14},... | collective-permute-start | bytes 172040 | tf_op jit(solution)/shard_map/ppermute | solution.py:366
  25.7 2.5 %collective-permute-done.9 = bf16[224,128]{1,0:T(8,128)(2,1)S(1)} collective-permute-done((bf16[224,128]{1,0:T(8,128)(2,1)S(1)}, bf16[224,128]{1,0:T(8,128)(2,1)S(1)}, u32[]{:S(2)}, u32[]{:S(2)}) %collective-permute-start.9) | collective-permute-done | bytes 57376 | tf_op jit(solution)/shard_map/ppermute | solution.py:366
  28.2 1.6 %collective-permute-start.12 = (bf16[224,128]{1,0:T(8,128)(2,1)S(1)}, bf16[224,128]{1,0:T(8,128)(2,1)S(1)}, u32[]{:S(2)}, u32[]{:S(2)}) collective-permute-start(bf16[224,128]{1,0:T(8,128)(2,1)S(1)} %add_convert_fusion.piece_0), channel_id=1, source_target_pairs={{0,6},{2,4},{4,2},{6,0},{8,14},{10,12},{12,10},{14,8},{1,7},{3,5},... | collective-permute-start | bytes 172040 | tf_op jit(solution)/shard_map/ppermute | solution.py:493
  29.8 0.4 %collective-permute-start.11 = (bf16[224,128]{1,0:T(8,128)(2,1)S(1)}, bf16[224,128]{1,0:T(8,128)(2,1)S(1)}, u32[]{:S(2)}, u32[]{:S(2)}) collective-permute-start(bf16[224,128]{1,0:T(8,128)(2,1)S(1)} %add_convert_fusion.piece_0), channel_id=1, source_target_pairs={{0,4},{2,6},{4,0},{6,2},{8,12},{10,14},{12,8},{14,10},{1,5},{3,7},... | collective-permute-start | bytes 172040 | tf_op jit(solution)/shard_map/ppermute | solution.py:493
  30.2 1.6 %collective-permute-start.10 = (bf16[224,128]{1,0:T(8,128)(2,1)S(1)}, bf16[224,128]{1,0:T(8,128)(2,1)S(1)}, u32[]{:S(2)}, u32[]{:S(2)}) collective-permute-start(bf16[224,128]{1,0:T(8,128)(2,1)S(1)} %add_convert_fusion.piece_0), channel_id=1, source_target_pairs={{0,2},{2,0},{4,6},{6,4},{8,10},{10,8},{12,14},{14,12},{1,3},{3,1},... | collective-permute-start | bytes 172040 | tf_op jit(solution)/shard_map/ppermute | solution.py:493
  31.7 0.5 %shard_map.96 = bf16[12,2,48,128]{3,2,1,0:T(8,128)(2,1)S(1)} custom-call(bf16[13,64,128]{2,1,0:T(8,128)(2,1)S(1)} %get-tuple-element.36.mid_ref, bf16[384,256]{1,0:T(8,128)(2,1)S(1)} %get-tuple-element.34.wa_ref), custom_call_target="tpu_custom_call" | custom-call | tf_op jit(solution)/shard_map/pallas_call | solution.py:474
  32.3 0.8 %copy.33 = bf16[3,8,48,128]{3,1,2,0:T(8,128)(2,1)} copy(bf16[3,8,48,128]{3,2,1,0:T(8,128)(2,1)S(1)} %bitcast.47) | data formatting | bytes 589824
  33.0 0.3 collective-permute-done.12.piece_3
  33.3 0.6 %collective-permute-done.11.piece_2 = bf16[224,128]{1,0:T(8,128)(2,1)S(1)} collective-permute-done((bf16[224,128]{1,0:T(8,128)(2,1)S(1)}, bf16[224,128]{1,0:T(8,128)(2,1)S(1)}, u32[]{:S(2)}, u32[]{:S(2)}) %collective-permute-start.11) | collective-permute-done | bytes 57376 | tf_op jit(solution)/shard_map/ppermute | solution.py:493
  34.0 0.4 %collective-permute-done.10.piece_1 = bf16[224,128]{1,0:T(8,128)(2,1)S(1)} collective-permute-done((bf16[224,128]{1,0:T(8,128)(2,1)S(1)}, bf16[224,128]{1,0:T(8,128)(2,1)S(1)}, u32[]{:S(2)}, u32[]{:S(2)}) %collective-permute-start.10) | collective-permute-done | bytes 57376 | tf_op jit(solution)/shard_map/ppermute | solution.py:493
  34.4 0.9 %shard_map.97 = (f32[9,64,64]{2,1,0:T(8,128)}, f32[9,64,128]{2,1,0:T(8,128)}) custom-call(bf16[224,128]{1,0:T(8,128)(2,1)S(1)} %add_convert_fusion.piece_0, bf16[224,128]{1,0:T(8,128)(2,1)S(1)} %collective-permute-done.10.piece_1, bf16[224,128]{1,0:T(8,128)(2,1)S(1)} %collective-permute-done.11.piece_2, bf16[224,128]{1,0:T(8,128)(2,1)S(1)} %collective-permute-done.12.piece_3), custom_call_target="tpu_custom_call" | custom-call | tf_op jit(solution)/shard_map/pallas_call | solution.py:512
  (26 shorter events, 0.4 us)
Async XLA Ops:
  0.6 2.3 %copy-start = (bf16[24,6144]{1,0:T(8,128)(2,1)S(1)}, bf16[24,6144]{1,0:T(8,128)(2,1)}, u32[]{:S(2)}) copy-start(bf16[24,6144]{1,0:T(8,128)(2,1)} %param.7) | copy-start | bytes 884740
  1.8 1.4 %collective-permute-start = (bf16[1,144,128]{2,1,0:T(8,128)(2,1)S(1)}, bf16[1,144,128]{2,1,0:T(8,128)(2,1)S(1)}, u32[]{:S(2)}, u32[]{:S(2)}) collective-permute-start(bf16[1,144,128]{2,1,0:T(8,128)(2,1)S(1)} %get-tuple-element.27), channel_id=1, source_target_pairs={{0,1},{1,0},{2,3},{3,2},{4,5},{5,4},{6,7},{7,6},{8,9},{9,8},{10,11... | collective-permute-start | bytes 110600 | tf_op jit(solution)/shard_map/ppermute | solution.py:23
  3.3 5.2 %collective-permute-start.2 = (bf16[240,128]{1,0:T(8,128)(2,1)S(1)}, bf16[240,128]{1,0:T(8,128)(2,1)S(1)}, u32[]{:S(2)}, u32[]{:S(2)}) collective-permute-start(bf16[240,128]{1,0:T(8,128)(2,1)S(1)} %pad_maximum_fusion), channel_id=1, source_target_pairs={{0,2},{2,0},{1,3},{3,1},{4,6},{6,4},{5,7},{7,5},{8,10},{10,8},{9,1... | collective-permute-start | bytes 184328 | tf_op jit(solution)/shard_map/ppermute | solution.py:59
  6.1 2.6 %collective-permute-start.1 = (bf16[12,48,128]{2,1,0:T(8,128)(2,1)S(1)}, bf16[12,48,128]{2,1,0:T(8,128)(2,1)S(1)}, u32[]{:S(2)}, u32[]{:S(2)}) collective-permute-start(bf16[12,48,128]{2,1,0:T(8,128)(2,1)S(1)} %bitcast_select_fusion.near_ref), channel_id=1, source_target_pairs={{0,1},{1,0},{2,3},{3,2},{4,5},{5,4},{6,7},{7,6},{8,9},{9,8},{10,11... | collective-permute-start | bytes 442376 | tf_op jit(solution)/shard_map/ppermute | solution.py:23
  8.6 5.4 %collective-permute-start.3 = (bf16[576,128]{1,0:T(8,128)(2,1)S(1)}, bf16[576,128]{1,0:T(8,128)(2,1)S(1)}, u32[]{:S(2)}, u32[]{:S(2)}) collective-permute-start(bf16[576,128]{1,0:T(8,128)(2,1)S(1)} %get-tuple-element.32.own_w2_ref), channel_id=1, source_target_pairs={{0,1},{1,0},{2,3},{3,2},{4,5},{5,4},{6,7},{7,6},{8,9},{9,8},{10,11... | collective-permute-start | bytes 442376 | tf_op jit(solution)/shard_map/ppermute | solution.py:23
  8.9 3.9 %collective-permute-start.4 = (bf16[100,128]{1,0:T(8,128)(2,1)S(1)}, bf16[100,128]{1,0:T(8,128)(2,1)S(1)}, u32[]{:S(2)}, u32[]{:S(2)}) collective-permute-start(bf16[100,128]{1,0:T(8,128)(2,1)S(1)} %concatenate.7), channel_id=1, source_target_pairs={{0,4},{1,3},{2,6},{3,1},{4,0},{5,9},{6,2},{7,11},{8,12},{9,5},{10,... | collective-permute-start | bytes 76808 | tf_op jit(solution)/shard_map/ppermute | solution.py:62
  12.8 1.2 %collective-permute-start.5 = (bf16[100,128]{1,0:T(8,128)(2,1)S(1)}, bf16[100,128]{1,0:T(8,128)(2,1)S(1)}, u32[]{:S(2)}, u32[]{:S(2)}) collective-permute-start(bf16[100,128]{1,0:T(8,128)(2,1)S(1)} %collective-permute-done.4.got_ref), channel_id=1, source_target_pairs={{0,1},{1,0},{2,3},{3,2},{4,5},{5,4},{6,7},{7,6},{8,9},{9,8},{10,11... | collective-permute-start | bytes 76808 | tf_op jit(solution)/shard_map/ppermute | solution.py:23
  15.5 5.2 %collective-permute-start.8 = (bf16[224,128]{1,0:T(8,128)(2,1)S(1)}, bf16[224,128]{1,0:T(8,128)(2,1)S(1)}, u32[]{:S(2)}, u32[]{:S(2)}) collective-permute-start(bf16[224,128]{1,0:T(8,128)(2,1)S(1)} %get-tuple-element.40), channel_id=1, source_target_pairs={{0,6},{2,4},{4,2},{6,0},{8,14},{10,12},{12,10},{14,8},{1,7},{3,5},... | collective-permute-start | bytes 172040 | tf_op jit(solution)/shard_map/ppermute | solution.py:493
  18.4 4.2 %collective-permute-start.7 = (bf16[224,128]{1,0:T(8,128)(2,1)S(1)}, bf16[224,128]{1,0:T(8,128)(2,1)S(1)}, u32[]{:S(2)}, u32[]{:S(2)}) collective-permute-start(bf16[224,128]{1,0:T(8,128)(2,1)S(1)} %get-tuple-element.38), channel_id=1, source_target_pairs={{0,4},{2,6},{4,0},{6,2},{8,12},{10,14},{12,8},{14,10},{1,5},{3,7},... | collective-permute-start | bytes 172040 | tf_op jit(solution)/shard_map/ppermute | solution.py:493
  18.8 4.2 %collective-permute-start.6 = (bf16[224,128]{1,0:T(8,128)(2,1)S(1)}, bf16[224,128]{1,0:T(8,128)(2,1)S(1)}, u32[]{:S(2)}, u32[]{:S(2)}) collective-permute-start(bf16[224,128]{1,0:T(8,128)(2,1)S(1)} %get-tuple-element.49), channel_id=1, source_target_pairs={{0,2},{2,0},{4,6},{6,4},{8,10},{10,8},{12,14},{14,12},{1,3},{3,1},... | collective-permute-start | bytes 172040 | tf_op jit(solution)/shard_map/ppermute | solution.py:493
  23.0 5.1 %collective-permute-start.9 = (bf16[224,128]{1,0:T(8,128)(2,1)S(1)}, bf16[224,128]{1,0:T(8,128)(2,1)S(1)}, u32[]{:S(2)}, u32[]{:S(2)}) collective-permute-start(bf16[224,128]{1,0:T(8,128)(2,1)S(1)} %fusion.1), channel_id=1, source_target_pairs={{0,8},{4,12},{8,0},{12,4},{1,9},{5,13},{9,1},{13,5},{2,10},{6,14},... | collective-permute-start | bytes 172040 | tf_op jit(solution)/shard_map/ppermute | solution.py:366
  28.2 5.1 %collective-permute-start.12 = (bf16[224,128]{1,0:T(8,128)(2,1)S(1)}, bf16[224,128]{1,0:T(8,128)(2,1)S(1)}, u32[]{:S(2)}, u32[]{:S(2)}) collective-permute-start(bf16[224,128]{1,0:T(8,128)(2,1)S(1)} %add_convert_fusion.piece_0), channel_id=1, source_target_pairs={{0,6},{2,4},{4,2},{6,0},{8,14},{10,12},{12,10},{14,8},{1,7},{3,5},... | collective-permute-start | bytes 172040 | tf_op jit(solution)/shard_map/ppermute | solution.py:493
  29.8 4.2 %collective-permute-start.11 = (bf16[224,128]{1,0:T(8,128)(2,1)S(1)}, bf16[224,128]{1,0:T(8,128)(2,1)S(1)}, u32[]{:S(2)}, u32[]{:S(2)}) collective-permute-start(bf16[224,128]{1,0:T(8,128)(2,1)S(1)} %add_convert_fusion.piece_0), channel_id=1, source_target_pairs={{0,4},{2,6},{4,0},{6,2},{8,12},{10,14},{12,8},{14,10},{1,5},{3,7},... | collective-permute-start | bytes 172040 | tf_op jit(solution)/shard_map/ppermute | solution.py:493
  30.2 4.2 %collective-permute-start.10 = (bf16[224,128]{1,0:T(8,128)(2,1)S(1)}, bf16[224,128]{1,0:T(8,128)(2,1)S(1)}, u32[]{:S(2)}, u32[]{:S(2)}) collective-permute-start(bf16[224,128]{1,0:T(8,128)(2,1)S(1)} %add_convert_fusion.piece_0), channel_id=1, source_target_pairs={{0,2},{2,0},{4,6},{6,4},{8,10},{10,8},{12,14},{14,12},{1,3},{3,1},... | collective-permute-start | bytes 172040 | tf_op jit(solution)/shard_map/ppermute | solution.py:493

commit v7 on v6

--- a/solution.py
+++ b/solution.py
@@ -427,13 +427,12 @@
     picture = acts.reshape(height, pairs, lanes)
     edge_a = jnp.where(last, picture[height - 2 :], picture[:2])
     strip = jnp.concatenate([edge_a.reshape(2 * cols, lanes), edge_u], axis=0)
-    strip, near = lax.optimization_barrier((strip, near))
+    strip, near, own_w2 = lax.optimization_barrier((strip, near, own_w2))
     before, after = (
         value.reshape(5, cols, lanes)
         for value in before_and_after(*traded(strip, "rows"), "rows")
     )
     far = core_swapped(near)
-    own_w2, before = lax.optimization_barrier((own_w2, before))
     other_w2 = core_swapped(own_w2)
 
     right = sends_last("tiles")

time: 35.4 us -> 35.3 us (level)
  waiting for transfers between devices: 13.3 us -> 12.8 us
  starting transfers between devices: 15.2 us -> 15.6 us
    ppermute x1, waiting for transfers between devices: 2.38 us -> 1.87 us  [traded(): got = lax.ppermute(value, axis, swaps(size, 1))]
    ppermute x4, starting transfers between devices: 0.59 us -> 1.03 us  [core_swapped(): return lax.ppermute(value, 'chan', [(0, 1), (1, 0)])]
where the time goes in v7:
time: 35.3 us; the launch traced here: 35.2 us
  starting transfers between devices  15.6 us (44%)
  waiting for transfers between devices  12.8 us (36%)
  Pallas kernels  3.91 us (11%)
  between operations  1.52 us (4%)
  local copies, waits for them, and re-layouts  1.12 us (3%)
    ppermute x6, starting transfers between devices, from_block(): got[d] = (value, lax.ppermute(value, ('tiles', 'rows'), pairs))  7.11 us
    ppermute x6, waiting for transfers between devices, from_block(): got[d] = (value, lax.ppermute(value, ('tiles', 'rows'), pairs))  5.3 us
    ppermute x1, starting transfers between devices, traded(): got = lax.ppermute(value, axis, swaps(size, 1))  2.84 us
    ppermute x1, starting transfers between devices, summed_pair(): got = lax.ppermute(value, axis, swaps(size, distance))  2.65 us
    ppermute x1, waiting for transfers between devices, summed_pair(): got = lax.ppermute(value, axis, swaps(size, distance))  2.49 us
    ppermute x1, starting transfers between devices, traded(): got = lax.ppermute(value, ('tiles', 'rows', 'chan'), pairs)  1.98 us
    ppermute x1, waiting for transfers between devices, traded(): got = lax.ppermute(value, ('tiles', 'rows', 'chan'), pairs)  1.93 us
    ppermute x1, waiting for transfers between devices, traded(): got = lax.ppermute(value, axis, swaps(size, 1))  1.87 us
  transfers between devices with their start and end apart: 13, of which 10 were waited for; matrix products, arithmetic and copies ran while one was open for 4% of the time, Pallas kernels for 1%

profile of v7, /device:TPU:0, one launch (start us, length us, event | category | flops | bytes accessed | tf_op | source)
XLA Modules:
  0.0 35.2 jit_solution(3442569788265297928)
XLA Ops:
  0.6 1.1 %shard_map.94 = (bf16[12,48,128]{2,1,0:T(8,128)(2,1)S(1)}, bf16[1,144,128]{2,1,0:T(8,128)(2,1)S(1)}, s32[2,48,128]{2,1,0:T(8,128)S(1)}, bf16[576,128]{1,0:T(8,12...) custom-call(s32[1,1,16]{2,1,0:T(1,128)} %order_hbm.1, bf16[12,48,64]{2,1,0:T(8,128)(2,1)} %cot_hbm.1, ...), custom_call_target="tpu_custom_call" | custom-call | tf_op jit(solution)/shard_map/pallas_call | solution.py:385
  1.8 0.5 %collective-permute-start = (bf16[1,144,128]{2,1,0:T(8,128)(2,1)S(1)}, bf16[1,144,128]{2,1,0:T(8,128)(2,1)S(1)}, u32[]{:S(2)}, u32[]{:S(2)}) collective-permute-start(bf16[1,144,128]{2,1,0:T(8,128)(2,1)S(1)} %get-tuple-element.26), channel_id=1, source_target_pairs={{0,1},{1,0},{2,3},{3,2},{4,5},{5,4},{6,7},{7,6},{8,9},{9,8},{10,11... | collective-permute-start | bytes 110600 | tf_op jit(solution)/shard_map/ppermute | solution.py:23
  3.2 0.0 collective-permute-done
  3.3 2.8 %collective-permute-start.3 = (bf16[240,128]{1,0:T(8,128)(2,1)S(1)}, bf16[240,128]{1,0:T(8,128)(2,1)S(1)}, u32[]{:S(2)}, u32[]{:S(2)}) collective-permute-start(bf16[240,128]{1,0:T(8,128)(2,1)S(1)} %pad_maximum_fusion), channel_id=1, source_target_pairs={{0,2},{2,0},{1,3},{3,1},{4,6},{6,4},{5,7},{7,5},{8,10},{10,8},{9,1... | collective-permute-start | bytes 184328 | tf_op jit(solution)/shard_map/ppermute | solution.py:59
  6.1 0.0 collective-permute-start.2
  6.1 0.5 %collective-permute-start.1 = (bf16[12,48,128]{2,1,0:T(8,128)(2,1)S(1)}, bf16[12,48,128]{2,1,0:T(8,128)(2,1)S(1)}, u32[]{:S(2)}, u32[]{:S(2)}) collective-permute-start(bf16[12,48,128]{2,1,0:T(8,128)(2,1)S(1)} %bitcast_select_fusion.near_ref), channel_id=1, source_target_pairs={{0,1},{1,0},{2,3},{3,2},{4,5},{5,4},{6,7},{7,6},{8,9},{9,8},{10,11... | collective-permute-start | bytes 442376 | tf_op jit(solution)/shard_map/ppermute | solution.py:23
  6.6 1.9 %collective-permute-done.3 = bf16[240,128]{1,0:T(8,128)(2,1)S(1)} collective-permute-done((bf16[240,128]{1,0:T(8,128)(2,1)S(1)}, bf16[240,128]{1,0:T(8,128)(2,1)S(1)}, u32[]{:S(2)}, u32[]{:S(2)}) %collective-permute-start.3) | collective-permute-done | bytes 61472 | tf_op jit(solution)/shard_map/ppermute | solution.py:59
  8.6 0.0 collective-permute-done.1.far_ref
  8.7 0.2 concatenate.7
  8.8 2.0 %collective-permute-start.4 = (bf16[100,128]{1,0:T(8,128)(2,1)S(1)}, bf16[100,128]{1,0:T(8,128)(2,1)S(1)}, u32[]{:S(2)}, u32[]{:S(2)}) collective-permute-start(bf16[100,128]{1,0:T(8,128)(2,1)S(1)} %concatenate.7), channel_id=1, source_target_pairs={{0,4},{1,3},{2,6},{3,1},{4,0},{5,9},{6,2},{7,11},{8,12},{9,5},{10,... | collective-permute-start | bytes 76808 | tf_op jit(solution)/shard_map/ppermute | solution.py:62
  10.8 1.9 %collective-permute-done.4.got_ref = bf16[100,128]{1,0:T(8,128)(2,1)S(1)} collective-permute-done((bf16[100,128]{1,0:T(8,128)(2,1)S(1)}, bf16[100,128]{1,0:T(8,128)(2,1)S(1)}, u32[]{:S(2)}, u32[]{:S(2)}) %collective-permute-start.4) | collective-permute-done | bytes 25632 | tf_op jit(solution)/shard_map/ppermute | solution.py:62
  12.8 0.0 collective-permute-start.5
  12.8 0.0 collective-permute-done.2.other_w2_ref
  12.8 1.2 %collective-permute-done.5.got_other_ref = bf16[100,128]{1,0:T(8,128)(2,1)S(1)} collective-permute-done((bf16[100,128]{1,0:T(8,128)(2,1)S(1)}, bf16[100,128]{1,0:T(8,128)(2,1)S(1)}, u32[]{:S(2)}, u32[]{:S(2)}) %collective-permute-start.5) | collective-permute-done | bytes 25632 | tf_op jit(solution)/shard_map/ppermute | solution.py:23
  14.0 1.4 %shard_map.95 = (bf16[13,64,128]{2,1,0:T(8,128)(2,1)S(1)}, bf16[4,224,128]{2,1,0:T(8,128)(2,1)S(1)}) custom-call(bf16[24,48,128]{2,1,0:T(8,128)(2,1)S(1)} %bitcast.48, bf16[12,48,128]{2,1,0:T(8,128)(2,1)S(1)} %bitcast_select_fusion.near_ref, bf16[12,48,128]{2,1,0:T(8,128)(2,1)S(1)} %collective-permute-done.1.far_ref, ...), custom_call_target="tpu_custom_call" | custom-call | tf_op jit(solution)/shard_map/pallas_call | solution.py:458
  15.4 2.9 %collective-permute-start.8 = (bf16[224,128]{1,0:T(8,128)(2,1)S(1)}, bf16[224,128]{1,0:T(8,128)(2,1)S(1)}, u32[]{:S(2)}, u32[]{:S(2)}) collective-permute-start(bf16[224,128]{1,0:T(8,128)(2,1)S(1)} %get-tuple-element.38), channel_id=1, source_target_pairs={{0,6},{2,4},{4,2},{6,0},{8,14},{10,12},{12,10},{14,8},{1,7},{3,5},... | collective-permute-start | bytes 172040 | tf_op jit(solution)/shard_map/ppermute | solution.py:492
  18.3 0.4 %collective-permute-start.7 = (bf16[224,128]{1,0:T(8,128)(2,1)S(1)}, bf16[224,128]{1,0:T(8,128)(2,1)S(1)}, u32[]{:S(2)}, u32[]{:S(2)}) collective-permute-start(bf16[224,128]{1,0:T(8,128)(2,1)S(1)} %get-tuple-element.36), channel_id=1, source_target_pairs={{0,4},{2,6},{4,0},{6,2},{8,12},{10,14},{12,8},{14,10},{1,5},{3,7},... | collective-permute-start | bytes 172040 | tf_op jit(solution)/shard_map/ppermute | solution.py:492
  18.7 0.2 collective-permute-start.6
  18.9 1.6 %collective-permute-done.8 = bf16[224,128]{1,0:T(8,128)(2,1)S(1)} collective-permute-done((bf16[224,128]{1,0:T(8,128)(2,1)S(1)}, bf16[224,128]{1,0:T(8,128)(2,1)S(1)}, u32[]{:S(2)}, u32[]{:S(2)}) %collective-permute-start.8) | collective-permute-done | bytes 57376 | tf_op jit(solution)/shard_map/ppermute | solution.py:492
  20.5 1.9 %collective-permute-done.7 = bf16[224,128]{1,0:T(8,128)(2,1)S(1)} collective-permute-done((bf16[224,128]{1,0:T(8,128)(2,1)S(1)}, bf16[224,128]{1,0:T(8,128)(2,1)S(1)}, u32[]{:S(2)}, u32[]{:S(2)}) %collective-permute-start.7) | collective-permute-done | bytes 57376 | tf_op jit(solution)/shard_map/ppermute | solution.py:492
  22.4 0.4 %collective-permute-done.6 = bf16[224,128]{1,0:T(8,128)(2,1)S(1)} collective-permute-done((bf16[224,128]{1,0:T(8,128)(2,1)S(1)}, bf16[224,128]{1,0:T(8,128)(2,1)S(1)}, u32[]{:S(2)}, u32[]{:S(2)}) %collective-permute-start.6) | collective-permute-done | bytes 57376 | tf_op jit(solution)/shard_map/ppermute | solution.py:492
  22.9 2.7 %collective-permute-start.9 = (bf16[224,128]{1,0:T(8,128)(2,1)S(1)}, bf16[224,128]{1,0:T(8,128)(2,1)S(1)}, u32[]{:S(2)}, u32[]{:S(2)}) collective-permute-start(bf16[224,128]{1,0:T(8,128)(2,1)S(1)} %fusion.1), channel_id=1, source_target_pairs={{0,8},{4,12},{8,0},{12,4},{1,9},{5,13},{9,1},{13,5},{2,10},{6,14},... | collective-permute-start | bytes 172040 | tf_op jit(solution)/shard_map/ppermute | solution.py:366
  25.6 2.5 %collective-permute-done.9 = bf16[224,128]{1,0:T(8,128)(2,1)S(1)} collective-permute-done((bf16[224,128]{1,0:T(8,128)(2,1)S(1)}, bf16[224,128]{1,0:T(8,128)(2,1)S(1)}, u32[]{:S(2)}, u32[]{:S(2)}) %collective-permute-start.9) | collective-permute-done | bytes 57376 | tf_op jit(solution)/shard_map/ppermute | solution.py:366
  28.1 1.6 %collective-permute-start.12 = (bf16[224,128]{1,0:T(8,128)(2,1)S(1)}, bf16[224,128]{1,0:T(8,128)(2,1)S(1)}, u32[]{:S(2)}, u32[]{:S(2)}) collective-permute-start(bf16[224,128]{1,0:T(8,128)(2,1)S(1)} %add_convert_fusion.piece_0), channel_id=1, source_target_pairs={{0,6},{2,4},{4,2},{6,0},{8,14},{10,12},{12,10},{14,8},{1,7},{3,5},... | collective-permute-start | bytes 172040 | tf_op jit(solution)/shard_map/ppermute | solution.py:492
  29.7 0.4 %collective-permute-start.11 = (bf16[224,128]{1,0:T(8,128)(2,1)S(1)}, bf16[224,128]{1,0:T(8,128)(2,1)S(1)}, u32[]{:S(2)}, u32[]{:S(2)}) collective-permute-start(bf16[224,128]{1,0:T(8,128)(2,1)S(1)} %add_convert_fusion.piece_0), channel_id=1, source_target_pairs={{0,4},{2,6},{4,0},{6,2},{8,12},{10,14},{12,8},{14,10},{1,5},{3,7},... | collective-permute-start | bytes 172040 | tf_op jit(solution)/shard_map/ppermute | solution.py:492
  30.1 1.6 %collective-permute-start.10 = (bf16[224,128]{1,0:T(8,128)(2,1)S(1)}, bf16[224,128]{1,0:T(8,128)(2,1)S(1)}, u32[]{:S(2)}, u32[]{:S(2)}) collective-permute-start(bf16[224,128]{1,0:T(8,128)(2,1)S(1)} %add_convert_fusion.piece_0), channel_id=1, source_target_pairs={{0,2},{2,0},{4,6},{6,4},{8,10},{10,8},{12,14},{14,12},{1,3},{3,1},... | collective-permute-start | bytes 172040 | tf_op jit(solution)/shard_map/ppermute | solution.py:492
  31.7 0.5 %shard_map.96 = bf16[12,2,48,128]{3,2,1,0:T(8,128)(2,1)S(1)} custom-call(bf16[13,64,128]{2,1,0:T(8,128)(2,1)S(1)} %get-tuple-element.34.mid_ref, bf16[384,256]{1,0:T(8,128)(2,1)S(1)} %get-tuple-element.32.wa_ref), custom_call_target="tpu_custom_call" | custom-call | tf_op jit(solution)/shard_map/pallas_call | solution.py:473
  32.2 0.8 %copy.34 = bf16[3,8,48,128]{3,1,2,0:T(8,128)(2,1)} copy(bf16[3,8,48,128]{3,2,1,0:T(8,128)(2,1)S(1)} %bitcast.49) | data formatting | bytes 589824
  33.0 0.3 collective-permute-done.12.piece_3
  33.2 0.6 %collective-permute-done.11.piece_2 = bf16[224,128]{1,0:T(8,128)(2,1)S(1)} collective-permute-done((bf16[224,128]{1,0:T(8,128)(2,1)S(1)}, bf16[224,128]{1,0:T(8,128)(2,1)S(1)}, u32[]{:S(2)}, u32[]{:S(2)}) %collective-permute-start.11) | collective-permute-done | bytes 57376 | tf_op jit(solution)/shard_map/ppermute | solution.py:492
  33.9 0.4 %collective-permute-done.10.piece_1 = bf16[224,128]{1,0:T(8,128)(2,1)S(1)} collective-permute-done((bf16[224,128]{1,0:T(8,128)(2,1)S(1)}, bf16[224,128]{1,0:T(8,128)(2,1)S(1)}, u32[]{:S(2)}, u32[]{:S(2)}) %collective-permute-start.10) | collective-permute-done | bytes 57376 | tf_op jit(solution)/shard_map/ppermute | solution.py:492
  34.3 0.9 %shard_map.97 = (f32[9,64,64]{2,1,0:T(8,128)}, f32[9,64,128]{2,1,0:T(8,128)}) custom-call(bf16[224,128]{1,0:T(8,128)(2,1)S(1)} %add_convert_fusion.piece_0, bf16[224,128]{1,0:T(8,128)(2,1)S(1)} %collective-permute-done.10.piece_1, bf16[224,128]{1,0:T(8,128)(2,1)S(1)} %collective-permute-done.11.piece_2, bf16[224,128]{1,0:T(8,128)(2,1)S(1)} %collective-permute-done.12.piece_3), custom_call_target="tpu_custom_call" | custom-call | tf_op jit(solution)/shard_map/pallas_call | solution.py:511
  (27 shorter events, 0.4 us)
Async XLA Ops:
  0.6 2.3 %copy-start = (bf16[24,6144]{1,0:T(8,128)(2,1)S(1)}, bf16[24,6144]{1,0:T(8,128)(2,1)}, u32[]{:S(2)}) copy-start(bf16[24,6144]{1,0:T(8,128)(2,1)} %param.7) | copy-start | bytes 884740
  1.8 1.4 %collective-permute-start = (bf16[1,144,128]{2,1,0:T(8,128)(2,1)S(1)}, bf16[1,144,128]{2,1,0:T(8,128)(2,1)S(1)}, u32[]{:S(2)}, u32[]{:S(2)}) collective-permute-start(bf16[1,144,128]{2,1,0:T(8,128)(2,1)S(1)} %get-tuple-element.26), channel_id=1, source_target_pairs={{0,1},{1,0},{2,3},{3,2},{4,5},{5,4},{6,7},{7,6},{8,9},{9,8},{10,11... | collective-permute-start | bytes 110600 | tf_op jit(solution)/shard_map/ppermute | solution.py:23
  3.3 5.2 %collective-permute-start.3 = (bf16[240,128]{1,0:T(8,128)(2,1)S(1)}, bf16[240,128]{1,0:T(8,128)(2,1)S(1)}, u32[]{:S(2)}, u32[]{:S(2)}) collective-permute-start(bf16[240,128]{1,0:T(8,128)(2,1)S(1)} %pad_maximum_fusion), channel_id=1, source_target_pairs={{0,2},{2,0},{1,3},{3,1},{4,6},{6,4},{5,7},{7,5},{8,10},{10,8},{9,1... | collective-permute-start | bytes 184328 | tf_op jit(solution)/shard_map/ppermute | solution.py:59
  6.1 6.7 %collective-permute-start.2 = (bf16[576,128]{1,0:T(8,128)(2,1)S(1)}, bf16[576,128]{1,0:T(8,128)(2,1)S(1)}, u32[]{:S(2)}, u32[]{:S(2)}) collective-permute-start(bf16[576,128]{1,0:T(8,128)(2,1)S(1)} %get-tuple-element.30.own_w2_ref), channel_id=1, source_target_pairs={{0,1},{1,0},{2,3},{3,2},{4,5},{5,4},{6,7},{7,6},{8,9},{9,8},{10,11... | collective-permute-start | bytes 442376 | tf_op jit(solution)/shard_map/ppermute | solution.py:23
  6.1 2.5 %collective-permute-start.1 = (bf16[12,48,128]{2,1,0:T(8,128)(2,1)S(1)}, bf16[12,48,128]{2,1,0:T(8,128)(2,1)S(1)}, u32[]{:S(2)}, u32[]{:S(2)}) collective-permute-start(bf16[12,48,128]{2,1,0:T(8,128)(2,1)S(1)} %bitcast_select_fusion.near_ref), channel_id=1, source_target_pairs={{0,1},{1,0},{2,3},{3,2},{4,5},{5,4},{6,7},{7,6},{8,9},{9,8},{10,11... | collective-permute-start | bytes 442376 | tf_op jit(solution)/shard_map/ppermute | solution.py:23
  8.8 3.9 %collective-permute-start.4 = (bf16[100,128]{1,0:T(8,128)(2,1)S(1)}, bf16[100,128]{1,0:T(8,128)(2,1)S(1)}, u32[]{:S(2)}, u32[]{:S(2)}) collective-permute-start(bf16[100,128]{1,0:T(8,128)(2,1)S(1)} %concatenate.7), channel_id=1, source_target_pairs={{0,4},{1,3},{2,6},{3,1},{4,0},{5,9},{6,2},{7,11},{8,12},{9,5},{10,... | collective-permute-start | bytes 76808 | tf_op jit(solution)/shard_map/ppermute | solution.py:62
  12.8 1.2 %collective-permute-start.5 = (bf16[100,128]{1,0:T(8,128)(2,1)S(1)}, bf16[100,128]{1,0:T(8,128)(2,1)S(1)}, u32[]{:S(2)}, u32[]{:S(2)}) collective-permute-start(bf16[100,128]{1,0:T(8,128)(2,1)S(1)} %collective-permute-done.4.got_ref), channel_id=1, source_target_pairs={{0,1},{1,0},{2,3},{3,2},{4,5},{5,4},{6,7},{7,6},{8,9},{9,8},{10,11... | collective-permute-start | bytes 76808 | tf_op jit(solution)/shard_map/ppermute | solution.py:23
  15.4 5.2 %collective-permute-start.8 = (bf16[224,128]{1,0:T(8,128)(2,1)S(1)}, bf16[224,128]{1,0:T(8,128)(2,1)S(1)}, u32[]{:S(2)}, u32[]{:S(2)}) collective-permute-start(bf16[224,128]{1,0:T(8,128)(2,1)S(1)} %get-tuple-element.38), channel_id=1, source_target_pairs={{0,6},{2,4},{4,2},{6,0},{8,14},{10,12},{12,10},{14,8},{1,7},{3,5},... | collective-permute-start | bytes 172040 | tf_op jit(solution)/shard_map/ppermute | solution.py:492
  18.3 4.2 %collective-permute-start.7 = (bf16[224,128]{1,0:T(8,128)(2,1)S(1)}, bf16[224,128]{1,0:T(8,128)(2,1)S(1)}, u32[]{:S(2)}, u32[]{:S(2)}) collective-permute-start(bf16[224,128]{1,0:T(8,128)(2,1)S(1)} %get-tuple-element.36), channel_id=1, source_target_pairs={{0,4},{2,6},{4,0},{6,2},{8,12},{10,14},{12,8},{14,10},{1,5},{3,7},... | collective-permute-start | bytes 172040 | tf_op jit(solution)/shard_map/ppermute | solution.py:492
  18.7 4.2 %collective-permute-start.6 = (bf16[224,128]{1,0:T(8,128)(2,1)S(1)}, bf16[224,128]{1,0:T(8,128)(2,1)S(1)}, u32[]{:S(2)}, u32[]{:S(2)}) collective-permute-start(bf16[224,128]{1,0:T(8,128)(2,1)S(1)} %get-tuple-element.47), channel_id=1, source_target_pairs={{0,2},{2,0},{4,6},{6,4},{8,10},{10,8},{12,14},{14,12},{1,3},{3,1},... | collective-permute-start | bytes 172040 | tf_op jit(solution)/shard_map/ppermute | solution.py:492
  22.9 5.1 %collective-permute-start.9 = (bf16[224,128]{1,0:T(8,128)(2,1)S(1)}, bf16[224,128]{1,0:T(8,128)(2,1)S(1)}, u32[]{:S(2)}, u32[]{:S(2)}) collective-permute-start(bf16[224,128]{1,0:T(8,128)(2,1)S(1)} %fusion.1), channel_id=1, source_target_pairs={{0,8},{4,12},{8,0},{12,4},{1,9},{5,13},{9,1},{13,5},{2,10},{6,14},... | collective-permute-start | bytes 172040 | tf_op jit(solution)/shard_map/ppermute | solution.py:366
  28.1 5.1 %collective-permute-start.12 = (bf16[224,128]{1,0:T(8,128)(2,1)S(1)}, bf16[224,128]{1,0:T(8,128)(2,1)S(1)}, u32[]{:S(2)}, u32[]{:S(2)}) collective-permute-start(bf16[224,128]{1,0:T(8,128)(2,1)S(1)} %add_convert_fusion.piece_0), channel_id=1, source_target_pairs={{0,6},{2,4},{4,2},{6,0},{8,14},{10,12},{12,10},{14,8},{1,7},{3,5},... | collective-permute-start | bytes 172040 | tf_op jit(solution)/shard_map/ppermute | solution.py:492
  29.7 4.2 %collective-permute-start.11 = (bf16[224,128]{1,0:T(8,128)(2,1)S(1)}, bf16[224,128]{1,0:T(8,128)(2,1)S(1)}, u32[]{:S(2)}, u32[]{:S(2)}) collective-permute-start(bf16[224,128]{1,0:T(8,128)(2,1)S(1)} %add_convert_fusion.piece_0), channel_id=1, source_target_pairs={{0,4},{2,6},{4,0},{6,2},{8,12},{10,14},{12,8},{14,10},{1,5},{3,7},... | collective-permute-start | bytes 172040 | tf_op jit(solution)/shard_map/ppermute | solution.py:492
  30.1 4.2 %collective-permute-start.10 = (bf16[224,128]{1,0:T(8,128)(2,1)S(1)}, bf16[224,128]{1,0:T(8,128)(2,1)S(1)}, u32[]{:S(2)}, u32[]{:S(2)}) collective-permute-start(bf16[224,128]{1,0:T(8,128)(2,1)S(1)} %add_convert_fusion.piece_0), channel_id=1, source_target_pairs={{0,2},{2,0},{4,6},{6,4},{8,10},{10,8},{12,14},{14,12},{1,3},{3,1},... | collective-permute-start | bytes 172040 | tf_op jit(solution)/shard_map/ppermute | solution.py:492

commit v8 on v7

--- a/solution.py
+++ b/solution.py
@@ -209,14 +209,14 @@
         value = [right_strip[at : at + count], fill, left_strip[at : at + count]]
         return jnp.concatenate(value, axis=0).astype(BF)
 
-    own_u, halo_a, halo_u = height, height + 4 * rows, height + 4 * rows + 4
+    own_a, halo_a, halo_u = 4 * rows, height + 4 * rows, height + 4 * rows + 4
     for i in range(height):
-        a_ref[i // 2 + 1, i % 2, own_cols:] = edge(i, 1)
+        a_ref[i // 2 + 1, i % 2, own_cols:] = edge(own_a + i, 1)
     for i in range(2):
         a_ref[0, i, own_cols:] = edge(halo_a + i, 1)
         a_ref[rows + 1, i, own_cols:] = edge(halo_a + 2 + i, 1)
     for i in range(rows):
-        u_ref[i + 3, own_cols:] = edge(own_u + 4 * i, 4)
+        u_ref[i + 3, own_cols:] = edge(4 * i, 4)
     for i in range(3):
         u_ref[i, own_cols:] = edge(halo_u + 4 * i, 4)
         u_ref[rows + 3 + i, own_cols:] = edge(halo_u + 12 + 4 * i, 4)
@@ -442,8 +442,8 @@
     got, got_other = traded(
         jnp.concatenate(
             [
+                side(near, 4) + side(far, 4),
                 side(picture, 1),
-                side(near, 4) + side(far, 4),
                 side(before[:2], 1),
                 side(after[:2], 1),
                 side(before[2:], 4),

time: 35.3 us -> 35.3 us (level)
  no operation moved by 1% of the time
where the time goes in v8:
time: 35.3 us; the launch traced here: 35.2 us
  starting transfers between devices  15.6 us (44%)
  waiting for transfers between devices  12.8 us (36%)
  Pallas kernels  3.89 us (11%)
  between operations  1.52 us (4%)
  local copies, waits for them, and re-layouts  1.12 us (3%)
    ppermute x6, starting transfers between devices, from_block(): got[d] = (value, lax.ppermute(value, ('tiles', 'rows'), pairs))  7.11 us
    ppermute x6, waiting for transfers between devices, from_block(): got[d] = (value, lax.ppermute(value, ('tiles', 'rows'), pairs))  5.31 us
    ppermute x1, starting transfers between devices, traded(): got = lax.ppermute(value, axis, swaps(size, 1))  2.84 us
    ppermute x1, starting transfers between devices, summed_pair(): got = lax.ppermute(value, axis, swaps(size, distance))  2.65 us
    ppermute x1, waiting for transfers between devices, summed_pair(): got = lax.ppermute(value, axis, swaps(size, distance))  2.49 us
    ppermute x1, starting transfers between devices, traded(): got = lax.ppermute(value, ('tiles', 'rows', 'chan'), pairs)  1.98 us
    ppermute x1, waiting for transfers between devices, traded(): got = lax.ppermute(value, ('tiles', 'rows', 'chan'), pairs)  1.93 us
    ppermute x1, waiting for transfers between devices, traded(): got = lax.ppermute(value, axis, swaps(size, 1))  1.87 us
  transfers between devices with their start and end apart: 13, of which 10 were waited for; matrix products, arithmetic and copies ran while one was open for 4% of the time, Pallas kernels for 1%

profile of v8, /device:TPU:0, one launch (start us, length us, event | category | flops | bytes accessed | tf_op | source)
XLA Modules:
  0.0 35.2 jit_solution(17227825019719022972)
XLA Ops:
  0.6 1.1 %shard_map.94 = (bf16[12,48,128]{2,1,0:T(8,128)(2,1)S(1)}, bf16[1,144,128]{2,1,0:T(8,128)(2,1)S(1)}, s32[2,48,128]{2,1,0:T(8,128)S(1)}, bf16[576,128]{1,0:T(8,12...) custom-call(s32[1,1,16]{2,1,0:T(1,128)} %order_hbm.1, bf16[12,48,64]{2,1,0:T(8,128)(2,1)} %cot_hbm.1, ...), custom_call_target="tpu_custom_call" | custom-call | tf_op jit(solution)/shard_map/pallas_call | solution.py:385
  1.8 0.5 %collective-permute-start = (bf16[1,144,128]{2,1,0:T(8,128)(2,1)S(1)}, bf16[1,144,128]{2,1,0:T(8,128)(2,1)S(1)}, u32[]{:S(2)}, u32[]{:S(2)}) collective-permute-start(bf16[1,144,128]{2,1,0:T(8,128)(2,1)S(1)} %get-tuple-element.26), channel_id=1, source_target_pairs={{0,1},{1,0},{2,3},{3,2},{4,5},{5,4},{6,7},{7,6},{8,9},{9,8},{10,11... | collective-permute-start | bytes 110600 | tf_op jit(solution)/shard_map/ppermute | solution.py:23
  3.2 0.0 collective-permute-done
  3.3 2.8 %collective-permute-start.3 = (bf16[240,128]{1,0:T(8,128)(2,1)S(1)}, bf16[240,128]{1,0:T(8,128)(2,1)S(1)}, u32[]{:S(2)}, u32[]{:S(2)}) collective-permute-start(bf16[240,128]{1,0:T(8,128)(2,1)S(1)} %pad_maximum_fusion), channel_id=1, source_target_pairs={{0,2},{2,0},{1,3},{3,1},{4,6},{6,4},{5,7},{7,5},{8,10},{10,8},{9,1... | collective-permute-start | bytes 184328 | tf_op jit(solution)/shard_map/ppermute | solution.py:59
  6.1 0.0 collective-permute-start.2
  6.1 0.5 %collective-permute-start.1 = (bf16[12,48,128]{2,1,0:T(8,128)(2,1)S(1)}, bf16[12,48,128]{2,1,0:T(8,128)(2,1)S(1)}, u32[]{:S(2)}, u32[]{:S(2)}) collective-permute-start(bf16[12,48,128]{2,1,0:T(8,128)(2,1)S(1)} %bitcast_select_fusion.near_ref), channel_id=1, source_target_pairs={{0,1},{1,0},{2,3},{3,2},{4,5},{5,4},{6,7},{7,6},{8,9},{9,8},{10,11... | collective-permute-start | bytes 442376 | tf_op jit(solution)/shard_map/ppermute | solution.py:23
  6.6 1.9 %collective-permute-done.3 = bf16[240,128]{1,0:T(8,128)(2,1)S(1)} collective-permute-done((bf16[240,128]{1,0:T(8,128)(2,1)S(1)}, bf16[240,128]{1,0:T(8,128)(2,1)S(1)}, u32[]{:S(2)}, u32[]{:S(2)}) %collective-permute-start.3) | collective-permute-done | bytes 61472 | tf_op jit(solution)/shard_map/ppermute | solution.py:59
  8.6 0.0 collective-permute-done.1.far_ref
  8.7 0.2 concatenate.7
  8.8 2.0 %collective-permute-start.4 = (bf16[100,128]{1,0:T(8,128)(2,1)S(1)}, bf16[100,128]{1,0:T(8,128)(2,1)S(1)}, u32[]{:S(2)}, u32[]{:S(2)}) collective-permute-start(bf16[100,128]{1,0:T(8,128)(2,1)S(1)} %concatenate.7), channel_id=1, source_target_pairs={{0,4},{1,3},{2,6},{3,1},{4,0},{5,9},{6,2},{7,11},{8,12},{9,5},{10,... | collective-permute-start | bytes 76808 | tf_op jit(solution)/shard_map/ppermute | solution.py:62
  10.8 1.9 %collective-permute-done.4.got_ref = bf16[100,128]{1,0:T(8,128)(2,1)S(1)} collective-permute-done((bf16[100,128]{1,0:T(8,128)(2,1)S(1)}, bf16[100,128]{1,0:T(8,128)(2,1)S(1)}, u32[]{:S(2)}, u32[]{:S(2)}) %collective-permute-start.4) | collective-permute-done | bytes 25632 | tf_op jit(solution)/shard_map/ppermute | solution.py:62
  12.8 0.0 collective-permute-start.5
  12.8 0.0 collective-permute-done.2.other_w2_ref
  12.8 1.2 %collective-permute-done.5.got_other_ref = bf16[100,128]{1,0:T(8,128)(2,1)S(1)} collective-permute-done((bf16[100,128]{1,0:T(8,128)(2,1)S(1)}, bf16[100,128]{1,0:T(8,128)(2,1)S(1)}, u32[]{:S(2)}, u32[]{:S(2)}) %collective-permute-start.5) | collective-permute-done | bytes 25632 | tf_op jit(solution)/shard_map/ppermute | solution.py:23
  14.0 1.4 %shard_map.95 = (bf16[13,64,128]{2,1,0:T(8,128)(2,1)S(1)}, bf16[4,224,128]{2,1,0:T(8,128)(2,1)S(1)}) custom-call(bf16[24,48,128]{2,1,0:T(8,128)(2,1)S(1)} %bitcast.48, bf16[12,48,128]{2,1,0:T(8,128)(2,1)S(1)} %bitcast_select_fusion.near_ref, bf16[12,48,128]{2,1,0:T(8,128)(2,1)S(1)} %collective-permute-done.1.far_ref, ...), custom_call_target="tpu_custom_call" | custom-call | tf_op jit(solution)/shard_map/pallas_call | solution.py:458
  15.4 2.9 %collective-permute-start.8 = (bf16[224,128]{1,0:T(8,128)(2,1)S(1)}, bf16[224,128]{1,0:T(8,128)(2,1)S(1)}, u32[]{:S(2)}, u32[]{:S(2)}) collective-permute-start(bf16[224,128]{1,0:T(8,128)(2,1)S(1)} %get-tuple-element.38), channel_id=1, source_target_pairs={{0,6},{2,4},{4,2},{6,0},{8,14},{10,12},{12,10},{14,8},{1,7},{3,5},... | collective-permute-start | bytes 172040 | tf_op jit(solution)/shard_map/ppermute | solution.py:492
  18.3 0.4 %collective-permute-start.7 = (bf16[224,128]{1,0:T(8,128)(2,1)S(1)}, bf16[224,128]{1,0:T(8,128)(2,1)S(1)}, u32[]{:S(2)}, u32[]{:S(2)}) collective-permute-start(bf16[224,128]{1,0:T(8,128)(2,1)S(1)} %get-tuple-element.36), channel_id=1, source_target_pairs={{0,4},{2,6},{4,0},{6,2},{8,12},{10,14},{12,8},{14,10},{1,5},{3,7},... | collective-permute-start | bytes 172040 | tf_op jit(solution)/shard_map/ppermute | solution.py:492
  18.7 0.2 collective-permute-start.6
  18.9 1.6 %collective-permute-done.8 = bf16[224,128]{1,0:T(8,128)(2,1)S(1)} collective-permute-done((bf16[224,128]{1,0:T(8,128)(2,1)S(1)}, bf16[224,128]{1,0:T(8,128)(2,1)S(1)}, u32[]{:S(2)}, u32[]{:S(2)}) %collective-permute-start.8) | collective-permute-done | bytes 57376 | tf_op jit(solution)/shard_map/ppermute | solution.py:492
  20.5 1.9 %collective-permute-done.7 = bf16[224,128]{1,0:T(8,128)(2,1)S(1)} collective-permute-done((bf16[224,128]{1,0:T(8,128)(2,1)S(1)}, bf16[224,128]{1,0:T(8,128)(2,1)S(1)}, u32[]{:S(2)}, u32[]{:S(2)}) %collective-permute-start.7) | collective-permute-done | bytes 57376 | tf_op jit(solution)/shard_map/ppermute | solution.py:492
  22.4 0.4 %collective-permute-done.6 = bf16[224,128]{1,0:T(8,128)(2,1)S(1)} collective-permute-done((bf16[224,128]{1,0:T(8,128)(2,1)S(1)}, bf16[224,128]{1,0:T(8,128)(2,1)S(1)}, u32[]{:S(2)}, u32[]{:S(2)}) %collective-permute-start.6) | collective-permute-done | bytes 57376 | tf_op jit(solution)/shard_map/ppermute | solution.py:492
  22.9 2.7 %collective-permute-start.9 = (bf16[224,128]{1,0:T(8,128)(2,1)S(1)}, bf16[224,128]{1,0:T(8,128)(2,1)S(1)}, u32[]{:S(2)}, u32[]{:S(2)}) collective-permute-start(bf16[224,128]{1,0:T(8,128)(2,1)S(1)} %fusion.1), channel_id=1, source_target_pairs={{0,8},{4,12},{8,0},{12,4},{1,9},{5,13},{9,1},{13,5},{2,10},{6,14},... | collective-permute-start | bytes 172040 | tf_op jit(solution)/shard_map/ppermute | solution.py:366
  25.6 2.5 %collective-permute-done.9 = bf16[224,128]{1,0:T(8,128)(2,1)S(1)} collective-permute-done((bf16[224,128]{1,0:T(8,128)(2,1)S(1)}, bf16[224,128]{1,0:T(8,128)(2,1)S(1)}, u32[]{:S(2)}, u32[]{:S(2)}) %collective-permute-start.9) | collective-permute-done | bytes 57376 | tf_op jit(solution)/shard_map/ppermute | solution.py:366
  28.1 1.6 %collective-permute-start.12 = (bf16[224,128]{1,0:T(8,128)(2,1)S(1)}, bf16[224,128]{1,0:T(8,128)(2,1)S(1)}, u32[]{:S(2)}, u32[]{:S(2)}) collective-permute-start(bf16[224,128]{1,0:T(8,128)(2,1)S(1)} %add_convert_fusion.piece_0), channel_id=1, source_target_pairs={{0,6},{2,4},{4,2},{6,0},{8,14},{10,12},{12,10},{14,8},{1,7},{3,5},... | collective-permute-start | bytes 172040 | tf_op jit(solution)/shard_map/ppermute | solution.py:492
  29.7 0.4 %collective-permute-start.11 = (bf16[224,128]{1,0:T(8,128)(2,1)S(1)}, bf16[224,128]{1,0:T(8,128)(2,1)S(1)}, u32[]{:S(2)}, u32[]{:S(2)}) collective-permute-start(bf16[224,128]{1,0:T(8,128)(2,1)S(1)} %add_convert_fusion.piece_0), channel_id=1, source_target_pairs={{0,4},{2,6},{4,0},{6,2},{8,12},{10,14},{12,8},{14,10},{1,5},{3,7},... | collective-permute-start | bytes 172040 | tf_op jit(solution)/shard_map/ppermute | solution.py:492
  30.1 1.6 %collective-permute-start.10 = (bf16[224,128]{1,0:T(8,128)(2,1)S(1)}, bf16[224,128]{1,0:T(8,128)(2,1)S(1)}, u32[]{:S(2)}, u32[]{:S(2)}) collective-permute-start(bf16[224,128]{1,0:T(8,128)(2,1)S(1)} %add_convert_fusion.piece_0), channel_id=1, source_target_pairs={{0,2},{2,0},{4,6},{6,4},{8,10},{10,8},{12,14},{14,12},{1,3},{3,1},... | collective-permute-start | bytes 172040 | tf_op jit(solution)/shard_map/ppermute | solution.py:492
  31.6 0.5 %shard_map.96 = bf16[12,2,48,128]{3,2,1,0:T(8,128)(2,1)S(1)} custom-call(bf16[13,64,128]{2,1,0:T(8,128)(2,1)S(1)} %get-tuple-element.34.mid_ref, bf16[384,256]{1,0:T(8,128)(2,1)S(1)} %get-tuple-element.32.wa_ref), custom_call_target="tpu_custom_call" | custom-call | tf_op jit(solution)/shard_map/pallas_call | solution.py:473
  32.1 0.8 %copy.34 = bf16[3,8,48,128]{3,1,2,0:T(8,128)(2,1)} copy(bf16[3,8,48,128]{3,2,1,0:T(8,128)(2,1)S(1)} %bitcast.49) | data formatting | bytes 589824
  32.9 0.3 collective-permute-done.12.piece_3
  33.2 0.7 %collective-permute-done.11.piece_2 = bf16[224,128]{1,0:T(8,128)(2,1)S(1)} collective-permute-done((bf16[224,128]{1,0:T(8,128)(2,1)S(1)}, bf16[224,128]{1,0:T(8,128)(2,1)S(1)}, u32[]{:S(2)}, u32[]{:S(2)}) %collective-permute-start.11) | collective-permute-done | bytes 57376 | tf_op jit(solution)/shard_map/ppermute | solution.py:492
  33.9 0.4 %collective-permute-done.10.piece_1 = bf16[224,128]{1,0:T(8,128)(2,1)S(1)} collective-permute-done((bf16[224,128]{1,0:T(8,128)(2,1)S(1)}, bf16[224,128]{1,0:T(8,128)(2,1)S(1)}, u32[]{:S(2)}, u32[]{:S(2)}) %collective-permute-start.10) | collective-permute-done | bytes 57376 | tf_op jit(solution)/shard_map/ppermute | solution.py:492
  34.3 0.9 %shard_map.97 = (f32[9,64,64]{2,1,0:T(8,128)}, f32[9,64,128]{2,1,0:T(8,128)}) custom-call(bf16[224,128]{1,0:T(8,128)(2,1)S(1)} %add_convert_fusion.piece_0, bf16[224,128]{1,0:T(8,128)(2,1)S(1)} %collective-permute-done.10.piece_1, bf16[224,128]{1,0:T(8,128)(2,1)S(1)} %collective-permute-done.11.piece_2, bf16[224,128]{1,0:T(8,128)(2,1)S(1)} %collective-permute-done.12.piece_3), custom_call_target="tpu_custom_call" | custom-call | tf_op jit(solution)/shard_map/pallas_call | solution.py:511
  (27 shorter events, 0.4 us)
Async XLA Ops:
  0.6 2.3 %copy-start = (bf16[24,6144]{1,0:T(8,128)(2,1)S(1)}, bf16[24,6144]{1,0:T(8,128)(2,1)}, u32[]{:S(2)}) copy-start(bf16[24,6144]{1,0:T(8,128)(2,1)} %param.7) | copy-start | bytes 884740
  1.8 1.4 %collective-permute-start = (bf16[1,144,128]{2,1,0:T(8,128)(2,1)S(1)}, bf16[1,144,128]{2,1,0:T(8,128)(2,1)S(1)}, u32[]{:S(2)}, u32[]{:S(2)}) collective-permute-start(bf16[1,144,128]{2,1,0:T(8,128)(2,1)S(1)} %get-tuple-element.26), channel_id=1, source_target_pairs={{0,1},{1,0},{2,3},{3,2},{4,5},{5,4},{6,7},{7,6},{8,9},{9,8},{10,11... | collective-permute-start | bytes 110600 | tf_op jit(solution)/shard_map/ppermute | solution.py:23
  3.3 5.2 %collective-permute-start.3 = (bf16[240,128]{1,0:T(8,128)(2,1)S(1)}, bf16[240,128]{1,0:T(8,128)(2,1)S(1)}, u32[]{:S(2)}, u32[]{:S(2)}) collective-permute-start(bf16[240,128]{1,0:T(8,128)(2,1)S(1)} %pad_maximum_fusion), channel_id=1, source_target_pairs={{0,2},{2,0},{1,3},{3,1},{4,6},{6,4},{5,7},{7,5},{8,10},{10,8},{9,1... | collective-permute-start | bytes 184328 | tf_op jit(solution)/shard_map/ppermute | solution.py:59
  6.1 6.7 %collective-permute-start.2 = (bf16[576,128]{1,0:T(8,128)(2,1)S(1)}, bf16[576,128]{1,0:T(8,128)(2,1)S(1)}, u32[]{:S(2)}, u32[]{:S(2)}) collective-permute-start(bf16[576,128]{1,0:T(8,128)(2,1)S(1)} %get-tuple-element.30.own_w2_ref), channel_id=1, source_target_pairs={{0,1},{1,0},{2,3},{3,2},{4,5},{5,4},{6,7},{7,6},{8,9},{9,8},{10,11... | collective-permute-start | bytes 442376 | tf_op jit(solution)/shard_map/ppermute | solution.py:23
  6.1 2.5 %collective-permute-start.1 = (bf16[12,48,128]{2,1,0:T(8,128)(2,1)S(1)}, bf16[12,48,128]{2,1,0:T(8,128)(2,1)S(1)}, u32[]{:S(2)}, u32[]{:S(2)}) collective-permute-start(bf16[12,48,128]{2,1,0:T(8,128)(2,1)S(1)} %bitcast_select_fusion.near_ref), channel_id=1, source_target_pairs={{0,1},{1,0},{2,3},{3,2},{4,5},{5,4},{6,7},{7,6},{8,9},{9,8},{10,11... | collective-permute-start | bytes 442376 | tf_op jit(solution)/shard_map/ppermute | solution.py:23
  8.8 3.9 %collective-permute-start.4 = (bf16[100,128]{1,0:T(8,128)(2,1)S(1)}, bf16[100,128]{1,0:T(8,128)(2,1)S(1)}, u32[]{:S(2)}, u32[]{:S(2)}) collective-permute-start(bf16[100,128]{1,0:T(8,128)(2,1)S(1)} %concatenate.7), channel_id=1, source_target_pairs={{0,4},{1,3},{2,6},{3,1},{4,0},{5,9},{6,2},{7,11},{8,12},{9,5},{10,... | collective-permute-start | bytes 76808 | tf_op jit(solution)/shard_map/ppermute | solution.py:62
  12.8 1.2 %collective-permute-start.5 = (bf16[100,128]{1,0:T(8,128)(2,1)S(1)}, bf16[100,128]{1,0:T(8,128)(2,1)S(1)}, u32[]{:S(2)}, u32[]{:S(2)}) collective-permute-start(bf16[100,128]{1,0:T(8,128)(2,1)S(1)} %collective-permute-done.4.got_ref), channel_id=1, source_target_pairs={{0,1},{1,0},{2,3},{3,2},{4,5},{5,4},{6,7},{7,6},{8,9},{9,8},{10,11... | collective-permute-start | bytes 76808 | tf_op jit(solution)/shard_map/ppermute | solution.py:23
  15.4 5.2 %collective-permute-start.8 = (bf16[224,128]{1,0:T(8,128)(2,1)S(1)}, bf16[224,128]{1,0:T(8,128)(2,1)S(1)}, u32[]{:S(2)}, u32[]{:S(2)}) collective-permute-start(bf16[224,128]{1,0:T(8,128)(2,1)S(1)} %get-tuple-element.38), channel_id=1, source_target_pairs={{0,6},{2,4},{4,2},{6,0},{8,14},{10,12},{12,10},{14,8},{1,7},{3,5},... | collective-permute-start | bytes 172040 | tf_op jit(solution)/shard_map/ppermute | solution.py:492
  18.3 4.2 %collective-permute-start.7 = (bf16[224,128]{1,0:T(8,128)(2,1)S(1)}, bf16[224,128]{1,0:T(8,128)(2,1)S(1)}, u32[]{:S(2)}, u32[]{:S(2)}) collective-permute-start(bf16[224,128]{1,0:T(8,128)(2,1)S(1)} %get-tuple-element.36), channel_id=1, source_target_pairs={{0,4},{2,6},{4,0},{6,2},{8,12},{10,14},{12,8},{14,10},{1,5},{3,7},... | collective-permute-start | bytes 172040 | tf_op jit(solution)/shard_map/ppermute | solution.py:492
  18.7 4.2 %collective-permute-start.6 = (bf16[224,128]{1,0:T(8,128)(2,1)S(1)}, bf16[224,128]{1,0:T(8,128)(2,1)S(1)}, u32[]{:S(2)}, u32[]{:S(2)}) collective-permute-start(bf16[224,128]{1,0:T(8,128)(2,1)S(1)} %get-tuple-element.47), channel_id=1, source_target_pairs={{0,2},{2,0},{4,6},{6,4},{8,10},{10,8},{12,14},{14,12},{1,3},{3,1},... | collective-permute-start | bytes 172040 | tf_op jit(solution)/shard_map/ppermute | solution.py:492
  22.9 5.1 %collective-permute-start.9 = (bf16[224,128]{1,0:T(8,128)(2,1)S(1)}, bf16[224,128]{1,0:T(8,128)(2,1)S(1)}, u32[]{:S(2)}, u32[]{:S(2)}) collective-permute-start(bf16[224,128]{1,0:T(8,128)(2,1)S(1)} %fusion.1), channel_id=1, source_target_pairs={{0,8},{4,12},{8,0},{12,4},{1,9},{5,13},{9,1},{13,5},{2,10},{6,14},... | collective-permute-start | bytes 172040 | tf_op jit(solution)/shard_map/ppermute | solution.py:366
  28.1 5.1 %collective-permute-start.12 = (bf16[224,128]{1,0:T(8,128)(2,1)S(1)}, bf16[224,128]{1,0:T(8,128)(2,1)S(1)}, u32[]{:S(2)}, u32[]{:S(2)}) collective-permute-start(bf16[224,128]{1,0:T(8,128)(2,1)S(1)} %add_convert_fusion.piece_0), channel_id=1, source_target_pairs={{0,6},{2,4},{4,2},{6,0},{8,14},{10,12},{12,10},{14,8},{1,7},{3,5},... | collective-permute-start | bytes 172040 | tf_op jit(solution)/shard_map/ppermute | solution.py:492
  29.7 4.2 %collective-permute-start.11 = (bf16[224,128]{1,0:T(8,128)(2,1)S(1)}, bf16[224,128]{1,0:T(8,128)(2,1)S(1)}, u32[]{:S(2)}, u32[]{:S(2)}) collective-permute-start(bf16[224,128]{1,0:T(8,128)(2,1)S(1)} %add_convert_fusion.piece_0), channel_id=1, source_target_pairs={{0,4},{2,6},{4,0},{6,2},{8,12},{10,14},{12,8},{14,10},{1,5},{3,7},... | collective-permute-start | bytes 172040 | tf_op jit(solution)/shard_map/ppermute | solution.py:492
  30.1 4.2 %collective-permute-start.10 = (bf16[224,128]{1,0:T(8,128)(2,1)S(1)}, bf16[224,128]{1,0:T(8,128)(2,1)S(1)}, u32[]{:S(2)}, u32[]{:S(2)}) collective-permute-start(bf16[224,128]{1,0:T(8,128)(2,1)S(1)} %add_convert_fusion.piece_0), channel_id=1, source_target_pairs={{0,2},{2,0},{4,6},{6,4},{8,10},{10,8},{12,14},{14,12},{1,3},{3,1},... | collective-permute-start | bytes 172040 | tf_op jit(solution)/shard_map/ppermute | solution.py:492
